TPU v7x, 512 devices: a whole 4x8x8 slice. The times are simulated.
512 devices in a mesh: rep: 16 (over z, x_hi), grp: 32 (over y, x_lo, core).
Axes of the slice: x: 4 (x_hi: 2, x_lo: 2; x = x_hi * 2 + x_lo), y: 8, z: 8, core: 2. Of those that a mesh axis runs over, the one named last changes fastest.
Arguments:
- features: bfloat16 [65536, 256], P(('rep', 'grp')), may hold values from -6 to 6
- weight: bfloat16 [256, 256], replicated, may hold values from -0.375 to 0.375
- bias: float32 [256], replicated, may hold values from -3 to 3
- cotangent: bfloat16 [65536, 256], P(('rep', 'grp')), may hold values from -6 to 6
- degree: int32 [65536], P(('rep', 'grp')), may hold values from 1 to 99
- tile_cols: int32 [512, 24], P(('rep', 'grp')), may hold values from 0 to 95, as said below
- edge_tile: int32 [512, 3840], P(('rep', 'grp')), may hold values from 0 to 23
- edge_row: int32 [512, 3840], P(('rep', 'grp')), may hold values from 0 to 127
- edge_col: int32 [512, 3840], P(('rep', 'grp')), may hold values from 0 to 127
Outputs:
- hidden: bfloat16 [65536, 256], P(('rep', 'grp'))
- grad_features: bfloat16 [65536, 256], P(('rep', 'grp'))
- grad_weight: float32 [256, 256], replicated
- grad_bias: float32 [256], replicated
Inputs may be any that keep to these rules, and one draw needn't show every extreme that they name: `tile_cols`: each row lists 8 different tile columns in each of the ranges 0 to 31, 32 to 63 and 64 to 95, in that order.
All inputs are finite; a program needn't handle non-finite values.
Results may differ from a plain program's by a relative error of at most 0.0062.
Values may be sent and summed in bfloat16 or wider, within the bound.
No kernel may reach another device: no remote copies, remote signals or barrier semaphores. Data moves between devices by JAX's collectives and lax.ppermute only.
A program may use at most 64 MiB of HBM per device.

v0:
```python
import jax
import jax.numpy as jnp
from jax import lax
from jax.sharding import PartitionSpec as P


def shifted(x, axis, by):
    size = lax.axis_size(axis)
    return lax.ppermute(x, axis, [(i, (i + by) % size) for i in range(size)])


def per_device(features, weight, bias, cotangent, degree, tile_cols, edge_tile, edge_row, edge_col):
    tile_rows = features.shape[0]
    members = lax.axis_size("grp")
    block = tile_rows * members
    dinv = lax.rsqrt(degree.astype(jnp.float32))
    scaled = (jnp.dot(features, weight, preferred_element_type=jnp.float32) * dinv[:, None]).astype(
        jnp.bfloat16
    )
    listed = tile_cols[0]
    columns = listed[edge_tile[0]]
    window = columns * tile_rows + edge_col[0]
    slab = (
        jnp.zeros((tile_rows, 3 * block), jnp.float32)
        .at[edge_row[0], window]
        .add(1.0)
        .astype(jnp.bfloat16)
    )
    width = scaled.shape[1]
    from_left = shifted(scaled, "rep", 1)
    from_right = shifted(scaled, "rep", -1)
    empty = jnp.zeros((tile_rows, width), jnp.float32)
    total = empty
    pieces = (
        lax.all_gather(from_left, "grp", axis=0, tiled=True),
        lax.all_gather(scaled, "grp", axis=0, tiled=True),
        lax.all_gather(from_right, "grp", axis=0, tiled=True),
    )
    count = pieces[0].shape[0]
    for part_index in range(3):
        cols = lax.dynamic_slice_in_dim(slab, part_index * block, count, 1)
        total = total + jnp.dot(cols, pieces[part_index], preferred_element_type=jnp.float32)
    pre = total * dinv[:, None] + bias[None, :]
    sig = jax.nn.sigmoid(pre)
    hidden = (pre * sig).astype(jnp.bfloat16)
    grad_pre = cotangent.astype(jnp.float32) * sig * (1.0 + pre * (1.0 - sig))
    back = (grad_pre * dinv[:, None]).astype(jnp.bfloat16)
    contract = (((0,), (0,)), ((), ()))
    previous_part = lax.dot_general(
        slab[:, :block], back, contract, preferred_element_type=jnp.float32
    ).astype(jnp.bfloat16)
    next_part = lax.dot_general(
        slab[:, 2 * block :], back, contract, preferred_element_type=jnp.float32
    ).astype(jnp.bfloat16)
    from_next = shifted(previous_part, "rep", -1)
    from_previous = shifted(next_part, "rep", 1)
    middle = lax.dynamic_slice_in_dim(slab, block, lax.axis_size("grp") * tile_rows, 1)
    own_term = lax.dot_general(middle, back, contract, preferred_element_type=jnp.float32)
    own_term = own_term + from_next.astype(jnp.float32)
    grad_sum = lax.psum_scatter(
        own_term + from_previous.astype(jnp.float32), "grp", scatter_dimension=0, tiled=True
    )
    grad_scaled = (grad_sum * dinv[:, None]).astype(jnp.bfloat16)
    grad_features = lax.dot_general(
        grad_scaled, weight, (((1,), (1,)), ((), ())), preferred_element_type=jnp.float32
    ).astype(jnp.bfloat16)
    local_weight = lax.dot_general(
        features, grad_scaled, contract, preferred_element_type=jnp.float32
    )
    local_bias = jnp.sum(grad_pre, axis=0)
    grad_weight, grad_bias = lax.psum((local_weight, local_bias), ("rep", "grp"))
    return (hidden, grad_features, grad_weight, grad_bias)


def solution(mesh):
    return jax.shard_map(
        per_device,
        mesh=mesh,
        in_specs=(
            P(("rep", "grp"), None),
            P(),
            P(),
            P(("rep", "grp"), None),
            P(("rep", "grp")),
            P(("rep", "grp"), None),
            P(("rep", "grp"), None),
            P(("rep", "grp"), None),
            P(("rep", "grp"), None),
        ),
        out_specs=(P(("rep", "grp"), None), P(("rep", "grp"), None), P(), P()),
        check_vma=False,
    )
```

profile of v0, /device:TPU:1, one launch (start us, length us, event | category | flops | bytes accessed | tf_op | source)
XLA Modules:
  0.0 737.3 jit_solution(12004582378413549706)
XLA Ops:
  9.8 13.9 %collective-permute-start.1 = (bf16[128,256]{1,0:T(8,128)(2,1)}, bf16[128,256]{1,0:T(8,128)(2,1)S(1)}, u32[]{:S(2)}, u32[]{:S(2)}) collective-permute-start(bf16[128,256]{1,0:T(8,128)(2,1)} %fusion.5), channel_id=1, source_target_pairs={{0,480},{32,0},{64,32},{96,64},{128,96},{160,128},{192,160},{224,1... | collective-permute-start | bytes 196616 | tf_op jit(solution)/shard_map/ppermute | solution.py:9
  26.1 1.9 collective-permute-start
  28.0 7.2 collective-permute-done
  37.4 2.1 fusion.19
  39.5 5.2 fusion.17
  45.4 10.6 %select_multiply_fusion = s32[3840]{0:T(1024)S(1)} fusion(pred[3840]{0:T(1024)(128)(4,1)S(1)} %get-tuple-element.28, pred[3840]{0:T(1024)(128)(4,1)S(1)} %get-tuple-element.27, pred[3840]{0:T(1024)(128)(4,1)S(1)} %get-tuple-element.26, pred[3840]{0:T(1024)(128)(4,1)S(1)} %get-tuple-element.25, pred[3840]{0:T(1024)(128)(4,1)S(1)} %get-tuple-element.24, ...), kind=kLoop, calls=%fused_computation.57 | loop fusion | flops 69120 | bytes 96068 | tf_op jit(solution)/shard_map/mul | solution.py:22
  58.4 23.6 %scatter_custom_fusion = f32[1572864]{0:T(1024)} fusion(s32[3840]{0:T(1024)S(1)} %broadcast_select_fusion, f32[3840]{0:T(1024)S(1)} %broadcast.126, f32[]{:T(128)} %constant.6.clone.1), kind=kCustom, calls=%fused_computation.4 | custom fusion | flops 3840 | bytes 6291460
  82.0 4.2 convert_element_type.48
  86.2 4.1 reshape.98
  90.4 2.0 fusion.11
  92.4 60.7 %all-gather.8.cloned.1.call-done = bf16[4096,256]{1,0:T(8,128)(2,1)} async-done(((bf16[128,256]{1,0:T(8,128)(2,1)}), bf16[4096,256]{1,0:T(8,128)(2,1)}) %all-gather.8.cloned.1.call-update) | async-done | bytes 2097168 | tf_op jit(solution)/shard_map/all_gather | solution.py:37
  153.1 2.0 fusion.7
  155.2 67.5 %all-gather.4.cloned.1.call-done = bf16[4096,256]{1,0:T(8,128)(2,1)} async-done(((bf16[128,256]{1,0:T(8,128)(2,1)}), bf16[4096,256]{1,0:T(8,128)(2,1)}) %all-gather.4.cloned.1.call-update) | async-done | bytes 2097168 | tf_op jit(solution)/shard_map/all_gather | solution.py:35
  222.6 2.7 fusion.18
  227.0 7.7 %collective-permute-start.2 = (bf16[4096,256]{1,0:T(8,128)(2,1)S(1)}, bf16[4096,256]{1,0:T(8,128)(2,1)S(1)}, u32[]{:S(2)}, u32[]{:S(2)}) collective-permute-start(bf16[4096,256]{1,0:T(8,128)(2,1)S(1)} %convolution_convert_fusion.1), channel_id=1, source_target_pairs={{0,480},{32,0},{64,32},{96,64},{128,96},{160,128},{192,160},{224,1... | collective-permute-start | bytes 6291464 | tf_op jit(solution)/shard_map/ppermute | solution.py:9
  234.7 1.9 collective-permute-start.3
  236.6 85.6 %collective-permute-done.2 = bf16[4096,256]{1,0:T(8,128)(2,1)S(1)} collective-permute-done((bf16[4096,256]{1,0:T(8,128)(2,1)S(1)}, bf16[4096,256]{1,0:T(8,128)(2,1)S(1)}, u32[]{:S(2)}, u32[]{:S(2)}) %collective-permute-start.2) | collective-permute-done | bytes 2097184 | tf_op jit(solution)/shard_map/ppermute | solution.py:9
  322.5 2.8 convert_add_fusion
  325.3 101.7 %psum.15 = f32[256]{0:T(256)} all-reduce(f32[256]{0:T(256)S(1)} %get-tuple-element.29), channel_id=1, replica_groups=mesh['rep'=16,'grp'=32] {'rep','grp'}, use_global_device_ids=true, to_apply=%region_4.0 | all-reduce | flops 256 | bytes 2048 | tf_op jit(solution)/shard_map/psum | solution.py:71
  427.0 23.8 %reduce-scatter.2.cloned.1.call-done = f32[128,256]{1,0:T(8,128)} async-done(((f32[4096,256]{1,0:T(8,128)}), f32[128,256]{1,0:T(8,128)}) %reduce-scatter.2.cloned.1.call-update) | async-done | bytes 131088 | tf_op jit(solution)/shard_map/reduce_scatter | solution.py:60
  450.8 1.9 convolution_bitcast_fusion
  452.8 1.7 convolution_convert_fusion.2
  454.5 274.5 %all-reduce.2.cloned.1.call-done = f32[256,256]{0,1:T(8,128)} async-done(((f32[256,256]{0,1:T(8,128)}), f32[256,256]{0,1:T(8,128)}) %all-reduce.2.cloned.1.call-update) | async-done | bytes 262160 | tf_op jit(solution)/shard_map/psum | solution.py:71
  729.0 1.8 copy.14
  (35 shorter events, 12.1 us)
Async XLA Ops:
  7.2 0.9 copy-start
  7.2 83.2 %all-gather.6.cloned.1.call-start = ((), (), s32[]{:S(2)}) async-start(), calls=%async_computation.2 | async-start | bytes 2162688 | tf_op jit(solution)/shard_map/all_gather | solution.py:36
  9.7 143.4 %all-gather.8.cloned.1.call-start = ((), (), s32[]{:S(2)}) async-start(), calls=%async_computation.3 | async-start | bytes 2162688 | tf_op jit(solution)/shard_map/all_gather | solution.py:37
  9.8 15.6 %collective-permute-start.1 = (bf16[128,256]{1,0:T(8,128)(2,1)}, bf16[128,256]{1,0:T(8,128)(2,1)S(1)}, u32[]{:S(2)}, u32[]{:S(2)}) collective-permute-start(bf16[128,256]{1,0:T(8,128)(2,1)} %fusion.5), channel_id=1, source_target_pairs={{0,480},{32,0},{64,32},{96,64},{128,96},{160,128},{192,160},{224,1... | collective-permute-start | bytes 196616 | tf_op jit(solution)/shard_map/ppermute | solution.py:9
  25.4 0.6 copy-start.2
  26.0 196.6 %all-gather.4.cloned.1.call-start = ((), (), s32[]{:S(2)}) async-start(), calls=%async_computation.1 | async-start | bytes 2162688 | tf_op jit(solution)/shard_map/all_gather | solution.py:35
  26.1 9.1 %collective-permute-start = (bf16[128,256]{1,0:T(8,128)(2,1)}, bf16[128,256]{1,0:T(8,128)(2,1)S(1)}, u32[]{:S(2)}, u32[]{:S(2)}) collective-permute-start(bf16[128,256]{1,0:T(8,128)(2,1)} %fusion.5), channel_id=1, source_target_pairs={{0,32},{32,64},{64,96},{96,128},{128,160},{160,192},{192,224},{224... | collective-permute-start | bytes 196616 | tf_op jit(solution)/shard_map/ppermute | solution.py:9
  35.2 0.6 copy-start.3
  35.8 415.0 %reduce-scatter.2.cloned.1.call-start = ((), (), s32[]{:S(2)}) async-start(), calls=%async_computation.4 | async-start | bytes 4325376 | tf_op jit(solution)/shard_map/reduce_scatter | solution.py:60
  90.3 132.3 %copy-start.4 = (f32[256]{0:T(256)S(1)}, f32[256]{0:T(256)}, u32[]{:S(2)}) copy-start(f32[256]{0:T(256)} %param.11) | copy-start | bytes 3076
  227.0 95.2 %collective-permute-start.2 = (bf16[4096,256]{1,0:T(8,128)(2,1)S(1)}, bf16[4096,256]{1,0:T(8,128)(2,1)S(1)}, u32[]{:S(2)}, u32[]{:S(2)}) collective-permute-start(bf16[4096,256]{1,0:T(8,128)(2,1)S(1)} %convolution_convert_fusion.1), channel_id=1, source_target_pairs={{0,480},{32,0},{64,32},{96,64},{128,96},{160,128},{192,160},{224,1... | collective-permute-start | bytes 6291464 | tf_op jit(solution)/shard_map/ppermute | solution.py:9
  234.7 87.8 %collective-permute-start.3 = (bf16[4096,256]{1,0:T(8,128)(2,1)S(1)}, bf16[4096,256]{1,0:T(8,128)(2,1)S(1)}, u32[]{:S(2)}, u32[]{:S(2)}) collective-permute-start(bf16[4096,256]{1,0:T(8,128)(2,1)S(1)} %convolution_convert_fusion), channel_id=1, source_target_pairs={{0,32},{32,64},{64,96},{96,128},{128,160},{160,192},{192,224},{224... | collective-permute-start | bytes 6291464 | tf_op jit(solution)/shard_map/ppermute | solution.py:9
  325.3 125.6 %copy-start.1 = (bf16[128,256]{1,0:T(8,128)(2,1)S(1)}, bf16[128,256]{1,0:T(8,128)(2,1)}, u32[]{:S(2)}) copy-start(bf16[128,256]{1,0:T(8,128)(2,1)} %param.9) | copy-start | bytes 196612
  325.3 403.7 %all-reduce.2.cloned.1.call-start = ((), (), s32[]{:S(2)}) async-start(), calls=%async_computation.5 | async-start | bytes 524288 | tf_op jit(solution)/shard_map/psum | solution.py:71
Sparse Core Ops, SparseCore 0:
  10.7 72.7 all-gather.5
  86.2 66.8 all-gather.7
  155.9 66.7 all-gather.3
  325.4 125.3 reduce-scatter.1
  456.2 272.6 all-reduce.1
where the time goes:
time: 738 us; the launch traced here: 737 us
  waiting for transfers between devices  521 us (71%)
  blocking collectives  102 us (14%)
  other arithmetic  47.5 us (6%)
  starting transfers between devices  25.7 us (3%)
  matrix products  16.3 us (2%)
  between operations  13.9 us (2%)
  local copies, waits for them, and re-layouts  10.9 us (1%)
    psum x1, waiting for transfers between devices, per_device(): lax.psum((local_weight, local_bias), ('rep', 'grp'))  274 us
    psum x1, blocking collectives, per_device(): lax.psum((local_weight, local_bias), ('rep', 'grp'))  102 us
    ppermute x4, waiting for transfers between devices, shifted(): return lax.ppermute(x, axis, [(i, (i + by) % size) for i in range(size)])  94.7 us
    all_gather x1, waiting for transfers between devices, per_device(): lax.all_gather(from_left, 'grp', axis=0, tiled=True)  67.5 us
    all_gather x1, waiting for transfers between devices, per_device(): lax.all_gather(from_right, 'grp', axis=0, tiled=True)  60.7 us
    ppermute x4, starting transfers between devices, shifted(): return lax.ppermute(x, axis, [(i, (i + by) % size) for i in range(size)])  25.5 us
    unnamed x4, other arithmetic  25.1 us
    reduce_scatter x1, waiting for transfers between devices, per_device(): lax.psum_scatter(own_term + from_previous.astype(jnp.float32), 'grp', sca...  23.8 us
  transfers between devices with their start and end apart: 9, of which 8 were waited for; matrix products, arithmetic and copies ran while one was open for 8% of the time, Pallas kernels for 0%

commit v1 on v0

v1 whole, which is shorter than its diff:
```python
import functools

import jax
import jax.numpy as jnp
from jax import lax
from jax.experimental import pallas as pl
from jax.experimental.pallas import tpu as pltpu
from jax.sharding import PartitionSpec as P

SUB = 8
LANE = 128


def shifted(x, axis, by):
    size = lax.axis_size(axis)
    return lax.ppermute(x, axis, [(i, (i + by) % size) for i in range(size)])


def vmem():
    return pl.BlockSpec(memory_space=pltpu.VMEM)


def smem():
    return pl.BlockSpec(memory_space=pltpu.SMEM)


def count_kernel(chunk, xk_ref, yk_ref, out_ref, acc_ref):
    edges = xk_ref.shape[1]
    tall = acc_ref.shape[0]
    wide = acc_ref.shape[1]
    for step in range(edges // chunk):
        xk = xk_ref[:, pl.ds(step * chunk, chunk)]
        yk = yk_ref[:, pl.ds(step * chunk, chunk)]
        left = (lax.broadcasted_iota(jnp.int32, (tall, chunk), 0) == xk).astype(jnp.float32).astype(jnp.bfloat16)
        right = (lax.broadcasted_iota(jnp.int32, (wide, chunk), 0) == yk).astype(jnp.float32).astype(jnp.bfloat16)
        part = lax.dot_general(left, right, (((1,), (1,)), ((), ())), preferred_element_type=jnp.float32)
        if step == 0:
            acc_ref[...] = part
        else:
            acc_ref[...] += part
    rows = out_ref.shape[0]
    for block in range(tall // rows):
        out_ref[:, pl.ds(block * wide, wide)] = acc_ref[pl.ds(block * rows, rows), :].astype(jnp.bfloat16)


def build_slab(row, key, rows, keys):
    wide = 256
    edges = row.shape[0]
    chunk = 768 if edges % 768 == 0 else 128
    tall = rows * (keys // wide)
    xk = ((key // wide) * rows + row).reshape(1, edges)
    yk = (key % wide).reshape(1, edges)
    return pl.pallas_call(
        functools.partial(count_kernel, chunk),
        out_shape=jax.ShapeDtypeStruct((rows, keys), jnp.bfloat16),
        in_specs=[vmem(), vmem()],
        out_specs=vmem(),
        scratch_shapes=[pltpu.VMEM((tall, wide), jnp.float32)],
        name="count",
    )(xk, yk)


def select_kernel(members, per_part, idx_ref, a_ref, b_ref, c_ref, out_ref):
    listed = 3 * per_part

    def one(d, carry):
        base = d * listed
        for t in range(listed):
            src = (a_ref, b_ref, c_ref)[t // per_part]
            at = jnp.bitwise_and(idx_ref[base + t], members - 1)
            out_ref[base + t] = src[at]
        return carry

    lax.fori_loop(0, members, one, 0)


def select(idx, left, own, right, per_part):
    members = own.shape[0]
    return pl.pallas_call(
        functools.partial(select_kernel, members, per_part),
        out_shape=jax.ShapeDtypeStruct((members * 3 * per_part, SUB, LANE), own.dtype),
        in_specs=[smem(), vmem(), vmem(), vmem()],
        out_specs=vmem(),
        name="select",
    )(idx, left, own, right)


def layer_kernel(listed, slab_ref, x_ref, dinv_ref, bias_ref, cot_ref, hid_ref, part_ref):
    dinv = dinv_ref[...]
    groups = part_ref.shape[1]
    span = listed * SUB
    sums = []
    for half in range(2):
        lanes = slice(half * LANE, (half + 1) * LANE)
        total = jnp.dot(slab_ref[...], x_ref[half], preferred_element_type=jnp.float32)
        pre = total * dinv + bias_ref[:, lanes]
        sig = jax.nn.sigmoid(pre)
        hid_ref[:, lanes] = (pre * sig).astype(hid_ref.dtype)
        grad_pre = cot_ref[:, lanes].astype(jnp.float32) * sig * (1.0 + pre * (1.0 - sig))
        sums.append(jnp.sum(grad_pre, axis=0, keepdims=True))
        back = (grad_pre * dinv).astype(jnp.bfloat16)
        partial = lax.dot_general(
            slab_ref[...], back, (((0,), (0,)), ((), ())), preferred_element_type=jnp.float32
        )
        for a in range(groups):
            piece = partial[a * span : (a + 1) * span, :].reshape(listed, SUB, LANE)
            part_ref[half, a, pl.ds(0, listed)] = piece.astype(jnp.bfloat16)
    high = [s.astype(jnp.bfloat16).astype(jnp.float32) for s in sums]
    low = [s - h for s, h in zip(sums, high)]
    at = lax.broadcasted_iota(jnp.int32, (SUB, LANE), 0)
    extra = jnp.zeros((SUB, LANE), jnp.float32)
    for index, value in enumerate(high + low):
        extra = jnp.where(at == index, value, extra)
    extra = extra.astype(jnp.bfloat16)
    for half in range(2):
        for a in range(groups):
            part_ref[half, a, listed] = extra


def layer(slab, x, dinv, bias, cotangent, listed):
    rows, width = cotangent.shape
    groups = rows // SUB
    return pl.pallas_call(
        functools.partial(layer_kernel, listed),
        out_shape=(
            jax.ShapeDtypeStruct((rows, width), jnp.bfloat16),
            jax.ShapeDtypeStruct((2, groups, listed + 1, SUB, LANE), jnp.bfloat16),
        ),
        in_specs=[vmem()] * 5,
        out_specs=(vmem(), vmem()),
        name="layer",
    )(slab, x, dinv, bias, cotangent)


def collect_kernel(members, per_part, chains, idx_ref, got_ref, prev_ref, own_ref, next_ref, extra_ref, acc_ref):
    listed = 3 * per_part
    acc_ref[...] = jnp.zeros_like(acc_ref)

    def some(step, extra):
        for t in range(listed):
            for j in range(chains):
                d = step * chains + j
                at = jnp.bitwise_and(idx_ref[d * listed + t], members - 1)
                acc_ref[j, t // per_part, at] += got_ref[d, t].astype(jnp.float32)
        for j in range(chains):
            extra = extra + got_ref[step * chains + j, listed].astype(jnp.float32)
        return extra

    extra = lax.fori_loop(0, members // chains, some, jnp.zeros((SUB, LANE), jnp.float32))
    extra_ref[...] = extra
    for k, ref in enumerate((prev_ref, own_ref, next_ref)):
        value = acc_ref[0, k]
        for j in range(1, chains):
            value = value + acc_ref[j, k]
        ref[...] = value.astype(ref.dtype)


def collect(idx, got, per_part):
    members = got.shape[0]
    chains = 4
    piece = (members, SUB, LANE)
    return pl.pallas_call(
        functools.partial(collect_kernel, members, per_part, chains),
        out_shape=(
            jax.ShapeDtypeStruct(piece, jnp.bfloat16),
            jax.ShapeDtypeStruct(piece, jnp.float32),
            jax.ShapeDtypeStruct(piece, jnp.bfloat16),
            jax.ShapeDtypeStruct((SUB, LANE), jnp.float32),
        ),
        in_specs=[smem(), vmem()],
        out_specs=(vmem(),) * 4,
        scratch_shapes=[pltpu.VMEM((chains, 3) + piece, jnp.float32)],
        name="collect",
    )(idx, got)


def swap(x, axis):
    return lax.all_to_all(x, axis, 0, 0, tiled=True)


def per_device(features, weight, bias, cotangent, degree, tile_cols, edge_tile, edge_row, edge_col):
    rows, width = features.shape
    members = lax.axis_size("grp")
    rings = lax.axis_size("rep")
    listed = tile_cols.shape[1]
    per_part = listed // 3
    groups = rows // SUB
    half = lax.axis_index("grp") // groups
    contract = (((0,), (0,)), ((), ()))

    cut = features.reshape(groups, SUB, 2, LANE).transpose(0, 2, 1, 3)
    lane = lax.broadcasted_iota(jnp.int32, (groups, SUB, LANE), 2)
    names = jnp.pad(tile_cols[0], (0, LANE - listed))
    note = jnp.where(lane < LANE // 2, names[None, None, :], degree.reshape(groups, SUB, 1))
    sent = jnp.concatenate([cut, note.astype(jnp.bfloat16)[:, None]], axis=1)
    got = swap(jnp.concatenate([sent, sent], axis=0), "grp")
    nodes = jnp.concatenate([got[:, 0].reshape(-1, LANE), got[:, 1].reshape(-1, LANE)], axis=1)
    idx = got[:, 2, 0, :listed].astype(jnp.int32).reshape(-1)
    dinv_piece = lax.rsqrt(got[:, 2, :, LANE // 2].astype(jnp.float32)).reshape(-1, 1)

    weight_half = lax.dynamic_slice_in_dim(weight, half * LANE, LANE, 1)
    scaled = (jnp.dot(nodes, weight_half, preferred_element_type=jnp.float32) * dinv_piece).astype(jnp.bfloat16)
    scaled = scaled.reshape(members, SUB, LANE)
    from_left = shifted(scaled, "rep", 1)
    from_right = shifted(scaled, "rep", -1)

    tile = edge_tile[0]
    col = edge_col[0]
    key = (col // SUB) * (listed * SUB) + tile * SUB + col % SUB
    slab = build_slab(edge_row[0], key, rows, listed * rows)

    chosen = select(idx, from_left, scaled, from_right, per_part)
    window = swap(chosen.reshape(members, listed, SUB, LANE), "grp")
    dinv = lax.rsqrt(degree.astype(jnp.float32))[:, None]
    hidden, partial = layer(
        slab, window.reshape(2, listed * rows, LANE), dinv, bias[None, :], cotangent, listed
    )
    mine = swap(partial.reshape(members, listed + 1, SUB, LANE), "grp")
    previous_part, own_part, next_part, extra = collect(idx, mine, per_part)
    from_next = shifted(previous_part, "rep", -1)
    from_previous = shifted(next_part, "rep", 1)
    grad_sum = own_part + from_next.astype(jnp.float32) + from_previous.astype(jnp.float32)
    grad_piece = (grad_sum.reshape(-1, LANE) * dinv_piece).astype(jnp.bfloat16)
    local_weight = lax.dot_general(nodes, grad_piece, contract, preferred_element_type=jnp.float32)

    both = jnp.stack(
        [local_weight.reshape(members, SUB, LANE), grad_piece.astype(jnp.float32).reshape(members, SUB, LANE)], axis=1
    )
    both = swap(both, "grp")
    chunk = both[:, 0].reshape(2, groups, SUB, LANE).sum(axis=1)
    grad_scaled = both[:, 1].reshape(2, rows, LANE).transpose(1, 0, 2).reshape(rows, width).astype(jnp.bfloat16)
    grad_features = lax.dot_general(
        grad_scaled, weight, (((1,), (1,)), ((), ())), preferred_element_type=jnp.float32
    ).astype(jnp.bfloat16)

    share = jnp.concatenate([chunk, extra[None]], axis=0)
    share = swap(jnp.broadcast_to(share[None], (rings, 3, SUB, LANE)), "rep").sum(axis=0)
    bias_rows = share[2]
    grad_bias = jnp.concatenate([bias_rows[0] + bias_rows[2], bias_rows[1] + bias_rows[3]])
    whole = swap(jnp.broadcast_to(share[None, :2], (members, 2, SUB, LANE)), "grp")
    grad_weight = whole.transpose(0, 2, 1, 3).reshape(width, width)
    return (hidden, grad_features, grad_weight, grad_bias)


def solution(mesh):
    return jax.shard_map(
        per_device,
        mesh=mesh,
        in_specs=(
            P(("rep", "grp"), None),
            P(),
            P(),
            P(("rep", "grp"), None),
            P(("rep", "grp")),
            P(("rep", "grp"), None),
            P(("rep", "grp"), None),
            P(("rep", "grp"), None),
            P(("rep", "grp"), None),
        ),
        out_specs=(P(("rep", "grp"), None), P(("rep", "grp"), None), P(), P()),
        check_vma=False,
    )
```

time: 738 us -> 217 us (0.29)
  waiting for transfers between devices: 521 us -> 113 us
  blocking collectives: 102 us -> 17 us
  other arithmetic: 47.5 us -> 5.08 us
  starting transfers between devices: 25.7 us -> 52.3 us
  Pallas kernels: 0 us -> 18.5 us
  matrix products: 16.3 us -> 1.18 us
  between operations: 13.9 us -> 0.95 us
    psum x1 -> x0, waiting for transfers between devices: 274 us -> none  [per_device(): lax.psum((local_weight, local_bias), ('rep', 'grp'))]
    all_gather x3 -> x0, waiting for transfers between devices: 128 us -> none  [the longest x1 67.5 us: per_device(): lax.all_gather(from_left, 'grp', axis=0, tiled=True)]
    all_to_all x0 -> x5, waiting for transfers between devices: none -> 103 us  [swap(): return lax.all_to_all(x, axis, 0, 0, tiled=True)]
    psum x1 -> x0, blocking collectives: 102 us -> none  [per_device(): lax.psum((local_weight, local_bias), ('rep', 'grp'))]
    ppermute x4, waiting for transfers between devices: 94.7 us -> 9.78 us  [shifted(): return lax.ppermute(x, axis, [(i, (i + by) % size) for i in range(size)])]
    all_to_all x0 -> x5, starting transfers between devices: none -> 31.6 us  [swap(): return lax.all_to_all(x, axis, 0, 0, tiled=True)]
    unnamed x4 -> x0, other arithmetic: 25.1 us -> none
    reduce_scatter x1 -> x0, waiting for transfers between devices: 23.8 us -> none  [per_device(): lax.psum_scatter(own_term + from_previous.astype(jnp.float32), 'grp', sca...]
  transfers between devices with their start and end apart: 9 -> 9, of which waited for: 8 -> 7; matrix products, arithmetic and copies ran while one was open for 8% -> 2% of each run, Pallas kernels for 0% -> 2%
where the time goes in v1:
time: 217 us; the launch traced here: 216 us
  waiting for transfers between devices  113 us (52%)
  starting transfers between devices  52.3 us (24%)
  Pallas kernels  18.5 us (9%)
  blocking collectives  17 us (8%)
  local copies, waits for them, and re-layouts  8.57 us (4%)
  other arithmetic  5.08 us (2%)
    all_to_all x5, waiting for transfers between devices, swap(): return lax.all_to_all(x, axis, 0, 0, tiled=True)  103 us
    all_to_all x5, starting transfers between devices, swap(): return lax.all_to_all(x, axis, 0, 0, tiled=True)  31.6 us
    ppermute x4, starting transfers between devices, shifted(): return lax.ppermute(x, axis, [(i, (i + by) % size) for i in range(size)])  20.7 us
    all_to_all x1, blocking collectives, swap(): return lax.all_to_all(x, axis, 0, 0, tiled=True)  17 us
    ppermute x4, waiting for transfers between devices, shifted(): return lax.ppermute(x, axis, [(i, (i + by) % size) for i in range(size)])  9.78 us
    pallas_call x1, Pallas kernels, collect(): pl.pallas_call(functools.partial(collect_kernel, members, per_part, chain...  5.82 us
    pallas_call x1, Pallas kernels, build_slab(): pl.pallas_call(functools.partial(count_kernel, chunk), out_shape=jax.Shap...  4.91 us
    pallas_call x1, Pallas kernels, layer(): pl.pallas_call(functools.partial(layer_kernel, listed), out_shape=(jax.Sh...  4.45 us
  transfers between devices with their start and end apart: 9, of which 7 were waited for; matrix products, arithmetic and copies ran while one was open for 2% of the time, Pallas kernels for 2%

profile of v1, /device:TPU:1, one launch (start us, length us, event | category | flops | bytes accessed | tf_op | source)
XLA Modules:
  0.0 216.5 jit_solution(16675918690641114600)
XLA Ops:
  2.2 1.6 maximum_maximum_fusion
  3.8 10.4 %all-to-all-start = ((bf16[32,3,8,128]{3,2,1,0:T(8,128)(2,1)}), bf16[32,3,8,128]{3,2,1,0:T(8,128)(2,1)S(1)}, u32[]{:S(2)}, u32[]{:S(2)}) async-start(bf16[32,3,8,128]{3,2,1,0:T(8,128)(2,1)} %maximum_maximum_fusion), calls=%async_computation | async-start | bytes 393216 | tf_op jit(solution)/shard_map/all_to_all | solution.py:178
  14.2 10.4 %all-to-all-done = bf16[32,3,8,128]{3,2,1,0:T(8,128)(2,1)S(1)} async-done(((bf16[32,3,8,128]{3,2,1,0:T(8,128)(2,1)}), bf16[32,3,8,128]{3,2,1,0:T(8,128)(2,1)S(1)}, u32[]{:S(2)}, u32[]{:S(2)}) %all-to-all-start) | async-done | bytes 196640 | tf_op jit(solution)/shard_map/all_to_all | solution.py:178
  25.1 12.0 %collective-permute-start.1 = (bf16[32,8,128]{2,1,0:T(8,128)(2,1)S(1)}, bf16[32,8,128]{2,1,0:T(8,128)(2,1)S(1)}, u32[]{:S(2)}, u32[]{:S(2)}) collective-permute-start(bf16[32,8,128]{2,1,0:T(8,128)(2,1)S(1)} %fusion.1.b_ref), channel_id=1, source_target_pairs={{0,480},{32,0},{64,32},{96,64},{128,96},{160,128},{192,160},{224,1... | collective-permute-start | bytes 196616 | tf_op jit(solution)/shard_map/ppermute | solution.py:16
  37.2 1.9 collective-permute-start
  39.8 6.0 %collective-permute-done.a_ref = bf16[32,8,128]{2,1,0:T(8,128)(2,1)S(1)} collective-permute-done((bf16[32,8,128]{2,1,0:T(8,128)(2,1)S(1)}, bf16[32,8,128]{2,1,0:T(8,128)(2,1)S(1)}, u32[]{:S(2)}, u32[]{:S(2)}) %collective-permute-start) | collective-permute-done | bytes 65568 | tf_op jit(solution)/shard_map/ppermute | solution.py:16
  46.4 3.3 %select.30 = bf16[768,8,128]{2,1,0:T(8,128)(2,1)} custom-call(s32[768]{0:T(1024)} %reshape.100.idx_ref, bf16[32,8,128]{2,1,0:T(8,128)(2,1)} %copy-done.5, bf16[32,8,128]{2,1,0:T(8,128)(2,1)} %copy-done.3, bf16[32,8,128]{2,1,0:T(8,128)(2,1)} %copy-done.4), custom_call_target="tpu_custom_call" | custom-call | tf_op jit(solution)/shard_map/select/pallas_call | solution.py:79
  49.7 5.9 %all-to-all-start.1 = ((bf16[32,24,8,128]{3,2,1,0:T(8,128)(2,1)}), bf16[32,24,8,128]{3,2,1,0:T(8,128)(2,1)S(1)}, u32[]{:S(2)}, u32[]{:S(2)}) async-start(bf16[32,24,8,128]{3,2,1,0:T(8,128)(2,1)} %bitcast.51), calls=%async_computation.1 | async-start | bytes 3145728 | tf_op jit(solution)/shard_map/all_to_all | solution.py:178
  57.9 4.9 %count.1.slab_ref = bf16[128,3072]{1,0:T(8,128)(2,1)} custom-call(s32[1,3840]{1,0:T(1,128)} %multiply_add_fusion.xk_ref, s32[1,3840]{1,0:T(1,128)} %get-tuple-element.18.yk_ref), custom_call_target="tpu_custom_call" | custom-call | tf_op jit(solution)/shard_map/count/pallas_call | solution.py:53
  62.8 32.0 %all-to-all-done.1 = bf16[32,24,8,128]{3,2,1,0:T(8,128)(2,1)S(1)} async-done(((bf16[32,24,8,128]{3,2,1,0:T(8,128)(2,1)}), bf16[32,24,8,128]{3,2,1,0:T(8,128)(2,1)S(1)}, u32[]{:S(2)}, u32[]{:S(2)}) %all-to-all-start.1) | async-done | bytes 1572896 | tf_op jit(solution)/shard_map/all_to_all | solution.py:178
  94.8 1.1 copy-done.2
  95.9 4.5 %layer.1 = (bf16[128,256]{1,0:T(8,128)(2,1)}, bf16[2,16,25,8,128]{4,3,2,1,0:T(8,128)(2,1)}) custom-call(bf16[128,3072]{1,0:T(8,128)(2,1)} %count.1.slab_ref, bf16[2,3072,128]{2,1,0:T(8,128)(2,1)} %bitcast.50, f32[128,1]{1,0:T(8,128)} %copy.35.dinv_ref, f32[1,256]{1,0:T(1,128)} %bitcast.60, bf16[128,256]{1,0:T(8,128)(2,1)} %cot_ref.1), custom_call_target="tpu_custom_call" | custom-call | tf_op jit(solution)/shard_map/layer/pallas_call | solution.py:123
  100.4 5.3 %all-to-all-start.2 = ((bf16[32,25,8,128]{3,2,1,0:T(8,128)(2,1)}), bf16[32,25,8,128]{3,2,1,0:T(8,128)(2,1)S(1)}, u32[]{:S(2)}, u32[]{:S(2)}) async-start(bf16[32,25,8,128]{3,2,1,0:T(8,128)(2,1)} %bitcast.52), calls=%async_computation.2 | async-start | bytes 3276800 | tf_op jit(solution)/shard_map/all_to_all | solution.py:178
  105.9 40.2 %all-to-all-done.2.got_ref = bf16[32,25,8,128]{3,2,1,0:T(8,128)(2,1)S(1)} async-done(((bf16[32,25,8,128]{3,2,1,0:T(8,128)(2,1)}), bf16[32,25,8,128]{3,2,1,0:T(8,128)(2,1)S(1)}, u32[]{:S(2)}, u32[]{:S(2)}) %all-to-all-start.2) | async-done | bytes 1638432 | tf_op jit(solution)/shard_map/all_to_all | solution.py:178
  146.2 1.2 copy-done.1
  147.3 5.8 %collect.1 = (bf16[32,8,128]{2,1,0:T(8,128)(2,1)}, f32[32,8,128]{2,1,0:T(8,128)}, bf16[32,8,128]{2,1,0:T(8,128)(2,1)}, f32[8,128]{1,0:T(8,128)}) custom-call(s32[768]{0:T(1024)} %reshape.100.idx_ref, bf16[32,25,8,128]{3,2,1,0:T(8,128)(2,1)} %copy-done.1), custom_call_target="tpu_custom_call" | custom-call | tf_op jit(solution)/shard_map/collect/pallas_call | solution.py:162
  153.2 1.9 collective-permute-start.2
  155.1 4.9 %collective-permute-start.3 = (bf16[32,8,128]{2,1,0:T(8,128)(2,1)}, bf16[32,8,128]{2,1,0:T(8,128)(2,1)S(1)}, u32[]{:S(2)}, u32[]{:S(2)}) collective-permute-start(bf16[32,8,128]{2,1,0:T(8,128)(2,1)} %get-tuple-element.14), channel_id=1, source_target_pairs={{0,32},{32,64},{64,96},{96,128},{128,160},{160,192},{192,224},{224... | collective-permute-start | bytes 196616 | tf_op jit(solution)/shard_map/ppermute | solution.py:16
  160.1 3.8 %collective-permute-done.3 = bf16[32,8,128]{2,1,0:T(8,128)(2,1)S(1)} collective-permute-done((bf16[32,8,128]{2,1,0:T(8,128)(2,1)}, bf16[32,8,128]{2,1,0:T(8,128)(2,1)S(1)}, u32[]{:S(2)}, u32[]{:S(2)}) %collective-permute-start.3) | collective-permute-done | bytes 65568 | tf_op jit(solution)/shard_map/ppermute | solution.py:16
  165.2 17.0 %all_to_all.30 = f32[32,2,8,128]{3,2,1,0:T(8,128)S(1)} all-to-all(f32[32,2,8,128]{3,2,1,0:T(8,128)S(1)} %copy.39), channel_id=1, replica_groups=mesh['rep'=16,'grp'=32] {'grp'}, dimensions={0} | all-to-all | bytes 524288 | tf_op jit(solution)/shard_map/all_to_all | solution.py:178
  183.0 3.5 %all-to-all-start.4 = ((f32[16,3,8,128]{3,2,1,0:T(8,128)}), f32[16,3,8,128]{3,2,1,0:T(8,128)S(1)}, u32[]{:S(2)}, u32[]{:S(2)}) async-start(f32[16,3,8,128]{3,2,1,0:T(8,128)} %broadcast_in_dim.47), calls=%async_computation.4 | async-start | bytes 393216 | tf_op jit(solution)/shard_map/all_to_all | solution.py:178
  186.7 10.4 %all-to-all-done.4 = f32[16,3,8,128]{3,2,1,0:T(8,128)S(1)} async-done(((f32[16,3,8,128]{3,2,1,0:T(8,128)}), f32[16,3,8,128]{3,2,1,0:T(8,128)S(1)}, u32[]{:S(2)}, u32[]{:S(2)}) %all-to-all-start.4) | async-done | bytes 196640 | tf_op jit(solution)/shard_map/all_to_all | solution.py:178
  197.8 6.5 %all-to-all-start.5 = ((f32[32,2,8,128]{3,2,1,0:T(8,128)}), f32[32,2,8,128]{3,2,1,0:T(8,128)S(1)}, u32[]{:S(2)}, u32[]{:S(2)}) async-start(f32[32,2,8,128]{3,2,1,0:T(8,128)} %broadcast_in_dim.48), calls=%async_computation.5 | async-start | bytes 524288 | tf_op jit(solution)/shard_map/all_to_all | solution.py:178
  205.7 10.1 %all-to-all-done.5 = f32[32,2,8,128]{3,2,1,0:T(8,128)S(1)} async-done(((f32[32,2,8,128]{3,2,1,0:T(8,128)}), f32[32,2,8,128]{3,2,1,0:T(8,128)S(1)}, u32[]{:S(2)}, u32[]{:S(2)}) %all-to-all-start.5) | async-done | bytes 262176 | tf_op jit(solution)/shard_map/all_to_all | solution.py:178
  (57 shorter events, 10.9 us)
Async XLA Ops:
  0.6 24.3 %copy-start = (bf16[256,256]{1,0:T(8,128)(2,1)S(1)}, bf16[256,256]{1,0:T(8,128)(2,1)}, u32[]{:S(2)}) copy-start(bf16[256,256]{1,0:T(8,128)(2,1)} %param.10) | copy-start | bytes 393220
  3.8 20.8 %all-to-all-start = ((bf16[32,3,8,128]{3,2,1,0:T(8,128)(2,1)}), bf16[32,3,8,128]{3,2,1,0:T(8,128)(2,1)S(1)}, u32[]{:S(2)}, u32[]{:S(2)}) async-start(bf16[32,3,8,128]{3,2,1,0:T(8,128)(2,1)} %maximum_maximum_fusion), calls=%async_computation | async-start | bytes 393216 | tf_op jit(solution)/shard_map/all_to_all | solution.py:178
  25.1 20.7 %copy-start.3 = (bf16[32,8,128]{2,1,0:T(8,128)(2,1)}, bf16[32,8,128]{2,1,0:T(8,128)(2,1)S(1)}, u32[]{:S(2)}) copy-start(bf16[32,8,128]{2,1,0:T(8,128)(2,1)S(1)} %fusion.1.b_ref) | copy-start | bytes 196612
  25.1 14.7 %collective-permute-start.1 = (bf16[32,8,128]{2,1,0:T(8,128)(2,1)S(1)}, bf16[32,8,128]{2,1,0:T(8,128)(2,1)S(1)}, u32[]{:S(2)}, u32[]{:S(2)}) collective-permute-start(bf16[32,8,128]{2,1,0:T(8,128)(2,1)S(1)} %fusion.1.b_ref), channel_id=1, source_target_pairs={{0,480},{32,0},{64,32},{96,64},{128,96},{160,128},{192,160},{224,1... | collective-permute-start | bytes 196616 | tf_op jit(solution)/shard_map/ppermute | solution.py:16
  37.2 8.6 %collective-permute-start = (bf16[32,8,128]{2,1,0:T(8,128)(2,1)S(1)}, bf16[32,8,128]{2,1,0:T(8,128)(2,1)S(1)}, u32[]{:S(2)}, u32[]{:S(2)}) collective-permute-start(bf16[32,8,128]{2,1,0:T(8,128)(2,1)S(1)} %fusion.1.b_ref), channel_id=1, source_target_pairs={{0,32},{32,64},{64,96},{96,128},{128,160},{160,192},{192,224},{224... | collective-permute-start | bytes 196616 | tf_op jit(solution)/shard_map/ppermute | solution.py:16
  39.8 6.0 %copy-start.4 = (bf16[32,8,128]{2,1,0:T(8,128)(2,1)}, bf16[32,8,128]{2,1,0:T(8,128)(2,1)S(1)}, u32[]{:S(2)}) copy-start(bf16[32,8,128]{2,1,0:T(8,128)(2,1)S(1)} %collective-permute-done.1.c_ref) | copy-start | bytes 196612
  45.8 0.6 copy-start.5
  49.7 5.9 %copy-start.10 = (s32[128]{0:T(128)S(1)}, s32[128]{0:T(128)}, u32[]{:S(2)}) copy-start(s32[128]{0:T(128)} %param.13) | copy-start | bytes 1540
  49.7 6.7 %copy-start.7 = (s32[1,3840]{1,0:T(1,128)S(1)}, s32[1,3840]{1,0:T(1,128)}, u32[]{:S(2)}) copy-start(s32[1,3840]{1,0:T(1,128)} %param.15) | copy-start | bytes 46084
  49.7 6.7 %copy-start.8 = (s32[1,3840]{1,0:T(1,128)S(1)}, s32[1,3840]{1,0:T(1,128)}, u32[]{:S(2)}) copy-start(s32[1,3840]{1,0:T(1,128)} %param.17) | copy-start | bytes 46084
  49.7 7.5 %copy-start.6 = (s32[1,3840]{1,0:T(1,128)S(1)}, s32[1,3840]{1,0:T(1,128)}, u32[]{:S(2)}) copy-start(s32[1,3840]{1,0:T(1,128)} %param.16) | copy-start | bytes 46084
  49.7 45.1 %all-to-all-start.1 = ((bf16[32,24,8,128]{3,2,1,0:T(8,128)(2,1)}), bf16[32,24,8,128]{3,2,1,0:T(8,128)(2,1)S(1)}, u32[]{:S(2)}, u32[]{:S(2)}) async-start(bf16[32,24,8,128]{3,2,1,0:T(8,128)(2,1)} %bitcast.51), calls=%async_computation.1 | async-start | bytes 3145728 | tf_op jit(solution)/shard_map/all_to_all | solution.py:178
  94.8 1.1 copy-start.2
  100.4 45.8 %all-to-all-start.2 = ((bf16[32,25,8,128]{3,2,1,0:T(8,128)(2,1)}), bf16[32,25,8,128]{3,2,1,0:T(8,128)(2,1)S(1)}, u32[]{:S(2)}, u32[]{:S(2)}) async-start(bf16[32,25,8,128]{3,2,1,0:T(8,128)(2,1)} %bitcast.52), calls=%async_computation.2 | async-start | bytes 3276800 | tf_op jit(solution)/shard_map/all_to_all | solution.py:178
  146.2 1.2 copy-start.1
  153.2 6.9 %collective-permute-start.2 = (bf16[32,8,128]{2,1,0:T(8,128)(2,1)}, bf16[32,8,128]{2,1,0:T(8,128)(2,1)S(1)}, u32[]{:S(2)}, u32[]{:S(2)}) collective-permute-start(bf16[32,8,128]{2,1,0:T(8,128)(2,1)} %get-tuple-element.13), channel_id=1, source_target_pairs={{0,480},{32,0},{64,32},{96,64},{128,96},{160,128},{192,160},{224,1... | collective-permute-start | bytes 196616 | tf_op jit(solution)/shard_map/ppermute | solution.py:16
  155.1 27.2 %copy-start.9 = (f32[8,128]{1,0:T(8,128)S(1)}, f32[8,128]{1,0:T(8,128)}, u32[]{:S(2)}) copy-start(f32[8,128]{1,0:T(8,128)} %get-tuple-element.15) | copy-start | bytes 12292
  155.1 8.8 %collective-permute-start.3 = (bf16[32,8,128]{2,1,0:T(8,128)(2,1)}, bf16[32,8,128]{2,1,0:T(8,128)(2,1)S(1)}, u32[]{:S(2)}, u32[]{:S(2)}) collective-permute-start(bf16[32,8,128]{2,1,0:T(8,128)(2,1)} %get-tuple-element.14), channel_id=1, source_target_pairs={{0,32},{32,64},{64,96},{96,128},{128,160},{160,192},{192,224},{224... | collective-permute-start | bytes 196616 | tf_op jit(solution)/shard_map/ppermute | solution.py:16
  183.0 14.1 %all-to-all-start.4 = ((f32[16,3,8,128]{3,2,1,0:T(8,128)}), f32[16,3,8,128]{3,2,1,0:T(8,128)S(1)}, u32[]{:S(2)}, u32[]{:S(2)}) async-start(f32[16,3,8,128]{3,2,1,0:T(8,128)} %broadcast_in_dim.47), calls=%async_computation.4 | async-start | bytes 393216 | tf_op jit(solution)/shard_map/all_to_all | solution.py:178
  197.8 18.0 %all-to-all-start.5 = ((f32[32,2,8,128]{3,2,1,0:T(8,128)}), f32[32,2,8,128]{3,2,1,0:T(8,128)S(1)}, u32[]{:S(2)}, u32[]{:S(2)}) async-start(f32[32,2,8,128]{3,2,1,0:T(8,128)} %broadcast_in_dim.48), calls=%async_computation.5 | async-start | bytes 524288 | tf_op jit(solution)/shard_map/all_to_all | solution.py:178

commit v2 on v1

v2 whole, which is shorter than its diff:
```python
import functools

import jax
import jax.numpy as jnp
from jax import lax
from jax.experimental import pallas as pl
from jax.experimental.pallas import tpu as pltpu
from jax.sharding import PartitionSpec as P

SUB = 8
LANE = 128


def shifted(x, axis, by):
    size = lax.axis_size(axis)
    return lax.ppermute(x, axis, [(i, (i + by) % size) for i in range(size)])


def vmem():
    return pl.BlockSpec(memory_space=pltpu.VMEM)


def smem():
    return pl.BlockSpec(memory_space=pltpu.SMEM)


def count_kernel(chunk, xk_ref, yk_ref, own_ref, far_ref, acc_ref):
    edges = xk_ref.shape[1]
    tall = acc_ref.shape[0]
    wide = acc_ref.shape[1]
    for step in range(edges // chunk):
        xk = xk_ref[:, pl.ds(step * chunk, chunk)]
        yk = yk_ref[:, pl.ds(step * chunk, chunk)]
        left = (lax.broadcasted_iota(jnp.int32, (tall, chunk), 0) == xk).astype(jnp.float32).astype(jnp.bfloat16)
        right = (lax.broadcasted_iota(jnp.int32, (wide, chunk), 0) == yk).astype(jnp.float32).astype(jnp.bfloat16)
        part = lax.dot_general(left, right, (((1,), (1,)), ((), ())), preferred_element_type=jnp.float32)
        if step == 0:
            acc_ref[...] = part
        else:
            acc_ref[...] += part
    rows = own_ref.shape[0]
    first = own_ref.shape[1] // wide
    for block in range(tall // rows):
        out_ref, at = (own_ref, block) if block < first else (far_ref, block - first)
        out_ref[:, pl.ds(at * wide, wide)] = acc_ref[pl.ds(block * rows, rows), :].astype(jnp.bfloat16)


def build_slab(row, key, rows, keys):
    wide = 256
    edges = row.shape[0]
    chunk = 768 if edges % 768 == 0 else 128
    tall = rows * (keys // wide)
    xk = ((key // wide) * rows + row).reshape(1, edges)
    yk = (key % wide).reshape(1, edges)
    return pl.pallas_call(
        functools.partial(count_kernel, chunk),
        out_shape=(
            jax.ShapeDtypeStruct((rows, keys // 3), jnp.bfloat16),
            jax.ShapeDtypeStruct((rows, keys - keys // 3), jnp.bfloat16),
        ),
        in_specs=[vmem(), vmem()],
        out_specs=(vmem(), vmem()),
        scratch_shapes=[pltpu.VMEM((tall, wide), jnp.float32)],
        name="count",
    )(xk, yk)


def select_kernel(members, per_part, parts, idx_ref, *refs):
    sources, out_ref = refs[:-1], refs[-1]

    def one(d, carry):
        for number, part in enumerate(parts):
            for t in range(per_part):
                at = jnp.bitwise_and(idx_ref[d * 3 * per_part + part * per_part + t], members - 1)
                out_ref[d, number * per_part + t] = sources[number][at]
        return carry

    lax.fori_loop(0, members, one, 0)


def select(idx, parts, sources, per_part):
    members = sources[0].shape[0]
    return pl.pallas_call(
        functools.partial(select_kernel, members, per_part, parts),
        out_shape=jax.ShapeDtypeStruct((members, len(parts) * per_part, SUB, LANE), sources[0].dtype),
        in_specs=[smem()] + [vmem()] * len(sources),
        out_specs=vmem(),
        name="select",
    )(idx, *sources)


def store_partial(slab_ref, back, part_ref, half):
    groups = part_ref.shape[1]
    listed = slab_ref.shape[1] // (groups * SUB)
    span = listed * SUB
    partial = lax.dot_general(slab_ref[...], back, (((0,), (0,)), ((), ())), preferred_element_type=jnp.float32)
    for a in range(groups):
        piece = partial[a * span : (a + 1) * span, :].reshape(listed, SUB, LANE)
        part_ref[half, a, pl.ds(0, listed)] = piece.astype(jnp.bfloat16)


def layer_kernel(own_ref, far_ref, xown_ref, xfar_ref, dinv_ref, bias_ref, cot_ref, hid_ref, part_ref, back_ref, extra_ref):
    dinv = dinv_ref[...]
    sums = []
    for half in range(2):
        lanes = slice(half * LANE, (half + 1) * LANE)
        total = jnp.dot(own_ref[...], xown_ref[half], preferred_element_type=jnp.float32)
        total = total + jnp.dot(far_ref[...], xfar_ref[half], preferred_element_type=jnp.float32)
        pre = total * dinv + bias_ref[:, lanes]
        sig = jax.nn.sigmoid(pre)
        hid_ref[:, lanes] = (pre * sig).astype(hid_ref.dtype)
        grad_pre = cot_ref[:, lanes].astype(jnp.float32) * sig * (1.0 + pre * (1.0 - sig))
        sums.append(jnp.sum(grad_pre, axis=0, keepdims=True))
        back = (grad_pre * dinv).astype(jnp.bfloat16)
        back_ref[:, lanes] = back
        store_partial(far_ref, back, part_ref, half)
    high = [s.astype(jnp.bfloat16).astype(jnp.float32) for s in sums]
    low = [s - h for s, h in zip(sums, high)]
    at = lax.broadcasted_iota(jnp.int32, (SUB, LANE), 0)
    extra = jnp.zeros((SUB, LANE), jnp.float32)
    for index, value in enumerate(high + low):
        extra = jnp.where(at == index, value, extra)
    extra_ref[...] = extra


def layer(own, far, xown, xfar, dinv, bias, cotangent, listed):
    rows, width = cotangent.shape
    groups = rows // SUB
    return pl.pallas_call(
        layer_kernel,
        out_shape=(
            jax.ShapeDtypeStruct((rows, width), jnp.bfloat16),
            jax.ShapeDtypeStruct((2, groups, listed - listed // 3, SUB, LANE), jnp.bfloat16),
            jax.ShapeDtypeStruct((rows, width), jnp.bfloat16),
            jax.ShapeDtypeStruct((SUB, LANE), jnp.float32),
        ),
        in_specs=[vmem()] * 7,
        out_specs=(vmem(),) * 4,
        name="layer",
    )(own, far, xown, xfar, dinv, bias, cotangent)


def own_kernel(own_ref, back_ref, extra_ref, part_ref):
    groups = part_ref.shape[1]
    last = part_ref.shape[2] - 1
    extra = extra_ref[...].astype(jnp.bfloat16)
    for half in range(2):
        store_partial(own_ref, back_ref[:, half * LANE : (half + 1) * LANE], part_ref, half)
        for a in range(groups):
            part_ref[half, a, last] = extra


def own_partial(own, back, extra):
    groups = back.shape[0] // SUB
    listed = own.shape[1] // (groups * SUB)
    return pl.pallas_call(
        own_kernel,
        out_shape=jax.ShapeDtypeStruct((2, groups, listed + 1, SUB, LANE), jnp.bfloat16),
        in_specs=[vmem()] * 3,
        out_specs=vmem(),
        name="own",
    )(own, back, extra)


def collect_kernel(members, per_part, parts, chains, idx_ref, got_ref, *refs):
    acc_ref = refs[-1]
    outs = refs[: len(parts)]
    more = len(refs) - 1 - len(parts)
    acc_ref[...] = jnp.zeros_like(acc_ref)

    def some(step, extra):
        for number, part in enumerate(parts):
            for t in range(per_part):
                for j in range(chains):
                    d = step * chains + j
                    at = jnp.bitwise_and(idx_ref[d * 3 * per_part + part * per_part + t], members - 1)
                    acc_ref[j, number, at] += got_ref[d, number * per_part + t].astype(jnp.float32)
        if more:
            for j in range(chains):
                extra = extra + got_ref[step * chains + j, len(parts) * per_part].astype(jnp.float32)
        return extra

    extra = lax.fori_loop(0, members // chains, some, jnp.zeros((SUB, LANE), jnp.float32))
    if more:
        refs[len(parts)][...] = extra
    for number, ref in enumerate(outs):
        value = acc_ref[0, number]
        for j in range(1, chains):
            value = value + acc_ref[j, number]
        ref[...] = value.astype(ref.dtype)


def collect(idx, parts, got, per_part, dtype):
    members = got.shape[0]
    chains = 4
    piece = (members, SUB, LANE)
    outs = [jax.ShapeDtypeStruct(piece, dtype) for _ in parts]
    if got.shape[1] > len(parts) * per_part:
        outs.append(jax.ShapeDtypeStruct((SUB, LANE), jnp.float32))
    return pl.pallas_call(
        functools.partial(collect_kernel, members, per_part, parts, chains),
        out_shape=tuple(outs),
        in_specs=[smem(), vmem()],
        out_specs=(vmem(),) * len(outs),
        scratch_shapes=[pltpu.VMEM((chains, len(parts)) + piece, jnp.float32)],
        name="collect",
    )(idx, got)


def swap(x, axis):
    return lax.all_to_all(x, axis, 0, 0, tiled=True)


def per_device(features, weight, bias, cotangent, degree, tile_cols, edge_tile, edge_row, edge_col):
    rows, width = features.shape
    members = lax.axis_size("grp")
    rings = lax.axis_size("rep")
    listed = tile_cols.shape[1]
    per_part = listed // 3
    groups = rows // SUB
    half = lax.axis_index("grp") // groups
    contract = (((0,), (0,)), ((), ()))

    cut = features.reshape(groups, SUB, 2, LANE).transpose(0, 2, 1, 3)
    lane = lax.broadcasted_iota(jnp.int32, (groups, SUB, LANE), 2)
    names = jnp.pad(tile_cols[0], (0, LANE - listed))
    note = jnp.where(lane < LANE // 2, names[None, None, :], degree.reshape(groups, SUB, 1))
    sent = jnp.concatenate([cut, note.astype(jnp.bfloat16)[:, None]], axis=1)
    got = swap(jnp.concatenate([sent, sent], axis=0), "grp")
    nodes = jnp.concatenate([got[:, 0].reshape(-1, LANE), got[:, 1].reshape(-1, LANE)], axis=1)
    idx = got[:, 2, 0, :listed].astype(jnp.int32).reshape(-1)
    dinv_piece = lax.rsqrt(got[:, 2, :, LANE // 2].astype(jnp.float32)).reshape(-1, 1)

    weight_half = lax.dynamic_slice_in_dim(weight, half * LANE, LANE, 1)
    scaled = (jnp.dot(nodes, weight_half, preferred_element_type=jnp.float32) * dinv_piece).astype(jnp.bfloat16)
    scaled = scaled.reshape(members, SUB, LANE)
    from_left = shifted(scaled, "rep", 1)
    from_right = shifted(scaled, "rep", -1)

    tile = edge_tile[0]
    col = edge_col[0]
    far_tile = jnp.where(tile < per_part, tile, tile - per_part)
    is_own = (tile >= per_part) & (tile < 2 * per_part)
    own_key = (col // SUB) * (per_part * SUB) + (tile - per_part) * SUB
    far_key = per_part * rows + (col // SUB) * (2 * per_part * SUB) + far_tile * SUB
    key = jnp.where(is_own, own_key, far_key) + col % SUB
    slab_own, slab_far = build_slab(edge_row[0], key, rows, listed * rows)

    chosen_own = select(idx, (1,), (scaled,), per_part)
    window_own = swap(chosen_own, "grp")
    chosen_far = select(idx, (0, 2), (from_left, from_right), per_part)
    window_far = swap(chosen_far, "grp")
    dinv = lax.rsqrt(degree.astype(jnp.float32))[:, None]
    hidden, partial_far, back, extra = layer(
        slab_own,
        slab_far,
        window_own.reshape(2, per_part * rows, LANE),
        window_far.reshape(2, 2 * per_part * rows, LANE),
        dinv,
        bias[None, :],
        cotangent,
        listed,
    )
    mine_far = swap(partial_far.reshape(members, 2 * per_part, SUB, LANE), "grp")
    partial_own = own_partial(slab_own, back, extra)
    mine_own = swap(partial_own.reshape(members, per_part + 1, SUB, LANE), "grp")
    previous_part, next_part = collect(idx, (0, 2), mine_far, per_part, jnp.bfloat16)
    from_next = shifted(previous_part, "rep", -1)
    from_previous = shifted(next_part, "rep", 1)
    own_part, extra = collect(idx, (1,), mine_own, per_part, jnp.float32)
    grad_sum = own_part + from_next.astype(jnp.float32) + from_previous.astype(jnp.float32)
    grad_piece = (grad_sum.reshape(-1, LANE) * dinv_piece).astype(jnp.bfloat16)
    local_weight = lax.dot_general(nodes, grad_piece, contract, preferred_element_type=jnp.float32)

    both = jnp.stack(
        [local_weight.astype(jnp.bfloat16).reshape(members, SUB, LANE), grad_piece.reshape(members, SUB, LANE)], axis=1
    )
    both = swap(both, "grp")
    chunk = both[:, 0].reshape(2, groups, SUB, LANE).astype(jnp.float32).sum(axis=1)
    grad_scaled = both[:, 1].reshape(2, rows, LANE).transpose(1, 0, 2).reshape(rows, width)
    grad_features = lax.dot_general(
        grad_scaled, weight, (((1,), (1,)), ((), ())), preferred_element_type=jnp.float32
    ).astype(jnp.bfloat16)

    share = jnp.concatenate([chunk, extra[None]], axis=0)
    share = swap(jnp.broadcast_to(share[None], (rings, 3, SUB, LANE)), "rep").sum(axis=0)
    bias_rows = share[2]
    grad_bias = jnp.concatenate([bias_rows[0] + bias_rows[2], bias_rows[1] + bias_rows[3]])
    final = share[None, :2].astype(jnp.bfloat16)
    whole = swap(jnp.broadcast_to(final, (members, 2, SUB, LANE)), "grp")
    grad_weight = whole.transpose(0, 2, 1, 3).reshape(width, width).astype(jnp.float32)
    return (hidden, grad_features, grad_weight, grad_bias)


def solution(mesh):
    return jax.shard_map(
        per_device,
        mesh=mesh,
        in_specs=(
            P(("rep", "grp"), None),
            P(),
            P(),
            P(("rep", "grp"), None),
            P(("rep", "grp")),
            P(("rep", "grp"), None),
            P(("rep", "grp"), None),
            P(("rep", "grp"), None),
            P(("rep", "grp"), None),
        ),
        out_specs=(P(("rep", "grp"), None), P(("rep", "grp"), None), P(), P()),
        check_vma=False,
    )
```

time: 217 us -> 209 us (0.963)
  waiting for transfers between devices: 113 us -> 90 us
  starting transfers between devices: 52.3 us -> 63.6 us
  Pallas kernels: 18.5 us -> 23.2 us
  blocking collectives: 17 us -> 13.3 us
    all_to_all x5 -> x7, waiting for transfers between devices: 103 us -> 83.3 us  [swap(): return lax.all_to_all(x, axis, 0, 0, tiled=True)]
    all_to_all x5 -> x7, starting transfers between devices: 31.6 us -> 43 us  [swap(): return lax.all_to_all(x, axis, 0, 0, tiled=True)]
    pallas_call x4 -> x7, Pallas kernels: 18.5 us -> 23.2 us  [the longest x2 7.39 us: collect(): pl.pallas_call(functools.partial(collect_kernel, members, per_part, parts...]
    all_to_all x1, blocking collectives: 17 us -> 13.3 us  [swap(): return lax.all_to_all(x, axis, 0, 0, tiled=True)]
    ppermute x4, waiting for transfers between devices: 9.78 us -> 6.68 us  [shifted(): return lax.ppermute(x, axis, [(i, (i + by) % size) for i in range(size)])]
    unnamed x24 -> x30, local copies, waits for them, and re-layouts: 3.7 us -> 5.26 us
  transfers between devices with their start and end apart: 9 -> 11, of which waited for: 7 -> 7; matrix products, arithmetic and copies ran while one was open for 2% -> 2% of each run, Pallas kernels for 2% -> 8%
where the time goes in v2:
time: 209 us; the launch traced here: 208 us
  waiting for transfers between devices  90 us (43%)
  starting transfers between devices  63.6 us (30%)
  Pallas kernels  23.2 us (11%)
  blocking collectives  13.3 us (6%)
  local copies, waits for them, and re-layouts  8.62 us (4%)
  other arithmetic  4.91 us (2%)
  matrix products  2.9 us (1%)
    all_to_all x7, waiting for transfers between devices, swap(): return lax.all_to_all(x, axis, 0, 0, tiled=True)  83.3 us
    all_to_all x7, starting transfers between devices, swap(): return lax.all_to_all(x, axis, 0, 0, tiled=True)  43 us
    ppermute x4, starting transfers between devices, shifted(): return lax.ppermute(x, axis, [(i, (i + by) % size) for i in range(size)])  20.6 us
    all_to_all x1, blocking collectives, swap(): return lax.all_to_all(x, axis, 0, 0, tiled=True)  13.3 us
    pallas_call x2, Pallas kernels, collect(): pl.pallas_call(functools.partial(collect_kernel, members, per_part, parts...  7.39 us
    ppermute x4, waiting for transfers between devices, shifted(): return lax.ppermute(x, axis, [(i, (i + by) % size) for i in range(size)])  6.68 us
    unnamed x30, local copies, waits for them, and re-layouts  5.26 us
    pallas_call x2, Pallas kernels, select(): pl.pallas_call(functools.partial(select_kernel, members, per_part, parts)...  4.87 us
  transfers between devices with their start and end apart: 11, of which 7 were waited for; matrix products, arithmetic and copies ran while one was open for 2% of the time, Pallas kernels for 8%

profile of v2, /device:TPU:1, one launch (start us, length us, event | category | flops | bytes accessed | tf_op | source)
XLA Modules:
  0.0 207.5 jit_solution(3000544979901137521)
XLA Ops:
  3.8 10.4 %all-to-all-start = ((bf16[32,3,8,128]{3,2,1,0:T(8,128)(2,1)}), bf16[32,3,8,128]{3,2,1,0:T(8,128)(2,1)S(1)}, u32[]{:S(2)}, u32[]{:S(2)}) async-start(bf16[32,3,8,128]{3,2,1,0:T(8,128)(2,1)} %maximum_maximum_fusion), calls=%async_computation | async-start | bytes 393216 | tf_op jit(solution)/shard_map/all_to_all | solution.py:211
  14.2 10.4 %all-to-all-done = bf16[32,3,8,128]{3,2,1,0:T(8,128)(2,1)S(1)} async-done(((bf16[32,3,8,128]{3,2,1,0:T(8,128)(2,1)}), bf16[32,3,8,128]{3,2,1,0:T(8,128)(2,1)S(1)}, u32[]{:S(2)}, u32[]{:S(2)}) %all-to-all-start) | async-done | bytes 196640 | tf_op jit(solution)/shard_map/all_to_all | solution.py:211
  26.5 2.2 %select.31 = bf16[32,8,8,128]{3,2,1,0:T(8,128)(2,1)} custom-call(s32[768]{0:T(1024)} %reshape.95.idx_ref, bf16[32,8,128]{2,1,0:T(8,128)(2,1)} %fusion.2.refs_0_), custom_call_target="tpu_custom_call" | custom-call | tf_op jit(solution)/shard_map/select/pallas_call | solution.py:83
  28.7 4.5 %all-to-all-start.1 = ((bf16[32,8,8,128]{3,2,1,0:T(8,128)(2,1)}), bf16[32,8,8,128]{3,2,1,0:T(8,128)(2,1)S(1)}, u32[]{:S(2)}, u32[]{:S(2)}) async-start(bf16[32,8,8,128]{3,2,1,0:T(8,128)(2,1)} %select.31), calls=%async_computation.1 | async-start | bytes 1048576 | tf_op jit(solution)/shard_map/all_to_all | solution.py:211
  33.2 11.9 %collective-permute-start.1 = (bf16[32,8,128]{2,1,0:T(8,128)(2,1)S(1)}, bf16[32,8,128]{2,1,0:T(8,128)(2,1)S(1)}, u32[]{:S(2)}, u32[]{:S(2)}) collective-permute-start(bf16[32,8,128]{2,1,0:T(8,128)(2,1)S(1)} %copy-done.6), channel_id=1, source_target_pairs={{0,480},{32,0},{64,32},{96,64},{128,96},{160,128},{192,160},{224,1... | collective-permute-start | bytes 196616 | tf_op jit(solution)/shard_map/ppermute | solution.py:16
  47.0 6.7 %collective-permute-done.refs_0_ = bf16[32,8,128]{2,1,0:T(8,128)(2,1)S(1)} collective-permute-done((bf16[32,8,128]{2,1,0:T(8,128)(2,1)S(1)}, bf16[32,8,128]{2,1,0:T(8,128)(2,1)S(1)}, u32[]{:S(2)}, u32[]{:S(2)}) %collective-permute-start) | collective-permute-done | bytes 65568 | tf_op jit(solution)/shard_map/ppermute | solution.py:16
  54.4 2.7 %select.32 = bf16[32,16,8,128]{3,2,1,0:T(8,128)(2,1)} custom-call(s32[768]{0:T(1024)} %reshape.95.idx_ref, bf16[32,8,128]{2,1,0:T(8,128)(2,1)} %copy-done.8, bf16[32,8,128]{2,1,0:T(8,128)(2,1)} %copy-done.7), custom_call_target="tpu_custom_call" | custom-call | tf_op jit(solution)/shard_map/select/pallas_call | solution.py:83
  57.9 9.2 %all-to-all-start.2 = ((bf16[32,16,8,128]{3,2,1,0:T(8,128)(2,1)}), bf16[32,16,8,128]{3,2,1,0:T(8,128)(2,1)S(1)}, u32[]{:S(2)}, u32[]{:S(2)}) async-start(bf16[32,16,8,128]{3,2,1,0:T(8,128)(2,1)} %select.32), calls=%async_computation.2 | async-start | bytes 2097152 | tf_op jit(solution)/shard_map/all_to_all | solution.py:211
  69.4 4.8 %count.1 = (bf16[128,1024]{1,0:T(8,128)(2,1)}, bf16[128,2048]{1,0:T(8,128)(2,1)}) custom-call(s32[1,3840]{1,0:T(1,128)} %multiply_add_fusion.xk_ref, s32[1,3840]{1,0:T(1,128)} %get-tuple-element.24.yk_ref), custom_call_target="tpu_custom_call" | custom-call | tf_op jit(solution)/shard_map/count/pallas_call | solution.py:55
  74.2 21.0 %all-to-all-done.2 = bf16[32,16,8,128]{3,2,1,0:T(8,128)(2,1)S(1)} async-done(((bf16[32,16,8,128]{3,2,1,0:T(8,128)(2,1)}), bf16[32,16,8,128]{3,2,1,0:T(8,128)(2,1)S(1)}, u32[]{:S(2)}, u32[]{:S(2)}) %all-to-all-start.2) | async-done | bytes 1048608 | tf_op jit(solution)/shard_map/all_to_all | solution.py:211
  96.1 4.0 %layer.1 = (bf16[128,256]{1,0:T(8,128)(2,1)}, bf16[2,16,16,8,128]{4,3,2,1,0:T(8,128)(2,1)}, bf16[128,256]{1,0:T(8,128)(2,1)}, f32[8,128]{1,0:T(8,128)}) custom-call(bf16[128,1024]{1,0:T(8,128)(2,1)} %get-tuple-element.14.own_ref, bf16[128,2048]{1,0:T(8,128)(2,1)} %get-tuple-element.15.far_ref, bf16[2,1024,128]{2,1,0:T(8,128)(2,1)} %bitcast.51, ...), custom_call_target="tpu_custom_call" | custom-call | tf_op jit(solution)/shard_map/layer/pallas_call | solution.py:129
  100.1 4.3 %all-to-all-start.4 = ((bf16[32,16,8,128]{3,2,1,0:T(8,128)(2,1)}), bf16[32,16,8,128]{3,2,1,0:T(8,128)(2,1)S(1)}, u32[]{:S(2)}, u32[]{:S(2)}) async-start(bf16[32,16,8,128]{3,2,1,0:T(8,128)(2,1)} %bitcast.52), calls=%async_computation.4 | async-start | bytes 2097152 | tf_op jit(solution)/shard_map/all_to_all | solution.py:211
  106.6 25.9 %all-to-all-done.4.got_ref = bf16[32,16,8,128]{3,2,1,0:T(8,128)(2,1)S(1)} async-done(((bf16[32,16,8,128]{3,2,1,0:T(8,128)(2,1)}), bf16[32,16,8,128]{3,2,1,0:T(8,128)(2,1)S(1)}, u32[]{:S(2)}, u32[]{:S(2)}) %all-to-all-start.4) | async-done | bytes 1048608 | tf_op jit(solution)/shard_map/all_to_all | solution.py:211
  132.5 5.1 %all-to-all-start.3 = ((bf16[32,9,8,128]{3,2,1,0:T(8,128)(2,1)}), bf16[32,9,8,128]{3,2,1,0:T(8,128)(2,1)S(1)}, u32[]{:S(2)}, u32[]{:S(2)}) async-start(bf16[32,9,8,128]{3,2,1,0:T(8,128)(2,1)} %bitcast.50), calls=%async_computation.3 | async-start | bytes 1179648 | tf_op jit(solution)/shard_map/all_to_all | solution.py:211
  137.6 4.5 %collect.3 = (bf16[32,8,128]{2,1,0:T(8,128)(2,1)}, bf16[32,8,128]{2,1,0:T(8,128)(2,1)}) custom-call(s32[768]{0:T(1024)} %reshape.95.idx_ref, bf16[32,16,8,128]{3,2,1,0:T(8,128)(2,1)} %copy-done.2), custom_call_target="tpu_custom_call" | custom-call | tf_op jit(solution)/shard_map/collect/pallas_call | solution.py:200
  142.1 4.1 %collective-permute-start.2 = (bf16[32,8,128]{2,1,0:T(8,128)(2,1)}, bf16[32,8,128]{2,1,0:T(8,128)(2,1)S(1)}, u32[]{:S(2)}, u32[]{:S(2)}) collective-permute-start(bf16[32,8,128]{2,1,0:T(8,128)(2,1)} %get-tuple-element.21), channel_id=1, source_target_pairs={{0,480},{32,0},{64,32},{96,64},{128,96},{160,128},{192,160},{224,1... | collective-permute-start | bytes 196616 | tf_op jit(solution)/shard_map/ppermute | solution.py:16
  146.2 2.7 %collective-permute-start.3 = (bf16[32,8,128]{2,1,0:T(8,128)(2,1)}, bf16[32,8,128]{2,1,0:T(8,128)(2,1)S(1)}, u32[]{:S(2)}, u32[]{:S(2)}) collective-permute-start(bf16[32,8,128]{2,1,0:T(8,128)(2,1)} %get-tuple-element.22), channel_id=1, source_target_pairs={{0,32},{32,64},{64,96},{96,128},{128,160},{160,192},{192,224},{224... | collective-permute-start | bytes 196616 | tf_op jit(solution)/shard_map/ppermute | solution.py:16
  149.1 7.1 %all-to-all-done.3.got_ref = bf16[32,9,8,128]{3,2,1,0:T(8,128)(2,1)S(1)} async-done(((bf16[32,9,8,128]{3,2,1,0:T(8,128)(2,1)}), bf16[32,9,8,128]{3,2,1,0:T(8,128)(2,1)S(1)}, u32[]{:S(2)}, u32[]{:S(2)}) %all-to-all-start.3) | async-done | bytes 589856 | tf_op jit(solution)/shard_map/all_to_all | solution.py:211
  157.0 2.9 %collect.2 = (f32[32,8,128]{2,1,0:T(8,128)}, f32[8,128]{1,0:T(8,128)}) custom-call(s32[768]{0:T(1024)} %reshape.95.idx_ref, bf16[32,9,8,128]{3,2,1,0:T(8,128)(2,1)} %copy-done.3), custom_call_target="tpu_custom_call" | custom-call | tf_op jit(solution)/shard_map/collect/pallas_call | solution.py:200
  161.3 13.3 %all_to_all.40 = bf16[32,2,8,128]{3,2,1,0:T(8,128)(2,1)S(1)} all-to-all(bf16[32,2,8,128]{3,2,1,0:T(8,128)(2,1)S(1)} %copy.34), channel_id=1, replica_groups=mesh['rep'=16,'grp'=32] {'grp'}, dimensions={0} | all-to-all | bytes 262144 | tf_op jit(solution)/shard_map/all_to_all | solution.py:211
  176.1 3.5 %all-to-all-start.6 = ((f32[16,3,8,128]{3,2,1,0:T(8,128)}), f32[16,3,8,128]{3,2,1,0:T(8,128)S(1)}, u32[]{:S(2)}, u32[]{:S(2)}) async-start(f32[16,3,8,128]{3,2,1,0:T(8,128)} %broadcast_in_dim.47), calls=%async_computation.6 | async-start | bytes 393216 | tf_op jit(solution)/shard_map/all_to_all | solution.py:211
  180.6 10.1 %all-to-all-done.6 = f32[16,3,8,128]{3,2,1,0:T(8,128)S(1)} async-done(((f32[16,3,8,128]{3,2,1,0:T(8,128)}), f32[16,3,8,128]{3,2,1,0:T(8,128)S(1)}, u32[]{:S(2)}, u32[]{:S(2)}) %all-to-all-start.6) | async-done | bytes 196640 | tf_op jit(solution)/shard_map/all_to_all | solution.py:211
  191.4 6.0 %all-to-all-start.7 = ((bf16[32,2,8,128]{3,2,1,0:T(8,128)(2,1)}), bf16[32,2,8,128]{3,2,1,0:T(8,128)(2,1)S(1)}, u32[]{:S(2)}, u32[]{:S(2)}) async-start(bf16[32,2,8,128]{3,2,1,0:T(8,128)(2,1)} %broadcast_in_dim.48), calls=%async_computation.7 | async-start | bytes 262144 | tf_op jit(solution)/shard_map/all_to_all | solution.py:211
  197.9 8.8 %all-to-all-done.7 = bf16[32,2,8,128]{3,2,1,0:T(8,128)(2,1)S(1)} async-done(((bf16[32,2,8,128]{3,2,1,0:T(8,128)(2,1)}), bf16[32,2,8,128]{3,2,1,0:T(8,128)(2,1)S(1)}, u32[]{:S(2)}, u32[]{:S(2)}) %all-to-all-start.7) | async-done | bytes 131104 | tf_op jit(solution)/shard_map/all_to_all | solution.py:211
  (68 shorter events, 20.5 us)
Async XLA Ops:
  0.6 25.0 %copy-start = (bf16[256,256]{1,0:T(8,128)(2,1)S(1)}, bf16[256,256]{1,0:T(8,128)(2,1)}, u32[]{:S(2)}) copy-start(bf16[256,256]{1,0:T(8,128)(2,1)} %param.10) | copy-start | bytes 393220
  0.6 0.7 copy-start.13
  3.8 20.8 %all-to-all-start = ((bf16[32,3,8,128]{3,2,1,0:T(8,128)(2,1)}), bf16[32,3,8,128]{3,2,1,0:T(8,128)(2,1)S(1)}, u32[]{:S(2)}, u32[]{:S(2)}) async-start(bf16[32,3,8,128]{3,2,1,0:T(8,128)(2,1)} %maximum_maximum_fusion), calls=%async_computation | async-start | bytes 393216 | tf_op jit(solution)/shard_map/all_to_all | solution.py:211
  28.7 4.5 %copy-start.6 = (bf16[32,8,128]{2,1,0:T(8,128)(2,1)S(1)}, bf16[32,8,128]{2,1,0:T(8,128)(2,1)}, u32[]{:S(2)}) copy-start(bf16[32,8,128]{2,1,0:T(8,128)(2,1)} %fusion.2.refs_0_) | copy-start | bytes 196612
  28.7 28.4 %all-to-all-start.1 = ((bf16[32,8,8,128]{3,2,1,0:T(8,128)(2,1)}), bf16[32,8,8,128]{3,2,1,0:T(8,128)(2,1)S(1)}, u32[]{:S(2)}, u32[]{:S(2)}) async-start(bf16[32,8,8,128]{3,2,1,0:T(8,128)(2,1)} %select.31), calls=%async_computation.1 | async-start | bytes 1048576 | tf_op jit(solution)/shard_map/all_to_all | solution.py:211
  33.2 13.9 %collective-permute-start.1 = (bf16[32,8,128]{2,1,0:T(8,128)(2,1)S(1)}, bf16[32,8,128]{2,1,0:T(8,128)(2,1)S(1)}, u32[]{:S(2)}, u32[]{:S(2)}) collective-permute-start(bf16[32,8,128]{2,1,0:T(8,128)(2,1)S(1)} %copy-done.6), channel_id=1, source_target_pairs={{0,480},{32,0},{64,32},{96,64},{128,96},{160,128},{192,160},{224,1... | collective-permute-start | bytes 196616 | tf_op jit(solution)/shard_map/ppermute | solution.py:16
  45.1 8.6 %collective-permute-start = (bf16[32,8,128]{2,1,0:T(8,128)(2,1)S(1)}, bf16[32,8,128]{2,1,0:T(8,128)(2,1)S(1)}, u32[]{:S(2)}, u32[]{:S(2)}) collective-permute-start(bf16[32,8,128]{2,1,0:T(8,128)(2,1)S(1)} %copy-done.6), channel_id=1, source_target_pairs={{0,32},{32,64},{64,96},{96,128},{128,160},{160,192},{192,224},{224... | collective-permute-start | bytes 196616 | tf_op jit(solution)/shard_map/ppermute | solution.py:16
  47.0 6.7 %copy-start.7 = (bf16[32,8,128]{2,1,0:T(8,128)(2,1)}, bf16[32,8,128]{2,1,0:T(8,128)(2,1)S(1)}, u32[]{:S(2)}) copy-start(bf16[32,8,128]{2,1,0:T(8,128)(2,1)S(1)} %collective-permute-done.1.refs_1_) | copy-start | bytes 196612
  57.0 0.8 copy-start.4
  57.9 37.3 %all-to-all-start.2 = ((bf16[32,16,8,128]{3,2,1,0:T(8,128)(2,1)}), bf16[32,16,8,128]{3,2,1,0:T(8,128)(2,1)S(1)}, u32[]{:S(2)}, u32[]{:S(2)}) async-start(bf16[32,16,8,128]{3,2,1,0:T(8,128)(2,1)} %select.32), calls=%async_computation.2 | async-start | bytes 2097152 | tf_op jit(solution)/shard_map/all_to_all | solution.py:211
  67.1 0.8 copy-start.10
  67.1 0.8 copy-start.11
  67.9 0.8 copy-start.9
  95.1 1.0 copy-start.1
  100.1 32.3 %all-to-all-start.4 = ((bf16[32,16,8,128]{3,2,1,0:T(8,128)(2,1)}), bf16[32,16,8,128]{3,2,1,0:T(8,128)(2,1)S(1)}, u32[]{:S(2)}, u32[]{:S(2)}) async-start(bf16[32,16,8,128]{3,2,1,0:T(8,128)(2,1)} %bitcast.52), calls=%async_computation.4 | async-start | bytes 2097152 | tf_op jit(solution)/shard_map/all_to_all | solution.py:211
  132.4 5.1 %copy-start.2 = (bf16[32,16,8,128]{3,2,1,0:T(8,128)(2,1)}, bf16[32,16,8,128]{3,2,1,0:T(8,128)(2,1)S(1)}, u32[]{:S(2)}) copy-start(bf16[32,16,8,128]{3,2,1,0:T(8,128)(2,1)S(1)} %all-to-all-done.4.got_ref) | copy-start | bytes 3145732
  132.5 23.7 %all-to-all-start.3 = ((bf16[32,9,8,128]{3,2,1,0:T(8,128)(2,1)}), bf16[32,9,8,128]{3,2,1,0:T(8,128)(2,1)S(1)}, u32[]{:S(2)}, u32[]{:S(2)}) async-start(bf16[32,9,8,128]{3,2,1,0:T(8,128)(2,1)} %bitcast.50), calls=%async_computation.3 | async-start | bytes 1179648 | tf_op jit(solution)/shard_map/all_to_all | solution.py:211
  142.1 17.9 %collective-permute-start.2 = (bf16[32,8,128]{2,1,0:T(8,128)(2,1)}, bf16[32,8,128]{2,1,0:T(8,128)(2,1)S(1)}, u32[]{:S(2)}, u32[]{:S(2)}) collective-permute-start(bf16[32,8,128]{2,1,0:T(8,128)(2,1)} %get-tuple-element.21), channel_id=1, source_target_pairs={{0,480},{32,0},{64,32},{96,64},{128,96},{160,128},{192,160},{224,1... | collective-permute-start | bytes 196616 | tf_op jit(solution)/shard_map/ppermute | solution.py:16
  146.2 13.7 %collective-permute-start.3 = (bf16[32,8,128]{2,1,0:T(8,128)(2,1)}, bf16[32,8,128]{2,1,0:T(8,128)(2,1)S(1)}, u32[]{:S(2)}, u32[]{:S(2)}) collective-permute-start(bf16[32,8,128]{2,1,0:T(8,128)(2,1)} %get-tuple-element.22), channel_id=1, source_target_pairs={{0,32},{32,64},{64,96},{96,128},{128,160},{160,192},{192,224},{224... | collective-permute-start | bytes 196616 | tf_op jit(solution)/shard_map/ppermute | solution.py:16
  156.2 0.8 copy-start.3
  159.9 1.3 copy-start.5
  174.7 0.7 copy-start.12
  176.1 14.6 %all-to-all-start.6 = ((f32[16,3,8,128]{3,2,1,0:T(8,128)}), f32[16,3,8,128]{3,2,1,0:T(8,128)S(1)}, u32[]{:S(2)}, u32[]{:S(2)}) async-start(f32[16,3,8,128]{3,2,1,0:T(8,128)} %broadcast_in_dim.47), calls=%async_computation.6 | async-start | bytes 393216 | tf_op jit(solution)/shard_map/all_to_all | solution.py:211
  191.4 15.4 %all-to-all-start.7 = ((bf16[32,2,8,128]{3,2,1,0:T(8,128)(2,1)}), bf16[32,2,8,128]{3,2,1,0:T(8,128)(2,1)S(1)}, u32[]{:S(2)}, u32[]{:S(2)}) async-start(bf16[32,2,8,128]{3,2,1,0:T(8,128)(2,1)} %broadcast_in_dim.48), calls=%async_computation.7 | async-start | bytes 262144 | tf_op jit(solution)/shard_map/all_to_all | solution.py:211
  (2 other events, 1.3 us)

commit v3 on v1

v3 whole, which is shorter than its diff:
```python
import functools

import jax
import jax.numpy as jnp
from jax import lax
from jax.experimental import pallas as pl
from jax.experimental.pallas import tpu as pltpu
from jax.sharding import PartitionSpec as P


SUB = 8
LANE = 128


def shifted(x, axis, by):
    size = lax.axis_size(axis)
    return lax.ppermute(x, axis, [(i, (i + by) % size) for i in range(size)])


def vmem():
    return pl.BlockSpec(memory_space=pltpu.VMEM)


def smem():
    return pl.BlockSpec(memory_space=pltpu.SMEM)


def count_kernel(chunk, xk_ref, yk_ref, out_ref, acc_ref):
    edges = xk_ref.shape[1]
    tall = acc_ref.shape[0]
    wide = acc_ref.shape[1]
    for step in range(edges // chunk):
        xk = xk_ref[:, pl.ds(step * chunk, chunk)]
        yk = yk_ref[:, pl.ds(step * chunk, chunk)]
        left = (lax.broadcasted_iota(jnp.int32, (tall, chunk), 0) == xk).astype(jnp.float32).astype(jnp.bfloat16)
        right = (lax.broadcasted_iota(jnp.int32, (wide, chunk), 0) == yk).astype(jnp.float32).astype(jnp.bfloat16)
        part = lax.dot_general(left, right, (((1,), (1,)), ((), ())), preferred_element_type=jnp.float32)
        if step == 0:
            acc_ref[...] = part
        else:
            acc_ref[...] += part
    rows = out_ref.shape[0]
    for block in range(tall // rows):
        out_ref[:, pl.ds(block * wide, wide)] = acc_ref[pl.ds(block * rows, rows), :].astype(jnp.bfloat16)


def build_slab(row, key, rows, keys):
    wide = 256
    edges = row.shape[0]
    chunk = 768 if edges % 768 == 0 else 128
    tall = rows * (keys // wide)
    xk = ((key // wide) * rows + row).reshape(1, edges)
    yk = (key % wide).reshape(1, edges)
    return pl.pallas_call(
        functools.partial(count_kernel, chunk),
        out_shape=jax.ShapeDtypeStruct((rows, keys), jnp.bfloat16),
        in_specs=[vmem(), vmem()],
        out_specs=vmem(),
        scratch_shapes=[pltpu.VMEM((tall, wide), jnp.float32)],
        name="count",
    )(xk, yk)


def select_kernel(members, per_part, idx_ref, a_ref, b_ref, c_ref, out_ref):
    listed = 3 * per_part

    def one(d, carry):
        base = d * listed
        for t in range(listed):
            src = (a_ref, b_ref, c_ref)[t // per_part]
            at = jnp.bitwise_and(idx_ref[base + t], members - 1)
            out_ref[base + t] = src[at]
        return carry

    lax.fori_loop(0, members, one, 0)


def select(idx, left, own, right, per_part):
    members = own.shape[0]
    return pl.pallas_call(
        functools.partial(select_kernel, members, per_part),
        out_shape=jax.ShapeDtypeStruct((members * 3 * per_part, SUB, LANE), own.dtype),
        in_specs=[smem(), vmem(), vmem(), vmem()],
        out_specs=vmem(),
        name="select",
    )(idx, left, own, right)


def layer_kernel(listed, slab_ref, x_ref, weight_ref, dinv_ref, bias_ref, cot_ref, hid_ref, part_ref):
    dinv = dinv_ref[...]
    groups = part_ref.shape[1]
    span = listed * SUB
    rows = [jnp.dot(slab_ref[...], x_ref[half], preferred_element_type=jnp.float32) for half in range(2)]
    gathered = jnp.concatenate(rows, axis=1)
    high = gathered.astype(jnp.bfloat16)
    low = (gathered - high.astype(jnp.float32)).astype(jnp.bfloat16)
    weight = weight_ref[...]
    total = jnp.dot(high, weight, preferred_element_type=jnp.float32)
    total = total + jnp.dot(low, weight, preferred_element_type=jnp.float32)
    pre = total * dinv + bias_ref[...]
    sig = jax.nn.sigmoid(pre)
    hid_ref[...] = (pre * sig).astype(hid_ref.dtype)
    grad_pre = cot_ref[...].astype(jnp.float32) * sig * (1.0 + pre * (1.0 - sig))
    back = (grad_pre * dinv).astype(jnp.bfloat16)
    contract = (((0,), (0,)), ((), ()))
    grad = lax.dot_general(high, back, contract, preferred_element_type=jnp.float32)
    grad = grad + lax.dot_general(low, back, contract, preferred_element_type=jnp.float32)
    sums = jnp.sum(grad_pre, axis=0, keepdims=True)
    sums_high = sums.astype(jnp.bfloat16).astype(jnp.float32)
    sums_low = sums - sums_high
    at = lax.broadcasted_iota(jnp.int32, (SUB, LANE), 0)
    extra = jnp.zeros((SUB, LANE), jnp.float32)
    for index, value in enumerate((sums_high, sums_low)):
        for half in range(2):
            lanes = slice(half * LANE, (half + 1) * LANE)
            extra = jnp.where(at == 2 * index + half, value[:, lanes], extra)
    extra = extra.astype(jnp.bfloat16)
    for half in range(2):
        lanes = slice(half * LANE, (half + 1) * LANE)
        partial = lax.dot_general(slab_ref[...], back[:, lanes], contract, preferred_element_type=jnp.float32)
        for a in range(groups):
            piece = partial[a * span : (a + 1) * span, :].reshape(listed, SUB, LANE)
            part_ref[half, a, pl.ds(0, listed)] = piece.astype(jnp.bfloat16)
            part_ref[half, a, listed] = extra
            top = (half * groups + a) * SUB
            for other in range(2):
                block = grad[top : top + SUB, other * LANE : (other + 1) * LANE]
                part_ref[half, a, listed + 1 + other] = block.astype(jnp.bfloat16)


def layer(slab, x, weight, dinv, bias, cotangent, listed):
    rows, width = cotangent.shape
    groups = rows // SUB
    return pl.pallas_call(
        functools.partial(layer_kernel, listed),
        out_shape=(
            jax.ShapeDtypeStruct((rows, width), jnp.bfloat16),
            jax.ShapeDtypeStruct((2, groups, listed + 3, SUB, LANE), jnp.bfloat16),
        ),
        in_specs=[vmem()] * 6,
        out_specs=(vmem(), vmem()),
        name="layer",
    )(slab, x, weight, dinv, bias, cotangent)


def collect_kernel(members, per_part, chains, idx_ref, got_ref, prev_ref, own_ref, next_ref, acc_ref):
    listed = 3 * per_part
    acc_ref[...] = jnp.zeros_like(acc_ref)

    def some(step, carry):
        for t in range(listed):
            for j in range(chains):
                d = step * chains + j
                at = jnp.bitwise_and(idx_ref[d * listed + t], members - 1)
                acc_ref[j, t // per_part, at] += got_ref[d, t].astype(jnp.float32)
        return carry

    lax.fori_loop(0, members // chains, some, 0)
    for k, ref in enumerate((prev_ref, own_ref, next_ref)):
        value = acc_ref[0, k]
        for j in range(1, chains):
            value = value + acc_ref[j, k]
        ref[...] = value.astype(ref.dtype)


def collect(idx, got, per_part):
    members = got.shape[0]
    chains = 4
    piece = (members, SUB, LANE)
    return pl.pallas_call(
        functools.partial(collect_kernel, members, per_part, chains),
        out_shape=(
            jax.ShapeDtypeStruct(piece, jnp.bfloat16),
            jax.ShapeDtypeStruct(piece, jnp.float32),
            jax.ShapeDtypeStruct(piece, jnp.bfloat16),
        ),
        in_specs=[smem(), vmem()],
        out_specs=(vmem(),) * 3,
        scratch_shapes=[pltpu.VMEM((chains, 3) + piece, jnp.float32)],
        name="collect",
    )(idx, got)


def swap(x, axis):
    return lax.all_to_all(x, axis, 0, 0, tiled=True)


def per_device(features, weight, bias, cotangent, degree, tile_cols, edge_tile, edge_row, edge_col):
    rows, width = features.shape
    members = lax.axis_size("grp")
    rings = lax.axis_size("rep")
    listed = tile_cols.shape[1]
    per_part = listed // 3
    groups = rows // SUB
    dinv = lax.rsqrt(degree.astype(jnp.float32))[:, None]

    scaled = (features.astype(jnp.float32) * dinv).astype(jnp.bfloat16)
    cut = scaled.reshape(groups, SUB, 2, LANE).transpose(2, 0, 1, 3).reshape(members, SUB, LANE)
    lane = lax.broadcasted_iota(jnp.int32, (groups, SUB, LANE), 2)
    names = jnp.pad(tile_cols[0], (0, LANE - listed))
    note = jnp.where(lane < LANE // 2, names[None, None, :], degree.reshape(groups, SUB, 1)).astype(jnp.bfloat16)
    got = swap(jnp.stack([cut, jnp.concatenate([note, note], axis=0)], axis=1), "grp")
    own = got[:, 0]
    idx = got[:, 1, 0, :listed].astype(jnp.int32).reshape(-1)
    dinv_piece = lax.rsqrt(got[:, 1, :, LANE // 2].astype(jnp.float32))[:, :, None]
    from_left = shifted(own, "rep", 1)
    from_right = shifted(own, "rep", -1)

    tile = edge_tile[0]
    col = edge_col[0]
    key = (col // SUB) * (listed * SUB) + tile * SUB + col % SUB
    slab = build_slab(edge_row[0], key, rows, listed * rows)

    chosen = select(idx, from_left, own, from_right, per_part)
    window = swap(chosen.reshape(members, listed, SUB, LANE), "grp")
    hidden, partial = layer(
        slab, window.reshape(2, listed * rows, LANE), weight, dinv, bias[None, :], cotangent, listed
    )
    mine = swap(partial.reshape(members, listed + 3, SUB, LANE), "grp")

    share = mine[:, listed:].astype(jnp.float32).sum(axis=0)
    share = swap(jnp.broadcast_to(share[None], (rings, 3, SUB, LANE)), "rep")
    share = share.sum(axis=0)
    grad_bias = jnp.concatenate([share[0, 0] + share[0, 2], share[0, 1] + share[0, 3]])

    previous_part, own_part, next_part = collect(idx, mine, per_part)
    from_next = shifted(previous_part, "rep", -1)
    from_previous = shifted(next_part, "rep", 1)
    grad_sum = own_part + from_next.astype(jnp.float32) + from_previous.astype(jnp.float32)
    grad_piece = (grad_sum * dinv_piece).astype(jnp.bfloat16)
    final = jnp.broadcast_to(share[None, 1:].astype(jnp.bfloat16), (members, 2, SUB, LANE))
    final = swap(jnp.concatenate([grad_piece[:, None], final], axis=1), "grp")
    grad_scaled = final[:, 0].reshape(2, rows, LANE).transpose(1, 0, 2).reshape(rows, width)
    grad_features = lax.dot_general(
        grad_scaled, weight, (((1,), (1,)), ((), ())), preferred_element_type=jnp.float32
    ).astype(jnp.bfloat16)
    grad_weight = final[:, 1:].transpose(0, 2, 1, 3).reshape(width, width).astype(jnp.float32)
    return (hidden, grad_features, grad_weight, grad_bias)


def solution(mesh):
    return jax.shard_map(
        per_device,
        mesh=mesh,
        in_specs=(
            P(("rep", "grp"), None),
            P(),
            P(),
            P(("rep", "grp"), None),
            P(("rep", "grp")),
            P(("rep", "grp"), None),
            P(("rep", "grp"), None),
            P(("rep", "grp"), None),
            P(("rep", "grp"), None),
        ),
        out_specs=(P(("rep", "grp"), None), P(("rep", "grp"), None), P(), P()),
        check_vma=False,
    )
```

time: 217 us -> 196 us (0.903)
  waiting for transfers between devices: 113 us -> 100 us
  starting transfers between devices: 52.3 us -> 42.8 us
    all_to_all x5 -> x4, starting transfers between devices: 31.6 us -> 21.5 us  [swap(): return lax.all_to_all(x, axis, 0, 0, tiled=True)]
    all_to_all x5 -> x4, waiting for transfers between devices: 103 us -> 94.3 us  [swap(): return lax.all_to_all(x, axis, 0, 0, tiled=True)]
    ppermute x4, waiting for transfers between devices: 9.78 us -> 5.96 us  [shifted(): return lax.ppermute(x, axis, [(i, (i + by) % size) for i in range(size)])]
  transfers between devices with their start and end apart: 9 -> 8, of which waited for: 7 -> 5; matrix products, arithmetic and copies ran while one was open for 2% -> 3% of each run, Pallas kernels for 2% -> 3%
where the time goes in v3:
time: 196 us; the launch traced here: 195 us
  waiting for transfers between devices  100 us (51%)
  starting transfers between devices  42.8 us (22%)
  blocking collectives  18.9 us (10%)
  Pallas kernels  17 us (9%)
  other arithmetic  7.22 us (4%)
  local copies, waits for them, and re-layouts  7.02 us (4%)
    all_to_all x4, waiting for transfers between devices, swap(): return lax.all_to_all(x, axis, 0, 0, tiled=True)  94.3 us
    all_to_all x4, starting transfers between devices, swap(): return lax.all_to_all(x, axis, 0, 0, tiled=True)  21.5 us
    ppermute x4, starting transfers between devices, shifted(): return lax.ppermute(x, axis, [(i, (i + by) % size) for i in range(size)])  21.3 us
    all_to_all x1, blocking collectives, swap(): return lax.all_to_all(x, axis, 0, 0, tiled=True)  18.9 us
    ppermute x4, waiting for transfers between devices, shifted(): return lax.ppermute(x, axis, [(i, (i + by) % size) for i in range(size)])  5.96 us
    pallas_call x1, Pallas kernels, build_slab(): pl.pallas_call(functools.partial(count_kernel, chunk), out_shape=jax.Shap...  4.91 us
    pallas_call x1, Pallas kernels, collect(): pl.pallas_call(functools.partial(collect_kernel, members, per_part, chain...  4.41 us
    pallas_call x1, Pallas kernels, layer(): pl.pallas_call(functools.partial(layer_kernel, listed), out_shape=(jax.Sh...  4.35 us
  transfers between devices with their start and end apart: 8, of which 5 were waited for; matrix products, arithmetic and copies ran while one was open for 3% of the time, Pallas kernels for 3%

profile of v3, /device:TPU:1, one launch (start us, length us, event | category | flops | bytes accessed | tf_op | source)
XLA Modules:
  0.0 194.8 jit_solution(13502998603103490587)
XLA Ops:
  2.8 0.9 fusion
  3.8 18.9 %all_to_all.25 = bf16[32,2,8,128]{3,2,1,0:T(8,128)(2,1)S(1)} all-to-all(bf16[32,2,8,128]{3,2,1,0:T(8,128)(2,1)S(1)} %pad_maximum_fusion.1), channel_id=1, replica_groups=mesh['rep'=16,'grp'=32] {'grp'}, dimensions={0} | all-to-all | bytes 262144 | tf_op jit(solution)/shard_map/all_to_all | solution.py:185
  22.7 12.6 %collective-permute-start.1 = (bf16[32,8,128]{2,1,0:T(8,128)(2,1)S(1)}, bf16[32,8,128]{2,1,0:T(8,128)(2,1)S(1)}, u32[]{:S(2)}, u32[]{:S(2)}) collective-permute-start(bf16[32,8,128]{2,1,0:T(8,128)(2,1)S(1)} %slice_bitcast_fusion.b_ref), channel_id=1, source_target_pairs={{0,480},{32,0},{64,32},{96,64},{128,96},{160,128},{192,160},{224,1... | collective-permute-start | bytes 196616 | tf_op jit(solution)/shard_map/ppermute | solution.py:17
  35.3 1.9 collective-permute-start
  38.0 5.9 %collective-permute-done.a_ref = bf16[32,8,128]{2,1,0:T(8,128)(2,1)S(1)} collective-permute-done((bf16[32,8,128]{2,1,0:T(8,128)(2,1)S(1)}, bf16[32,8,128]{2,1,0:T(8,128)(2,1)S(1)}, u32[]{:S(2)}, u32[]{:S(2)}) %collective-permute-start) | collective-permute-done | bytes 65568 | tf_op jit(solution)/shard_map/ppermute | solution.py:17
  44.6 3.3 %select.26 = bf16[768,8,128]{2,1,0:T(8,128)(2,1)} custom-call(s32[768]{0:T(1024)} %reshape.54.idx_ref, bf16[32,8,128]{2,1,0:T(8,128)(2,1)} %copy-done.5, bf16[32,8,128]{2,1,0:T(8,128)(2,1)} %copy-done.3, bf16[32,8,128]{2,1,0:T(8,128)(2,1)} %copy-done.4), custom_call_target="tpu_custom_call" | custom-call | tf_op jit(solution)/shard_map/select/pallas_call | solution.py:80
  47.9 5.6 %all-to-all-start.1 = ((bf16[32,24,8,128]{3,2,1,0:T(8,128)(2,1)}), bf16[32,24,8,128]{3,2,1,0:T(8,128)(2,1)S(1)}, u32[]{:S(2)}, u32[]{:S(2)}) async-start(bf16[32,24,8,128]{3,2,1,0:T(8,128)(2,1)} %bitcast.41), calls=%async_computation.1 | async-start | bytes 3145728 | tf_op jit(solution)/shard_map/all_to_all | solution.py:185
  55.8 4.9 %count.1.slab_ref = bf16[128,3072]{1,0:T(8,128)(2,1)} custom-call(s32[1,3840]{1,0:T(1,128)} %multiply_add_fusion.xk_ref, s32[1,3840]{1,0:T(1,128)} %get-tuple-element.14.yk_ref), custom_call_target="tpu_custom_call" | custom-call | tf_op jit(solution)/shard_map/count/pallas_call | solution.py:54
  60.7 32.0 %all-to-all-done.1 = bf16[32,24,8,128]{3,2,1,0:T(8,128)(2,1)S(1)} async-done(((bf16[32,24,8,128]{3,2,1,0:T(8,128)(2,1)}), bf16[32,24,8,128]{3,2,1,0:T(8,128)(2,1)S(1)}, u32[]{:S(2)}, u32[]{:S(2)}) %all-to-all-start.1) | async-done | bytes 1572896 | tf_op jit(solution)/shard_map/all_to_all | solution.py:185
  92.7 1.1 copy-done.1
  93.8 4.4 %layer.1 = (bf16[128,256]{1,0:T(8,128)(2,1)}, bf16[2,16,27,8,128]{4,3,2,1,0:T(8,128)(2,1)}) custom-call(bf16[128,3072]{1,0:T(8,128)(2,1)} %count.1.slab_ref, bf16[2,3072,128]{2,1,0:T(8,128)(2,1)} %bitcast.40, bf16[256,256]{1,0:T(8,128)(2,1)} %weight_ref.1, f32[128,1]{1,0:T(8,128)} %copy.42.dinv_ref, f32[1,256]{1,0:T(1,128)} %bitcast.46, bf16[128,256]{1,0:T(8,128)(2,1)} %cot_ref.1), custom_call_target="tpu_custom_call" | custom-call | tf_op jit(solution)/shard_map/layer/pallas_call | solution.py:134
  98.2 5.3 %all-to-all-start.2 = ((bf16[32,27,8,128]{3,2,1,0:T(8,128)(2,1)}), bf16[32,27,8,128]{3,2,1,0:T(8,128)(2,1)S(1)}, u32[]{:S(2)}, u32[]{:S(2)}) async-start(bf16[32,27,8,128]{3,2,1,0:T(8,128)(2,1)} %bitcast.42), calls=%async_computation.2 | async-start | bytes 3538944 | tf_op jit(solution)/shard_map/all_to_all | solution.py:185
  103.7 43.0 %all-to-all-done.2.got_ref = bf16[32,27,8,128]{3,2,1,0:T(8,128)(2,1)S(1)} async-done(((bf16[32,27,8,128]{3,2,1,0:T(8,128)(2,1)}), bf16[32,27,8,128]{3,2,1,0:T(8,128)(2,1)S(1)}, u32[]{:S(2)}, u32[]{:S(2)}) %all-to-all-start.2) | async-done | bytes 1769504 | tf_op jit(solution)/shard_map/all_to_all | solution.py:185
  146.7 1.2 copy-done
  148.0 4.4 %collect.1 = (bf16[32,8,128]{2,1,0:T(8,128)(2,1)}, f32[32,8,128]{2,1,0:T(8,128)}, bf16[32,8,128]{2,1,0:T(8,128)(2,1)}) custom-call(s32[768]{0:T(1024)} %reshape.54.idx_ref, bf16[32,27,8,128]{3,2,1,0:T(8,128)(2,1)} %copy-done), custom_call_target="tpu_custom_call" | custom-call | tf_op jit(solution)/shard_map/collect/pallas_call | solution.py:170
  152.4 1.9 collective-permute-start.2
  154.3 4.9 %collective-permute-start.3 = (bf16[32,8,128]{2,1,0:T(8,128)(2,1)}, bf16[32,8,128]{2,1,0:T(8,128)(2,1)S(1)}, u32[]{:S(2)}, u32[]{:S(2)}) collective-permute-start(bf16[32,8,128]{2,1,0:T(8,128)(2,1)} %get-tuple-element.13), channel_id=1, source_target_pairs={{0,32},{32,64},{64,96},{96,128},{128,160},{160,192},{192,224},{224... | collective-permute-start | bytes 196616 | tf_op jit(solution)/shard_map/ppermute | solution.py:17
  159.2 1.0 convert_reduce_fusion
  160.8 3.5 %all-to-all-start.3 = ((f32[16,3,8,128]{3,2,1,0:T(8,128)}), f32[16,3,8,128]{3,2,1,0:T(8,128)S(1)}, u32[]{:S(2)}, u32[]{:S(2)}) async-start(f32[16,3,8,128]{3,2,1,0:T(8,128)} %broadcast_in_dim.47), calls=%async_computation.3 | async-start | bytes 393216 | tf_op jit(solution)/shard_map/all_to_all | solution.py:185
  164.5 1.0 fusion.1
  165.5 9.4 %all-to-all-done.3 = f32[16,3,8,128]{3,2,1,0:T(8,128)S(1)} async-done(((f32[16,3,8,128]{3,2,1,0:T(8,128)}), f32[16,3,8,128]{3,2,1,0:T(8,128)S(1)}, u32[]{:S(2)}, u32[]{:S(2)}) %all-to-all-start.3) | async-done | bytes 196640 | tf_op jit(solution)/shard_map/all_to_all | solution.py:185
  175.7 7.0 %all-to-all-start.4 = ((bf16[32,3,8,128]{3,2,1,0:T(8,128)(2,1)}), bf16[32,3,8,128]{3,2,1,0:T(8,128)(2,1)S(1)}, u32[]{:S(2)}, u32[]{:S(2)}) async-start(bf16[32,3,8,128]{3,2,1,0:T(8,128)(2,1)} %pad_maximum_fusion), calls=%async_computation.4 | async-start | bytes 393216 | tf_op jit(solution)/shard_map/all_to_all | solution.py:185
  183.2 9.9 %all-to-all-done.4 = bf16[32,3,8,128]{3,2,1,0:T(8,128)(2,1)S(1)} async-done(((bf16[32,3,8,128]{3,2,1,0:T(8,128)(2,1)}), bf16[32,3,8,128]{3,2,1,0:T(8,128)(2,1)S(1)}, u32[]{:S(2)}, u32[]{:S(2)}) %all-to-all-start.4) | async-done | bytes 196640 | tf_op jit(solution)/shard_map/all_to_all | solution.py:185
  193.3 0.8 convolution_convert_fusion
  (47 shorter events, 9.0 us)
Async XLA Ops:
  22.7 21.3 %copy-start.3 = (bf16[32,8,128]{2,1,0:T(8,128)(2,1)}, bf16[32,8,128]{2,1,0:T(8,128)(2,1)S(1)}, u32[]{:S(2)}) copy-start(bf16[32,8,128]{2,1,0:T(8,128)(2,1)S(1)} %slice_bitcast_fusion.b_ref) | copy-start | bytes 196612
  22.7 15.3 %collective-permute-start.1 = (bf16[32,8,128]{2,1,0:T(8,128)(2,1)S(1)}, bf16[32,8,128]{2,1,0:T(8,128)(2,1)S(1)}, u32[]{:S(2)}, u32[]{:S(2)}) collective-permute-start(bf16[32,8,128]{2,1,0:T(8,128)(2,1)S(1)} %slice_bitcast_fusion.b_ref), channel_id=1, source_target_pairs={{0,480},{32,0},{64,32},{96,64},{128,96},{160,128},{192,160},{224,1... | collective-permute-start | bytes 196616 | tf_op jit(solution)/shard_map/ppermute | solution.py:17
  35.3 8.6 %collective-permute-start = (bf16[32,8,128]{2,1,0:T(8,128)(2,1)S(1)}, bf16[32,8,128]{2,1,0:T(8,128)(2,1)S(1)}, u32[]{:S(2)}, u32[]{:S(2)}) collective-permute-start(bf16[32,8,128]{2,1,0:T(8,128)(2,1)S(1)} %slice_bitcast_fusion.b_ref), channel_id=1, source_target_pairs={{0,32},{32,64},{64,96},{96,128},{128,160},{160,192},{192,224},{224... | collective-permute-start | bytes 196616 | tf_op jit(solution)/shard_map/ppermute | solution.py:17
  38.0 6.0 %copy-start.4 = (bf16[32,8,128]{2,1,0:T(8,128)(2,1)}, bf16[32,8,128]{2,1,0:T(8,128)(2,1)S(1)}, u32[]{:S(2)}) copy-start(bf16[32,8,128]{2,1,0:T(8,128)(2,1)S(1)} %collective-permute-done.1.c_ref) | copy-start | bytes 196612
  44.0 0.6 copy-start.5
  47.9 6.4 %copy-start.7 = (s32[1,3840]{1,0:T(1,128)S(1)}, s32[1,3840]{1,0:T(1,128)}, u32[]{:S(2)}) copy-start(s32[1,3840]{1,0:T(1,128)} %param.15) | copy-start | bytes 46084
  47.9 6.4 %copy-start.8 = (s32[1,3840]{1,0:T(1,128)S(1)}, s32[1,3840]{1,0:T(1,128)}, u32[]{:S(2)}) copy-start(s32[1,3840]{1,0:T(1,128)} %param.17) | copy-start | bytes 46084
  47.9 7.2 %copy-start.6 = (s32[1,3840]{1,0:T(1,128)S(1)}, s32[1,3840]{1,0:T(1,128)}, u32[]{:S(2)}) copy-start(s32[1,3840]{1,0:T(1,128)} %param.16) | copy-start | bytes 46084
  47.9 44.8 %all-to-all-start.1 = ((bf16[32,24,8,128]{3,2,1,0:T(8,128)(2,1)}), bf16[32,24,8,128]{3,2,1,0:T(8,128)(2,1)S(1)}, u32[]{:S(2)}, u32[]{:S(2)}) async-start(bf16[32,24,8,128]{3,2,1,0:T(8,128)(2,1)} %bitcast.41), calls=%async_computation.1 | async-start | bytes 3145728 | tf_op jit(solution)/shard_map/all_to_all | solution.py:185
  92.7 1.1 copy-start.1
  98.2 48.5 %all-to-all-start.2 = ((bf16[32,27,8,128]{3,2,1,0:T(8,128)(2,1)}), bf16[32,27,8,128]{3,2,1,0:T(8,128)(2,1)S(1)}, u32[]{:S(2)}, u32[]{:S(2)}) async-start(bf16[32,27,8,128]{3,2,1,0:T(8,128)(2,1)} %bitcast.42), calls=%async_computation.2 | async-start | bytes 3538944 | tf_op jit(solution)/shard_map/all_to_all | solution.py:185
  103.7 89.5 %copy-start.2 = (bf16[256,256]{1,0:T(8,128)(2,1)S(1)}, bf16[256,256]{1,0:T(8,128)(2,1)}, u32[]{:S(2)}) copy-start(bf16[256,256]{1,0:T(8,128)(2,1)} %weight_ref.1) | copy-start | bytes 393220
  146.7 1.2 copy-start
  152.4 12.1 %collective-permute-start.2 = (bf16[32,8,128]{2,1,0:T(8,128)(2,1)}, bf16[32,8,128]{2,1,0:T(8,128)(2,1)S(1)}, u32[]{:S(2)}, u32[]{:S(2)}) collective-permute-start(bf16[32,8,128]{2,1,0:T(8,128)(2,1)} %get-tuple-element.12), channel_id=1, source_target_pairs={{0,480},{32,0},{64,32},{96,64},{128,96},{160,128},{192,160},{224,1... | collective-permute-start | bytes 196616 | tf_op jit(solution)/shard_map/ppermute | solution.py:17
  154.3 10.2 %collective-permute-start.3 = (bf16[32,8,128]{2,1,0:T(8,128)(2,1)}, bf16[32,8,128]{2,1,0:T(8,128)(2,1)S(1)}, u32[]{:S(2)}, u32[]{:S(2)}) collective-permute-start(bf16[32,8,128]{2,1,0:T(8,128)(2,1)} %get-tuple-element.13), channel_id=1, source_target_pairs={{0,32},{32,64},{64,96},{96,128},{128,160},{160,192},{192,224},{224... | collective-permute-start | bytes 196616 | tf_op jit(solution)/shard_map/ppermute | solution.py:17
  160.8 14.1 %all-to-all-start.3 = ((f32[16,3,8,128]{3,2,1,0:T(8,128)}), f32[16,3,8,128]{3,2,1,0:T(8,128)S(1)}, u32[]{:S(2)}, u32[]{:S(2)}) async-start(f32[16,3,8,128]{3,2,1,0:T(8,128)} %broadcast_in_dim.47), calls=%async_computation.3 | async-start | bytes 393216 | tf_op jit(solution)/shard_map/all_to_all | solution.py:185
  175.7 17.5 %all-to-all-start.4 = ((bf16[32,3,8,128]{3,2,1,0:T(8,128)(2,1)}), bf16[32,3,8,128]{3,2,1,0:T(8,128)(2,1)S(1)}, u32[]{:S(2)}, u32[]{:S(2)}) async-start(bf16[32,3,8,128]{3,2,1,0:T(8,128)(2,1)} %pad_maximum_fusion), calls=%async_computation.4 | async-start | bytes 393216 | tf_op jit(solution)/shard_map/all_to_all | solution.py:185

commit v4 on v3

v4 whole, which is shorter than its diff:
```python
import functools

import jax
import jax.numpy as jnp
from jax import lax
from jax.experimental import pallas as pl
from jax.experimental.pallas import tpu as pltpu
from jax.sharding import PartitionSpec as P


SUB = 8
LANE = 128
MIB = 1 << 20


def with_partner(x, axis):
    return lax.ppermute(x, axis, [(i, i ^ 1) for i in range(lax.axis_size(axis))])


def with_other(x, axis):
    size = lax.axis_size(axis)
    return lax.ppermute(x, axis, [(i, (i + 1 if i % 2 else i - 1) % size) for i in range(size)])


def vmem():
    return pl.BlockSpec(memory_space=pltpu.VMEM)


def smem():
    return pl.BlockSpec(memory_space=pltpu.SMEM)


def hbm():
    return pl.BlockSpec(memory_space=pltpu.HBM)


def call(kernel, mib, out_shape, in_specs, out_specs, scratch=()):
    return pl.pallas_call(
        kernel,
        out_shape=out_shape,
        in_specs=in_specs,
        out_specs=out_specs,
        scratch_shapes=list(scratch),
        compiler_params=pltpu.CompilerParams(vmem_limit_bytes=mib * MIB),
    )


def cut_kernel(x_ref, degree_ref, cols_ref, out_ref, dinv_ref, names_ref):
    rows = x_ref.shape[0]
    groups = rows // SUB
    square = (rows, rows)
    diagonal = lax.broadcasted_iota(jnp.int32, square, 0) == lax.broadcasted_iota(jnp.int32, square, 1)
    degree = jnp.sum(jnp.where(diagonal, degree_ref[...].astype(jnp.float32), 0.0), axis=1, keepdims=True)
    dinv = lax.rsqrt(degree)
    dinv_ref[...] = dinv
    names_ref[...] = jnp.zeros_like(names_ref)
    names_ref[:, pl.ds(0, cols_ref.shape[1])] = cols_ref[...].astype(jnp.float32)
    lane = lax.broadcasted_iota(jnp.int32, (rows, LANE), 1)
    note = jnp.where(lane < LANE // 2, names_ref[...], degree).reshape(groups, SUB, LANE).astype(jnp.bfloat16)
    for half in range(2):
        scaled = x_ref[:, half * LANE : (half + 1) * LANE].astype(jnp.float32) * dinv
        scaled = scaled.reshape(groups, SUB, LANE).astype(jnp.bfloat16)
        for a in range(groups):
            out_ref[half * groups + a, 0] = scaled[a]
            out_ref[half * groups + a, 1] = note[a]


def cut(features, degree, cols):
    rows = features.shape[0]
    return call(
        cut_kernel,
        60,
        (
            jax.ShapeDtypeStruct((2 * rows // SUB, 2, SUB, LANE), jnp.bfloat16),
            jax.ShapeDtypeStruct((rows, 1), jnp.float32),
        ),
        [vmem()] * 3,
        (vmem(), vmem()),
        [pltpu.VMEM((1, LANE), jnp.float32)],
    )(features, degree, cols)


def count_kernel(chunk, xk_ref, yk_ref, out_ref, acc_ref):
    edges = xk_ref.shape[1]
    tall = acc_ref.shape[0]
    wide = acc_ref.shape[1]
    for step in range(edges // chunk):
        xk = xk_ref[:, pl.ds(step * chunk, chunk)]
        yk = yk_ref[:, pl.ds(step * chunk, chunk)]
        left = (lax.broadcasted_iota(jnp.int32, (tall, chunk), 0) == xk).astype(jnp.float32).astype(jnp.bfloat16)
        right = (lax.broadcasted_iota(jnp.int32, (wide, chunk), 0) == yk).astype(jnp.float32).astype(jnp.bfloat16)
        part = lax.dot_general(left, right, (((1,), (1,)), ((), ())), preferred_element_type=jnp.float32)
        if step == 0:
            acc_ref[...] = part
        else:
            acc_ref[...] += part
    rows = out_ref.shape[0]
    for block in range(tall // rows):
        out_ref[:, pl.ds(block * wide, wide)] = acc_ref[pl.ds(block * rows, rows), :].astype(jnp.bfloat16)


def build_slab(row, key, rows, keys):
    wide = 256
    edges = row.shape[0]
    chunk = 768 if edges % 768 == 0 else 128
    tall = rows * (keys // wide)
    xk = ((key // wide) * rows + row).reshape(1, edges)
    yk = (key % wide).reshape(1, edges)
    return pl.pallas_call(
        functools.partial(count_kernel, chunk),
        out_shape=jax.ShapeDtypeStruct((rows, keys), jnp.bfloat16),
        in_specs=[vmem(), vmem()],
        out_specs=vmem(),
        scratch_shapes=[pltpu.VMEM((tall, wide), jnp.float32)],
        compiler_params=pltpu.CompilerParams(vmem_limit_bytes=24 * MIB),
        name="count",
    )(xk, yk)


def select_kernel(members, per_part, idx_ref, first_ref, own_ref, second_ref, out_ref, near_ref, made_ref, sems):
    listed = 3 * per_part
    near_ref[pl.ds(0, members)] = first_ref[...]
    near_ref[pl.ds(members, members)] = second_ref[...]
    steps = sems.shape[0]
    span = members // steps

    def one(d, carry):
        for t in range(listed):
            at = idx_ref[d * listed + t]
            if t // per_part == 1:
                made_ref[d, t] = own_ref[jnp.bitwise_and(at, members - 1)]
            else:
                made_ref[d, t] = near_ref[jnp.bitwise_and(at, 2 * members - 1)]
        return carry

    copies = []
    for step in range(steps):
        lax.fori_loop(step * span, (step + 1) * span, one, 0)
        part = pl.ds(step * span, span)
        copies.append(pltpu.make_async_copy(made_ref.at[part], out_ref.at[part], sems.at[step]))
        copies[-1].start()
    for copy in copies:
        copy.wait()


def select(idx, first, own, second, per_part):
    members = own.shape[0]
    shape = (members, 3 * per_part, SUB, LANE)
    return call(
        functools.partial(select_kernel, members, per_part),
        6,
        jax.ShapeDtypeStruct(shape, own.dtype),
        [smem()] + [vmem()] * 3,
        hbm(),
        [
            pltpu.VMEM((2 * members, SUB, LANE), own.dtype),
            pltpu.VMEM(shape, own.dtype),
            pltpu.SemaphoreType.DMA((4,)),
        ],
    )(idx, first, own, second)


def layer_kernel(listed, slab_ref, x_ref, weight_ref, dinv_ref, bias_ref, cot_ref, hid_ref, out_ref, part_ref, sems):
    dinv = dinv_ref[...]
    groups = part_ref.shape[1]
    span = listed * SUB
    rows = [jnp.dot(slab_ref[...], x_ref[half], preferred_element_type=jnp.float32) for half in range(2)]
    gathered = jnp.concatenate(rows, axis=1)
    high = gathered.astype(jnp.bfloat16)
    low = (gathered - high.astype(jnp.float32)).astype(jnp.bfloat16)
    weight = weight_ref[...]
    total = jnp.dot(high, weight, preferred_element_type=jnp.float32)
    total = total + jnp.dot(low, weight, preferred_element_type=jnp.float32)
    pre = total * dinv + bias_ref[...]
    sig = jax.nn.sigmoid(pre)
    hid_ref[...] = (pre * sig).astype(hid_ref.dtype)
    grad_pre = cot_ref[...].astype(jnp.float32) * sig * (1.0 + pre * (1.0 - sig))
    back = (grad_pre * dinv).astype(jnp.bfloat16)
    contract = (((0,), (0,)), ((), ()))
    grad = lax.dot_general(high, back, contract, preferred_element_type=jnp.float32)
    grad = grad + lax.dot_general(low, back, contract, preferred_element_type=jnp.float32)
    sums = jnp.sum(grad_pre, axis=0, keepdims=True)
    sums_high = sums.astype(jnp.bfloat16).astype(jnp.float32)
    sums_low = sums - sums_high
    at = lax.broadcasted_iota(jnp.int32, (SUB, LANE), 0)
    extra = jnp.zeros((SUB, LANE), jnp.float32)
    for index, value in enumerate((sums_high, sums_low)):
        for half in range(2):
            lanes = slice(half * LANE, (half + 1) * LANE)
            extra = jnp.where(at == 2 * index + half, value[:, lanes], extra)
    extra = extra.astype(jnp.bfloat16)
    copies = []
    for half in range(2):
        lanes = slice(half * LANE, (half + 1) * LANE)
        partial = lax.dot_general(slab_ref[...], back[:, lanes], contract, preferred_element_type=jnp.float32)
        for a in range(groups):
            piece = partial[a * span : (a + 1) * span, :].reshape(listed, SUB, LANE)
            part_ref[half, a, pl.ds(0, listed)] = piece.astype(jnp.bfloat16)
            part_ref[half, a, listed] = extra
            top = (half * groups + a) * SUB
            for other in range(2):
                block = grad[top : top + SUB, other * LANE : (other + 1) * LANE]
                part_ref[half, a, listed + 1 + other] = block.astype(jnp.bfloat16)
        copies.append(pltpu.make_async_copy(part_ref.at[half], out_ref.at[half], sems.at[half]))
        copies[-1].start()
    for copy in copies:
        copy.wait()


def layer(slab, x, weight, dinv, bias, cotangent, listed):
    rows, width = cotangent.shape
    shape = (2, rows // SUB, listed + 3, SUB, LANE)
    return call(
        functools.partial(layer_kernel, listed),
        16,
        (jax.ShapeDtypeStruct((rows, width), jnp.bfloat16), jax.ShapeDtypeStruct(shape, jnp.bfloat16)),
        [vmem()] * 6,
        (vmem(), hbm()),
        [pltpu.VMEM(shape, jnp.bfloat16), pltpu.SemaphoreType.DMA((2,))],
    )(slab, x, weight, dinv, bias, cotangent)


def collect_kernel(members, per_part, parts, chains, idx_ref, got_ref, *refs):
    outs, acc_ref = refs[:-1], refs[-1]
    acc_ref[...] = jnp.zeros_like(acc_ref)
    tiles = acc_ref.shape[1]

    def some(step, carry):
        for part in parts:
            for t in range(part * per_part, (part + 1) * per_part):
                for j in range(chains):
                    d = step * chains + j
                    at = jnp.bitwise_and(idx_ref[d * 3 * per_part + t], tiles - 1)
                    acc_ref[j, at] += got_ref[d, t].astype(jnp.float32)
        return carry

    lax.fori_loop(0, members // chains, some, 0)
    for number, ref in enumerate(outs):
        part = pl.ds(number * members, members)
        value = acc_ref[0, part]
        for j in range(1, chains):
            value = value + acc_ref[j, part]
        ref[...] = value.astype(ref.dtype)


def collect(idx, parts, got, per_part, dtype):
    members = got.shape[0]
    chains = 4
    piece = (members, SUB, LANE)
    return call(
        functools.partial(collect_kernel, members, per_part, parts, chains),
        6,
        tuple(jax.ShapeDtypeStruct(piece, dtype) for _ in parts),
        [smem(), vmem()],
        (vmem(),) * len(parts),
        [pltpu.VMEM((chains, len(parts) * members, SUB, LANE), jnp.float32)],
    )(idx, got)


def join_kernel(got_ref, own_ref, first_ref, second_ref, share_ref, out_ref, bias_ref):
    members = own_ref.shape[0]
    total = share_ref[0]
    for ring in range(1, share_ref.shape[0]):
        total = total + share_ref[ring]
    for half in range(2):
        bias_ref[:, half * LANE : (half + 1) * LANE] = total[0, half : half + 1] + total[0, half + 2 : half + 3]
    rows = [total[1].astype(jnp.bfloat16), total[2].astype(jnp.bfloat16)]
    for m in range(members):
        dinv = lax.rsqrt(got_ref[m, 1].astype(jnp.float32)[:, LANE // 2 : LANE // 2 + 1])
        grad = own_ref[m] + first_ref[m].astype(jnp.float32) + second_ref[m].astype(jnp.float32)
        out_ref[m, 0] = (grad * dinv).astype(jnp.bfloat16)
        out_ref[m, 1] = rows[0]
        out_ref[m, 2] = rows[1]


def join(got, own, first, second, share):
    members = own.shape[0]
    return call(
        join_kernel,
        4,
        (
            jax.ShapeDtypeStruct((members, 3, SUB, LANE), jnp.bfloat16),
            jax.ShapeDtypeStruct((1, 2 * LANE), jnp.float32),
        ),
        [vmem()] * 5,
        (vmem(), vmem()),
    )(got, own, first, second, share)


def swap(x, axis):
    return lax.all_to_all(x, axis, 0, 0, tiled=True)


def per_device(features, weight, bias, cotangent, degree, tile_cols, edge_tile, edge_row, edge_col):
    rows, width = features.shape
    members = lax.axis_size("grp")
    rings = lax.axis_size("rep")
    listed = tile_cols.shape[1]
    per_part = listed // 3

    payload, dinv = cut(features, degree[None, :], tile_cols)
    got = swap(payload, "grp")
    own = got[:, 0]
    first = with_partner(own, "rep")
    second = with_other(own, "rep")

    names = got[:, 1, 0, :listed].astype(jnp.int32)
    part = lax.broadcasted_iota(jnp.int32, names.shape, 1) // per_part
    even = lax.axis_index("rep") % 2 == 0
    late = jnp.where(even, part == 0, part == 2)
    idx = (names % members + jnp.where(late, members, 0)).reshape(-1)

    tile = edge_tile[0]
    col = edge_col[0]
    key = (col // SUB) * (listed * SUB) + tile * SUB + col % SUB
    slab = build_slab(edge_row[0], key, rows, listed * rows)

    window = swap(select(idx, first, own, second, per_part), "grp")
    hidden, partial = layer(
        slab, window.reshape(2, listed * rows, LANE), weight, dinv, bias[None, :], cotangent, listed
    )
    mine = swap(partial.reshape(members, listed + 3, SUB, LANE), "grp")

    share = mine[:, listed:].astype(jnp.float32).sum(axis=0)
    share = swap(jnp.broadcast_to(share[None], (rings, 3, SUB, LANE)), "rep")
    to_first, to_second = collect(idx, (0, 2), mine, per_part, jnp.bfloat16)
    from_first = with_partner(to_first, "rep")
    from_second = with_other(to_second, "rep")
    (own_sum,) = collect(idx, (1,), mine, per_part, jnp.float32)

    final, grad_bias = join(got, own_sum, from_first, from_second, share)
    final = swap(final, "grp")
    grad_scaled = final[:, 0].reshape(2, rows, LANE).transpose(1, 0, 2).reshape(rows, width)
    grad_features = lax.dot_general(
        grad_scaled, weight, (((1,), (1,)), ((), ())), preferred_element_type=jnp.float32
    ).astype(jnp.bfloat16)
    grad_weight = final[:, 1:].transpose(0, 2, 1, 3).reshape(width, width).astype(jnp.float32)
    return (hidden, grad_features, grad_weight, grad_bias[0])


def solution(mesh):
    return jax.shard_map(
        per_device,
        mesh=mesh,
        in_specs=(
            P(("rep", "grp"), None),
            P(),
            P(),
            P(("rep", "grp"), None),
            P(("rep", "grp")),
            P(("rep", "grp"), None),
            P(("rep", "grp"), None),
            P(("rep", "grp"), None),
            P(("rep", "grp"), None),
        ),
        out_specs=(P(("rep", "grp"), None), P(("rep", "grp"), None), P(), P()),
        check_vma=False,
    )
```

time: 196 us -> 178 us (0.908)
  waiting for transfers between devices: 100 us -> 51.7 us
  blocking collectives: 18.9 us -> 64.1 us
  other arithmetic: 7.22 us -> 1.1 us
  local copies, waits for them, and re-layouts: 7.02 us -> 1.03 us
    all_to_all x4 -> x3, waiting for transfers between devices: 94.3 us -> 44.8 us  [swap(): return lax.all_to_all(x, axis, 0, 0, tiled=True)]
    all_to_all x1 -> x2, blocking collectives: 18.9 us -> 64.1 us  [swap(): return lax.all_to_all(x, axis, 0, 0, tiled=True)]
    unnamed x19 -> x14, local copies, waits for them, and re-layouts: 3.18 us -> 0.04 us
    all_to_all x4 -> x3, starting transfers between devices: 21.5 us -> 19.5 us  [swap(): return lax.all_to_all(x, axis, 0, 0, tiled=True)]
    pallas_call x3 -> x6, Pallas kernels: 12.1 us -> 11.9 us  [the longest x2 4.11 us: collect(): call(functools.partial(collect_kernel, members, per_part, parts, chains),...]
  transfers between devices with their start and end apart: 8 -> 7, of which waited for: 5 -> 4; matrix products, arithmetic and copies ran while one was open for 3% -> 0% of each run, Pallas kernels for 3% -> 4%
where the time goes in v4:
time: 178 us; the launch traced here: 177 us
  blocking collectives  64.1 us (36%)
  waiting for transfers between devices  51.7 us (29%)
  starting transfers between devices  42.4 us (24%)
  Pallas kernels  15.2 us (9%)
    all_to_all x2, blocking collectives, swap(): return lax.all_to_all(x, axis, 0, 0, tiled=True)  64.1 us
    all_to_all x3, waiting for transfers between devices, swap(): return lax.all_to_all(x, axis, 0, 0, tiled=True)  44.8 us
    all_to_all x3, starting transfers between devices, swap(): return lax.all_to_all(x, axis, 0, 0, tiled=True)  19.5 us
    ppermute x2, starting transfers between devices, with_other(): lax.ppermute(x, axis, [(i, (i + 1 if i % 2 else i - 1) % size) for i in r...  16.3 us
    ppermute x2, starting transfers between devices, with_partner(): lax.ppermute(x, axis, [(i, i ^ 1) for i in range(lax.axis_size(axis))])  6.58 us
    ppermute x2, waiting for transfers between devices, with_partner(): lax.ppermute(x, axis, [(i, i ^ 1) for i in range(lax.axis_size(axis))])  4.41 us
    pallas_call x2, Pallas kernels, collect(): call(functools.partial(collect_kernel, members, per_part, parts, chains),...  4.11 us
  transfers between devices with their start and end apart: 7, of which 4 were waited for; matrix products, arithmetic and copies ran while one was open for 0% of the time, Pallas kernels for 4%

profile of v4, /device:TPU:1, one launch (start us, length us, event | category | flops | bytes accessed | tf_op | source)
XLA Modules:
  0.0 177.3 jit_solution(7739089309215526291)
XLA Ops:
  0.6 1.6 shard_map.120
  2.3 10.4 %all-to-all-start = ((bf16[32,2,8,128]{3,2,1,0:T(8,128)(2,1)}), bf16[32,2,8,128]{3,2,1,0:T(8,128)(2,1)S(1)}, u32[]{:S(2)}, u32[]{:S(2)}) async-start(bf16[32,2,8,128]{3,2,1,0:T(8,128)(2,1)} %get-tuple-element.12), calls=%async_computation | async-start | bytes 262144 | tf_op jit(solution)/shard_map/all_to_all | solution.py:291
  12.8 9.3 %all-to-all-done.got_ref = bf16[32,2,8,128]{3,2,1,0:T(8,128)(2,1)S(1)} async-done(((bf16[32,2,8,128]{3,2,1,0:T(8,128)(2,1)}), bf16[32,2,8,128]{3,2,1,0:T(8,128)(2,1)S(1)}, u32[]{:S(2)}, u32[]{:S(2)}) %all-to-all-start) | async-done | bytes 131104 | tf_op jit(solution)/shard_map/all_to_all | solution.py:291
  22.1 11.9 %collective-permute-start.1 = (bf16[32,8,128]{2,1,0:T(8,128)(2,1)S(1)}, bf16[32,8,128]{2,1,0:T(8,128)(2,1)S(1)}, u32[]{:S(2)}, u32[]{:S(2)}) collective-permute-start(bf16[32,8,128]{2,1,0:T(8,128)(2,1)S(1)} %slice_bitcast_fusion.own_ref), channel_id=1, source_target_pairs={{0,480},{32,64},{64,32},{96,128},{128,96},{160,192},{192,160},{224... | collective-permute-start | bytes 196616 | tf_op jit(solution)/shard_map/ppermute | solution.py:22
  34.0 1.9 %collective-permute-start = (bf16[32,8,128]{2,1,0:T(8,128)(2,1)S(1)}, bf16[32,8,128]{2,1,0:T(8,128)(2,1)S(1)}, u32[]{:S(2)}, u32[]{:S(2)}) collective-permute-start(bf16[32,8,128]{2,1,0:T(8,128)(2,1)S(1)} %slice_bitcast_fusion.own_ref), channel_id=1, source_target_pairs={{0,32},{32,0},{64,96},{96,64},{128,160},{160,128},{192,224},{224,1... | collective-permute-start | bytes 196616 | tf_op jit(solution)/shard_map/ppermute | solution.py:17
  36.1 4.4 %collective-permute-done.first_ref = bf16[32,8,128]{2,1,0:T(8,128)(2,1)S(1)} collective-permute-done((bf16[32,8,128]{2,1,0:T(8,128)(2,1)S(1)}, bf16[32,8,128]{2,1,0:T(8,128)(2,1)S(1)}, u32[]{:S(2)}, u32[]{:S(2)}) %collective-permute-start) | collective-permute-done | bytes 65568 | tf_op jit(solution)/shard_map/ppermute | solution.py:17
  40.5 2.6 %shard_map.121 = bf16[32,24,8,128]{3,2,1,0:T(8,128)(2,1)} custom-call(s32[768]{0:T(1024)S(1)} %fusion.5.idx_ref, bf16[32,8,128]{2,1,0:T(8,128)(2,1)S(1)} %collective-permute-done.first_ref, bf16[32,8,128]{2,1,0:T(8,128)(2,1)S(1)} %slice_bitcast_fusion.own_ref, bf16[32,8,128]{2,1,0:T(8,128)(2,1)S(1)} %collective-permute-done.1.second_ref), custom_call_target="tpu_custom_call" | custom-call | tf_op jit(solution)/shard_map/pallas_call | solution.py:149
  43.2 5.6 %all-to-all-start.1 = ((bf16[32,24,8,128]{3,2,1,0:T(8,128)(2,1)}), bf16[32,24,8,128]{3,2,1,0:T(8,128)(2,1)S(1)}, u32[]{:S(2)}, u32[]{:S(2)}) async-start(bf16[32,24,8,128]{3,2,1,0:T(8,128)(2,1)} %shard_map.121), calls=%async_computation.1 | async-start | bytes 3145728 | tf_op jit(solution)/shard_map/all_to_all | solution.py:291
  48.9 0.2 and_select_fusion
  49.2 3.3 %count.1.slab_ref = bf16[128,3072]{1,0:T(8,128)(2,1)S(1)} custom-call(s32[1,3840]{1,0:T(1,128)S(1)} %multiply_add_fusion.xk_ref, s32[1,3840]{1,0:T(1,128)S(1)} %get-tuple-element.20.yk_ref), custom_call_target="tpu_custom_call" | custom-call | tf_op jit(solution)/shard_map/count/pallas_call | solution.py:109
  52.5 35.5 %all-to-all-done.1 = bf16[32,24,8,128]{3,2,1,0:T(8,128)(2,1)S(1)} async-done(((bf16[32,24,8,128]{3,2,1,0:T(8,128)(2,1)}), bf16[32,24,8,128]{3,2,1,0:T(8,128)(2,1)S(1)}, u32[]{:S(2)}, u32[]{:S(2)}) %all-to-all-start.1) | async-done | bytes 1572896 | tf_op jit(solution)/shard_map/all_to_all | solution.py:291
  88.0 3.0 %shard_map.122 = (bf16[128,256]{1,0:T(8,128)(2,1)}, bf16[2,16,27,8,128]{4,3,2,1,0:T(8,128)(2,1)S(1)}) custom-call(bf16[128,3072]{1,0:T(8,128)(2,1)S(1)} %count.1.slab_ref, bf16[2,3072,128]{2,1,0:T(8,128)(2,1)S(1)} %bitcast.17, bf16[256,256]{1,0:T(8,128)(2,1)S(1)} %copy-done, f32[128,1]{1,0:T(8,128)S(1)} %copy-done.2, f32[1,256]{1,0:T(1,128)S(1)} %bitcast.19, ...), custom_call_target="tpu_custom_call" | custom-call | tf_op jit(solution)/shard_map/pallas_call | solution.py:213
  91.0 48.1 %all_to_all.25.got_ref = bf16[32,27,8,128]{3,2,1,0:T(8,128)(2,1)S(1)} all-to-all(bf16[32,27,8,128]{3,2,1,0:T(8,128)(2,1)S(1)} %bitcast.18), channel_id=1, replica_groups=mesh['rep'=16,'grp'=32] {'grp'}, dimensions={0} | all-to-all | bytes 3538944 | tf_op jit(solution)/shard_map/all_to_all | solution.py:291
  139.2 0.7 broadcast_in_dim.18
  139.8 3.5 %all-to-all-start.3 = ((f32[16,3,8,128]{3,2,1,0:T(8,128)}), f32[16,3,8,128]{3,2,1,0:T(8,128)S(1)}, u32[]{:S(2)}, u32[]{:S(2)}) async-start(f32[16,3,8,128]{3,2,1,0:T(8,128)} %broadcast_in_dim.18), calls=%async_computation.3 | async-start | bytes 393216 | tf_op jit(solution)/shard_map/all_to_all | solution.py:291
  143.4 2.4 %shard_map.124 = (bf16[32,8,128]{2,1,0:T(8,128)(2,1)S(1)}, bf16[32,8,128]{2,1,0:T(8,128)(2,1)S(1)}) custom-call(s32[768]{0:T(1024)S(1)} %fusion.5.idx_ref, bf16[32,27,8,128]{3,2,1,0:T(8,128)(2,1)S(1)} %all_to_all.25.got_ref), custom_call_target="tpu_custom_call" | custom-call | tf_op jit(solution)/shard_map/pallas_call | solution.py:250
  145.7 4.7 %collective-permute-start.2 = (bf16[32,8,128]{2,1,0:T(8,128)(2,1)S(1)}, bf16[32,8,128]{2,1,0:T(8,128)(2,1)S(1)}, u32[]{:S(2)}, u32[]{:S(2)}) collective-permute-start(bf16[32,8,128]{2,1,0:T(8,128)(2,1)S(1)} %get-tuple-element.16), channel_id=1, source_target_pairs={{0,32},{32,0},{64,96},{96,64},{128,160},{160,128},{192,224},{224,1... | collective-permute-start | bytes 196616 | tf_op jit(solution)/shard_map/ppermute | solution.py:17
  150.4 4.4 %collective-permute-start.3 = (bf16[32,8,128]{2,1,0:T(8,128)(2,1)S(1)}, bf16[32,8,128]{2,1,0:T(8,128)(2,1)S(1)}, u32[]{:S(2)}, u32[]{:S(2)}) collective-permute-start(bf16[32,8,128]{2,1,0:T(8,128)(2,1)S(1)} %get-tuple-element.17), channel_id=1, source_target_pairs={{0,480},{32,64},{64,32},{96,128},{128,96},{160,192},{192,160},{224... | collective-permute-start | bytes 196616 | tf_op jit(solution)/shard_map/ppermute | solution.py:22
  154.8 1.7 shard_map.123.own_ref
  156.6 2.5 %collective-permute-done.3.second_ref = bf16[32,8,128]{2,1,0:T(8,128)(2,1)S(1)} collective-permute-done((bf16[32,8,128]{2,1,0:T(8,128)(2,1)S(1)}, bf16[32,8,128]{2,1,0:T(8,128)(2,1)S(1)}, u32[]{:S(2)}, u32[]{:S(2)}) %collective-permute-start.3) | collective-permute-done | bytes 65568 | tf_op jit(solution)/shard_map/ppermute | solution.py:22
  159.0 0.6 shard_map.125
  159.6 15.9 %all_to_all.26 = bf16[32,3,8,128]{3,2,1,0:T(8,128)(2,1)S(1)} all-to-all(bf16[32,3,8,128]{3,2,1,0:T(8,128)(2,1)S(1)} %get-tuple-element.18), channel_id=1, replica_groups=mesh['rep'=16,'grp'=32] {'grp'}, dimensions={0} | all-to-all | bytes 393216 | tf_op jit(solution)/shard_map/all_to_all | solution.py:291
  175.7 0.8 convolution_convert_fusion
  176.5 0.7 convert_bitcast_fusion
  (29 shorter events, 0.6 us)
Async XLA Ops:
  2.3 19.8 %all-to-all-start = ((bf16[32,2,8,128]{3,2,1,0:T(8,128)(2,1)}), bf16[32,2,8,128]{3,2,1,0:T(8,128)(2,1)S(1)}, u32[]{:S(2)}, u32[]{:S(2)}) async-start(bf16[32,2,8,128]{3,2,1,0:T(8,128)(2,1)} %get-tuple-element.12), calls=%async_computation | async-start | bytes 262144 | tf_op jit(solution)/shard_map/all_to_all | solution.py:291
  22.1 14.0 %collective-permute-start.1 = (bf16[32,8,128]{2,1,0:T(8,128)(2,1)S(1)}, bf16[32,8,128]{2,1,0:T(8,128)(2,1)S(1)}, u32[]{:S(2)}, u32[]{:S(2)}) collective-permute-start(bf16[32,8,128]{2,1,0:T(8,128)(2,1)S(1)} %slice_bitcast_fusion.own_ref), channel_id=1, source_target_pairs={{0,480},{32,64},{64,32},{96,128},{128,96},{160,192},{192,160},{224... | collective-permute-start | bytes 196616 | tf_op jit(solution)/shard_map/ppermute | solution.py:22
  34.0 6.5 %collective-permute-start = (bf16[32,8,128]{2,1,0:T(8,128)(2,1)S(1)}, bf16[32,8,128]{2,1,0:T(8,128)(2,1)S(1)}, u32[]{:S(2)}, u32[]{:S(2)}) collective-permute-start(bf16[32,8,128]{2,1,0:T(8,128)(2,1)S(1)} %slice_bitcast_fusion.own_ref), channel_id=1, source_target_pairs={{0,32},{32,0},{64,96},{96,64},{128,160},{160,128},{192,224},{224,1... | collective-permute-start | bytes 196616 | tf_op jit(solution)/shard_map/ppermute | solution.py:17
  43.1 5.7 %copy-start.5 = (s32[1,3840]{1,0:T(1,128)S(1)}, s32[1,3840]{1,0:T(1,128)}, u32[]{:S(2)}) copy-start(s32[1,3840]{1,0:T(1,128)} %param.15) | copy-start | bytes 46084
  43.1 5.7 %copy-start.6 = (s32[1,3840]{1,0:T(1,128)S(1)}, s32[1,3840]{1,0:T(1,128)}, u32[]{:S(2)}) copy-start(s32[1,3840]{1,0:T(1,128)} %param.17) | copy-start | bytes 46084
  43.1 5.9 %copy-start.4 = (s32[1,3840]{1,0:T(1,128)S(1)}, s32[1,3840]{1,0:T(1,128)}, u32[]{:S(2)}) copy-start(s32[1,3840]{1,0:T(1,128)} %param.16) | copy-start | bytes 46084
  43.2 44.8 %copy-start = (bf16[256,256]{1,0:T(8,128)(2,1)S(1)}, bf16[256,256]{1,0:T(8,128)(2,1)}, u32[]{:S(2)}) copy-start(bf16[256,256]{1,0:T(8,128)(2,1)} %weight_ref.1) | copy-start | bytes 393220
  43.2 44.8 %copy-start.1 = (bf16[128,256]{1,0:T(8,128)(2,1)S(1)}, bf16[128,256]{1,0:T(8,128)(2,1)}, u32[]{:S(2)}) copy-start(bf16[128,256]{1,0:T(8,128)(2,1)} %cot_ref.1) | copy-start | bytes 196612
  43.2 44.8 %copy-start.2 = (f32[128,1]{1,0:T(8,128)S(1)}, f32[128,1]{1,0:T(8,128)}, u32[]{:S(2)}) copy-start(f32[128,1]{1,0:T(8,128)} %get-tuple-element.13.dinv_ref) | copy-start | bytes 1540
  43.2 44.8 %copy-start.3 = (f32[256]{0:T(256)S(1)}, f32[256]{0:T(256)}, u32[]{:S(2)}) copy-start(f32[256]{0:T(256)} %param.11) | copy-start | bytes 3076
  43.2 44.8 %all-to-all-start.1 = ((bf16[32,24,8,128]{3,2,1,0:T(8,128)(2,1)}), bf16[32,24,8,128]{3,2,1,0:T(8,128)(2,1)S(1)}, u32[]{:S(2)}, u32[]{:S(2)}) async-start(bf16[32,24,8,128]{3,2,1,0:T(8,128)(2,1)} %shard_map.121), calls=%async_computation.1 | async-start | bytes 3145728 | tf_op jit(solution)/shard_map/all_to_all | solution.py:291
  139.8 19.2 %all-to-all-start.3 = ((f32[16,3,8,128]{3,2,1,0:T(8,128)}), f32[16,3,8,128]{3,2,1,0:T(8,128)S(1)}, u32[]{:S(2)}, u32[]{:S(2)}) async-start(f32[16,3,8,128]{3,2,1,0:T(8,128)} %broadcast_in_dim.18), calls=%async_computation.3 | async-start | bytes 393216 | tf_op jit(solution)/shard_map/all_to_all | solution.py:291
  145.7 10.8 %collective-permute-start.2 = (bf16[32,8,128]{2,1,0:T(8,128)(2,1)S(1)}, bf16[32,8,128]{2,1,0:T(8,128)(2,1)S(1)}, u32[]{:S(2)}, u32[]{:S(2)}) collective-permute-start(bf16[32,8,128]{2,1,0:T(8,128)(2,1)S(1)} %get-tuple-element.16), channel_id=1, source_target_pairs={{0,32},{32,0},{64,96},{96,64},{128,160},{160,128},{192,224},{224,1... | collective-permute-start | bytes 196616 | tf_op jit(solution)/shard_map/ppermute | solution.py:17
  150.4 8.6 %collective-permute-start.3 = (bf16[32,8,128]{2,1,0:T(8,128)(2,1)S(1)}, bf16[32,8,128]{2,1,0:T(8,128)(2,1)S(1)}, u32[]{:S(2)}, u32[]{:S(2)}) collective-permute-start(bf16[32,8,128]{2,1,0:T(8,128)(2,1)S(1)} %get-tuple-element.17), channel_id=1, source_target_pairs={{0,480},{32,64},{64,32},{96,128},{128,96},{160,192},{192,160},{224... | collective-permute-start | bytes 196616 | tf_op jit(solution)/shard_map/ppermute | solution.py:22

commit v5 on v4

--- a/solution.py
+++ b/solution.py
@@ -28,10 +28,6 @@
 
 def smem():
     return pl.BlockSpec(memory_space=pltpu.SMEM)
-
-
-def hbm():
-    return pl.BlockSpec(memory_space=pltpu.HBM)
 
 
 def call(kernel, mib, out_shape, in_specs, out_specs, scratch=()):
@@ -117,50 +113,36 @@
     )(xk, yk)
 
 
-def select_kernel(members, per_part, idx_ref, first_ref, own_ref, second_ref, out_ref, near_ref, made_ref, sems):
+def select_kernel(members, per_part, idx_ref, first_ref, own_ref, second_ref, out_ref, near_ref):
     listed = 3 * per_part
     near_ref[pl.ds(0, members)] = first_ref[...]
     near_ref[pl.ds(members, members)] = second_ref[...]
-    steps = sems.shape[0]
-    span = members // steps
 
     def one(d, carry):
         for t in range(listed):
             at = idx_ref[d * listed + t]
             if t // per_part == 1:
-                made_ref[d, t] = own_ref[jnp.bitwise_and(at, members - 1)]
+                out_ref[d, t] = own_ref[jnp.bitwise_and(at, members - 1)]
             else:
-                made_ref[d, t] = near_ref[jnp.bitwise_and(at, 2 * members - 1)]
+                out_ref[d, t] = near_ref[jnp.bitwise_and(at, 2 * members - 1)]
         return carry
 
-    copies = []
-    for step in range(steps):
-        lax.fori_loop(step * span, (step + 1) * span, one, 0)
-        part = pl.ds(step * span, span)
-        copies.append(pltpu.make_async_copy(made_ref.at[part], out_ref.at[part], sems.at[step]))
-        copies[-1].start()
-    for copy in copies:
-        copy.wait()
+    lax.fori_loop(0, members, one, 0)
 
 
 def select(idx, first, own, second, per_part):
     members = own.shape[0]
-    shape = (members, 3 * per_part, SUB, LANE)
     return call(
         functools.partial(select_kernel, members, per_part),
         6,
-        jax.ShapeDtypeStruct(shape, own.dtype),
+        jax.ShapeDtypeStruct((members, 3 * per_part, SUB, LANE), own.dtype),
         [smem()] + [vmem()] * 3,
-        hbm(),
-        [
-            pltpu.VMEM((2 * members, SUB, LANE), own.dtype),
-            pltpu.VMEM(shape, own.dtype),
-            pltpu.SemaphoreType.DMA((4,)),
-        ],
+        vmem(),
+        [pltpu.VMEM((2 * members, SUB, LANE), own.dtype)],
     )(idx, first, own, second)
 
 
-def layer_kernel(listed, slab_ref, x_ref, weight_ref, dinv_ref, bias_ref, cot_ref, hid_ref, out_ref, part_ref, sems):
+def layer_kernel(listed, slab_ref, x_ref, weight_ref, dinv_ref, bias_ref, cot_ref, hid_ref, part_ref):
     dinv = dinv_ref[...]
     groups = part_ref.shape[1]
     span = listed * SUB
@@ -189,7 +171,6 @@
             lanes = slice(half * LANE, (half + 1) * LANE)
             extra = jnp.where(at == 2 * index + half, value[:, lanes], extra)
     extra = extra.astype(jnp.bfloat16)
-    copies = []
     for half in range(2):
         lanes = slice(half * LANE, (half + 1) * LANE)
         partial = lax.dot_general(slab_ref[...], back[:, lanes], contract, preferred_element_type=jnp.float32)
@@ -201,10 +182,6 @@
             for other in range(2):
                 block = grad[top : top + SUB, other * LANE : (other + 1) * LANE]
                 part_ref[half, a, listed + 1 + other] = block.astype(jnp.bfloat16)
-        copies.append(pltpu.make_async_copy(part_ref.at[half], out_ref.at[half], sems.at[half]))
-        copies[-1].start()
-    for copy in copies:
-        copy.wait()
 
 
 def layer(slab, x, weight, dinv, bias, cotangent, listed):
@@ -215,8 +192,7 @@
         16,
         (jax.ShapeDtypeStruct((rows, width), jnp.bfloat16), jax.ShapeDtypeStruct(shape, jnp.bfloat16)),
         [vmem()] * 6,
-        (vmem(), hbm()),
-        [pltpu.VMEM(shape, jnp.bfloat16), pltpu.SemaphoreType.DMA((2,))],
+        (vmem(), vmem()),
     )(slab, x, weight, dinv, bias, cotangent)
 
 
@@ -287,12 +263,40 @@
     )(got, own, first, second, share)
 
 
+def finish_kernel(final_ref, weight_ref, features_ref, weight_grad_ref):
+    members = final_ref.shape[0]
+    groups = members // 2
+    sides = [final_ref[pl.ds(half * groups, groups), 0].astype(jnp.float32).reshape(-1, LANE) for half in range(2)]
+    grad = jnp.concatenate(sides, axis=1).astype(jnp.bfloat16)
+    features_ref[...] = lax.dot_general(
+        grad, weight_ref[...], (((1,), (1,)), ((), ())), preferred_element_type=jnp.float32
+    ).astype(features_ref.dtype)
+    for half in range(2):
+        rows = final_ref[:, 1 + half].astype(jnp.float32).reshape(-1, LANE)
+        weight_grad_ref[:, half * LANE : (half + 1) * LANE] = rows
+
+
+def finish(final, weight):
+    width = weight.shape[0]
+    rows = final.shape[0] // 2 * SUB
+    return call(
+        finish_kernel,
+        6,
+        (
+            jax.ShapeDtypeStruct((rows, width), jnp.bfloat16),
+            jax.ShapeDtypeStruct((width, width), jnp.float32),
+        ),
+        [vmem(), vmem()],
+        (vmem(), vmem()),
+    )(final, weight)
+
+
 def swap(x, axis):
     return lax.all_to_all(x, axis, 0, 0, tiled=True)
 
 
 def per_device(features, weight, bias, cotangent, degree, tile_cols, edge_tile, edge_row, edge_col):
-    rows, width = features.shape
+    rows, _ = features.shape
     members = lax.axis_size("grp")
     rings = lax.axis_size("rep")
     listed = tile_cols.shape[1]
@@ -330,11 +334,7 @@
 
     final, grad_bias = join(got, own_sum, from_first, from_second, share)
     final = swap(final, "grp")
-    grad_scaled = final[:, 0].reshape(2, rows, LANE).transpose(1, 0, 2).reshape(rows, width)
-    grad_features = lax.dot_general(
-        grad_scaled, weight, (((1,), (1,)), ((), ())), preferred_element_type=jnp.float32
-    ).astype(jnp.bfloat16)
-    grad_weight = final[:, 1:].transpose(0, 2, 1, 3).reshape(width, width).astype(jnp.float32)
+    grad_features, grad_weight = finish(final, weight)
     return (hidden, grad_features, grad_weight, grad_bias[0])
 
 

time: 178 us -> 176 us (0.989)
  no operation moved by 1% of the time
where the time goes in v5:
time: 176 us; the launch traced here: 175 us
  blocking collectives  64.1 us (36%)
  waiting for transfers between devices  51.7 us (29%)
  starting transfers between devices  42.4 us (24%)
  Pallas kernels  14.9 us (8%)
    all_to_all x2, blocking collectives, swap(): return lax.all_to_all(x, axis, 0, 0, tiled=True)  64.1 us
    all_to_all x3, waiting for transfers between devices, swap(): return lax.all_to_all(x, axis, 0, 0, tiled=True)  44.8 us
    all_to_all x3, starting transfers between devices, swap(): return lax.all_to_all(x, axis, 0, 0, tiled=True)  19.5 us
    ppermute x2, starting transfers between devices, with_other(): lax.ppermute(x, axis, [(i, (i + 1 if i % 2 else i - 1) % size) for i in r...  16.3 us
    ppermute x2, starting transfers between devices, with_partner(): lax.ppermute(x, axis, [(i, i ^ 1) for i in range(lax.axis_size(axis))])  6.58 us
    ppermute x2, waiting for transfers between devices, with_partner(): lax.ppermute(x, axis, [(i, i ^ 1) for i in range(lax.axis_size(axis))])  4.41 us
    pallas_call x2, Pallas kernels, collect(): call(functools.partial(collect_kernel, members, per_part, parts, chains),...  4.11 us
  transfers between devices with their start and end apart: 7, of which 4 were waited for; matrix products, arithmetic and copies ran while one was open for 0% of the time, Pallas kernels for 4%

profile of v5, /device:TPU:1, one launch (start us, length us, event | category | flops | bytes accessed | tf_op | source)
XLA Modules:
  0.0 175.3 jit_solution(12185330799173882113)
XLA Ops:
  0.6 1.6 shard_map.120
  2.3 10.4 %all-to-all-start = ((bf16[32,2,8,128]{3,2,1,0:T(8,128)(2,1)}), bf16[32,2,8,128]{3,2,1,0:T(8,128)(2,1)S(1)}, u32[]{:S(2)}, u32[]{:S(2)}) async-start(bf16[32,2,8,128]{3,2,1,0:T(8,128)(2,1)} %get-tuple-element.14), calls=%async_computation | async-start | bytes 262144 | tf_op jit(solution)/shard_map/all_to_all | solution.py:295
  12.8 9.3 %all-to-all-done.got_ref = bf16[32,2,8,128]{3,2,1,0:T(8,128)(2,1)S(1)} async-done(((bf16[32,2,8,128]{3,2,1,0:T(8,128)(2,1)}), bf16[32,2,8,128]{3,2,1,0:T(8,128)(2,1)S(1)}, u32[]{:S(2)}, u32[]{:S(2)}) %all-to-all-start) | async-done | bytes 131104 | tf_op jit(solution)/shard_map/all_to_all | solution.py:295
  22.1 11.9 %collective-permute-start.1 = (bf16[32,8,128]{2,1,0:T(8,128)(2,1)S(1)}, bf16[32,8,128]{2,1,0:T(8,128)(2,1)S(1)}, u32[]{:S(2)}, u32[]{:S(2)}) collective-permute-start(bf16[32,8,128]{2,1,0:T(8,128)(2,1)S(1)} %slice_bitcast_fusion.own_ref), channel_id=1, source_target_pairs={{0,480},{32,64},{64,32},{96,128},{128,96},{160,192},{192,160},{224... | collective-permute-start | bytes 196616 | tf_op jit(solution)/shard_map/ppermute | solution.py:22
  34.0 1.9 %collective-permute-start = (bf16[32,8,128]{2,1,0:T(8,128)(2,1)S(1)}, bf16[32,8,128]{2,1,0:T(8,128)(2,1)S(1)}, u32[]{:S(2)}, u32[]{:S(2)}) collective-permute-start(bf16[32,8,128]{2,1,0:T(8,128)(2,1)S(1)} %slice_bitcast_fusion.own_ref), channel_id=1, source_target_pairs={{0,32},{32,0},{64,96},{96,64},{128,160},{160,128},{192,224},{224,1... | collective-permute-start | bytes 196616 | tf_op jit(solution)/shard_map/ppermute | solution.py:17
  36.1 4.4 %collective-permute-done.first_ref = bf16[32,8,128]{2,1,0:T(8,128)(2,1)S(1)} collective-permute-done((bf16[32,8,128]{2,1,0:T(8,128)(2,1)S(1)}, bf16[32,8,128]{2,1,0:T(8,128)(2,1)S(1)}, u32[]{:S(2)}, u32[]{:S(2)}) %collective-permute-start) | collective-permute-done | bytes 65568 | tf_op jit(solution)/shard_map/ppermute | solution.py:17
  40.5 3.0 %shard_map.121 = bf16[32,24,8,128]{3,2,1,0:T(8,128)(2,1)} custom-call(s32[768]{0:T(1024)S(1)} %fusion.5.idx_ref, bf16[32,8,128]{2,1,0:T(8,128)(2,1)S(1)} %collective-permute-done.first_ref, bf16[32,8,128]{2,1,0:T(8,128)(2,1)S(1)} %slice_bitcast_fusion.own_ref, bf16[32,8,128]{2,1,0:T(8,128)(2,1)S(1)} %collective-permute-done.1.second_ref), custom_call_target="tpu_custom_call" | custom-call | tf_op jit(solution)/shard_map/pallas_call | solution.py:135
  43.6 5.6 %all-to-all-start.1 = ((bf16[32,24,8,128]{3,2,1,0:T(8,128)(2,1)}), bf16[32,24,8,128]{3,2,1,0:T(8,128)(2,1)S(1)}, u32[]{:S(2)}, u32[]{:S(2)}) async-start(bf16[32,24,8,128]{3,2,1,0:T(8,128)(2,1)} %shard_map.121), calls=%async_computation.1 | async-start | bytes 3145728 | tf_op jit(solution)/shard_map/all_to_all | solution.py:295
  49.2 0.2 and_select_fusion
  49.4 0.1 multiply_add_fusion.xk_ref
  49.5 3.3 %count.1.slab_ref = bf16[128,3072]{1,0:T(8,128)(2,1)S(1)} custom-call(s32[1,3840]{1,0:T(1,128)S(1)} %multiply_add_fusion.xk_ref, s32[1,3840]{1,0:T(1,128)S(1)} %get-tuple-element.24.yk_ref), custom_call_target="tpu_custom_call" | custom-call | tf_op jit(solution)/shard_map/count/pallas_call | solution.py:105
  52.8 35.5 %all-to-all-done.1 = bf16[32,24,8,128]{3,2,1,0:T(8,128)(2,1)S(1)} async-done(((bf16[32,24,8,128]{3,2,1,0:T(8,128)(2,1)}), bf16[32,24,8,128]{3,2,1,0:T(8,128)(2,1)S(1)}, u32[]{:S(2)}, u32[]{:S(2)}) %all-to-all-start.1) | async-done | bytes 1572896 | tf_op jit(solution)/shard_map/all_to_all | solution.py:295
  88.3 1.5 shard_map.122
  89.8 48.1 %all_to_all.25.got_ref = bf16[32,27,8,128]{3,2,1,0:T(8,128)(2,1)S(1)} all-to-all(bf16[32,27,8,128]{3,2,1,0:T(8,128)(2,1)S(1)} %bitcast.8), channel_id=1, replica_groups=mesh['rep'=16,'grp'=32] {'grp'}, dimensions={0} | all-to-all | bytes 3538944 | tf_op jit(solution)/shard_map/all_to_all | solution.py:295
  138.0 0.7 broadcast_in_dim.18
  138.7 3.5 %all-to-all-start.3 = ((f32[16,3,8,128]{3,2,1,0:T(8,128)}), f32[16,3,8,128]{3,2,1,0:T(8,128)S(1)}, u32[]{:S(2)}, u32[]{:S(2)}) async-start(f32[16,3,8,128]{3,2,1,0:T(8,128)} %broadcast_in_dim.18), calls=%async_computation.3 | async-start | bytes 393216 | tf_op jit(solution)/shard_map/all_to_all | solution.py:295
  142.2 2.4 %shard_map.124 = (bf16[32,8,128]{2,1,0:T(8,128)(2,1)S(1)}, bf16[32,8,128]{2,1,0:T(8,128)(2,1)S(1)}) custom-call(s32[768]{0:T(1024)S(1)} %fusion.5.idx_ref, bf16[32,27,8,128]{3,2,1,0:T(8,128)(2,1)S(1)} %all_to_all.25.got_ref), custom_call_target="tpu_custom_call" | custom-call | tf_op jit(solution)/shard_map/pallas_call | solution.py:226
  144.6 4.7 %collective-permute-start.2 = (bf16[32,8,128]{2,1,0:T(8,128)(2,1)S(1)}, bf16[32,8,128]{2,1,0:T(8,128)(2,1)S(1)}, u32[]{:S(2)}, u32[]{:S(2)}) collective-permute-start(bf16[32,8,128]{2,1,0:T(8,128)(2,1)S(1)} %get-tuple-element.18), channel_id=1, source_target_pairs={{0,32},{32,0},{64,96},{96,64},{128,160},{160,128},{192,224},{224,1... | collective-permute-start | bytes 196616 | tf_op jit(solution)/shard_map/ppermute | solution.py:17
  149.3 4.4 %collective-permute-start.3 = (bf16[32,8,128]{2,1,0:T(8,128)(2,1)S(1)}, bf16[32,8,128]{2,1,0:T(8,128)(2,1)S(1)}, u32[]{:S(2)}, u32[]{:S(2)}) collective-permute-start(bf16[32,8,128]{2,1,0:T(8,128)(2,1)S(1)} %get-tuple-element.19), channel_id=1, source_target_pairs={{0,480},{32,64},{64,32},{96,128},{128,96},{160,192},{192,160},{224... | collective-permute-start | bytes 196616 | tf_op jit(solution)/shard_map/ppermute | solution.py:22
  153.7 1.7 shard_map.123.own_ref
  155.4 2.5 %collective-permute-done.3.second_ref = bf16[32,8,128]{2,1,0:T(8,128)(2,1)S(1)} collective-permute-done((bf16[32,8,128]{2,1,0:T(8,128)(2,1)S(1)}, bf16[32,8,128]{2,1,0:T(8,128)(2,1)S(1)}, u32[]{:S(2)}, u32[]{:S(2)}) %collective-permute-start.3) | collective-permute-done | bytes 65568 | tf_op jit(solution)/shard_map/ppermute | solution.py:22
  157.9 0.6 shard_map.125
  158.5 15.9 %all_to_all.26.final_ref = bf16[32,3,8,128]{3,2,1,0:T(8,128)(2,1)S(1)} all-to-all(bf16[32,3,8,128]{3,2,1,0:T(8,128)(2,1)S(1)} %get-tuple-element.20), channel_id=1, replica_groups=mesh['rep'=16,'grp'=32] {'grp'}, dimensions={0} | all-to-all | bytes 393216 | tf_op jit(solution)/shard_map/all_to_all | solution.py:295
  174.4 0.8 shard_map.126
  (26 shorter events, 0.3 us)
Async XLA Ops:
  2.3 19.8 %all-to-all-start = ((bf16[32,2,8,128]{3,2,1,0:T(8,128)(2,1)}), bf16[32,2,8,128]{3,2,1,0:T(8,128)(2,1)S(1)}, u32[]{:S(2)}, u32[]{:S(2)}) async-start(bf16[32,2,8,128]{3,2,1,0:T(8,128)(2,1)} %get-tuple-element.14), calls=%async_computation | async-start | bytes 262144 | tf_op jit(solution)/shard_map/all_to_all | solution.py:295
  22.1 14.0 %collective-permute-start.1 = (bf16[32,8,128]{2,1,0:T(8,128)(2,1)S(1)}, bf16[32,8,128]{2,1,0:T(8,128)(2,1)S(1)}, u32[]{:S(2)}, u32[]{:S(2)}) collective-permute-start(bf16[32,8,128]{2,1,0:T(8,128)(2,1)S(1)} %slice_bitcast_fusion.own_ref), channel_id=1, source_target_pairs={{0,480},{32,64},{64,32},{96,128},{128,96},{160,192},{192,160},{224... | collective-permute-start | bytes 196616 | tf_op jit(solution)/shard_map/ppermute | solution.py:22
  34.0 6.5 %collective-permute-start = (bf16[32,8,128]{2,1,0:T(8,128)(2,1)S(1)}, bf16[32,8,128]{2,1,0:T(8,128)(2,1)S(1)}, u32[]{:S(2)}, u32[]{:S(2)}) collective-permute-start(bf16[32,8,128]{2,1,0:T(8,128)(2,1)S(1)} %slice_bitcast_fusion.own_ref), channel_id=1, source_target_pairs={{0,32},{32,0},{64,96},{96,64},{128,160},{160,128},{192,224},{224,1... | collective-permute-start | bytes 196616 | tf_op jit(solution)/shard_map/ppermute | solution.py:17
  43.5 5.7 %copy-start.5 = (s32[1,3840]{1,0:T(1,128)S(1)}, s32[1,3840]{1,0:T(1,128)}, u32[]{:S(2)}) copy-start(s32[1,3840]{1,0:T(1,128)} %param.15) | copy-start | bytes 46084
  43.5 5.7 %copy-start.6 = (s32[1,3840]{1,0:T(1,128)S(1)}, s32[1,3840]{1,0:T(1,128)}, u32[]{:S(2)}) copy-start(s32[1,3840]{1,0:T(1,128)} %param.17) | copy-start | bytes 46084
  43.5 5.9 %copy-start.4 = (s32[1,3840]{1,0:T(1,128)S(1)}, s32[1,3840]{1,0:T(1,128)}, u32[]{:S(2)}) copy-start(s32[1,3840]{1,0:T(1,128)} %param.16) | copy-start | bytes 46084
  43.5 44.8 %copy-start = (bf16[256,256]{1,0:T(8,128)(2,1)S(1)}, bf16[256,256]{1,0:T(8,128)(2,1)}, u32[]{:S(2)}) copy-start(bf16[256,256]{1,0:T(8,128)(2,1)} %weight_ref.3) | copy-start | bytes 393220
  43.5 44.8 %copy-start.1 = (bf16[128,256]{1,0:T(8,128)(2,1)S(1)}, bf16[128,256]{1,0:T(8,128)(2,1)}, u32[]{:S(2)}) copy-start(bf16[128,256]{1,0:T(8,128)(2,1)} %cot_ref.1) | copy-start | bytes 196612
  43.5 44.8 %copy-start.2 = (f32[128,1]{1,0:T(8,128)S(1)}, f32[128,1]{1,0:T(8,128)}, u32[]{:S(2)}) copy-start(f32[128,1]{1,0:T(8,128)} %get-tuple-element.15.dinv_ref) | copy-start | bytes 1540
  43.5 44.8 %copy-start.3 = (f32[256]{0:T(256)S(1)}, f32[256]{0:T(256)}, u32[]{:S(2)}) copy-start(f32[256]{0:T(256)} %param.11) | copy-start | bytes 3076
  43.6 44.8 %all-to-all-start.1 = ((bf16[32,24,8,128]{3,2,1,0:T(8,128)(2,1)}), bf16[32,24,8,128]{3,2,1,0:T(8,128)(2,1)S(1)}, u32[]{:S(2)}, u32[]{:S(2)}) async-start(bf16[32,24,8,128]{3,2,1,0:T(8,128)(2,1)} %shard_map.121), calls=%async_computation.1 | async-start | bytes 3145728 | tf_op jit(solution)/shard_map/all_to_all | solution.py:295
  138.7 19.2 %all-to-all-start.3 = ((f32[16,3,8,128]{3,2,1,0:T(8,128)}), f32[16,3,8,128]{3,2,1,0:T(8,128)S(1)}, u32[]{:S(2)}, u32[]{:S(2)}) async-start(f32[16,3,8,128]{3,2,1,0:T(8,128)} %broadcast_in_dim.18), calls=%async_computation.3 | async-start | bytes 393216 | tf_op jit(solution)/shard_map/all_to_all | solution.py:295
  144.6 10.8 %collective-permute-start.2 = (bf16[32,8,128]{2,1,0:T(8,128)(2,1)S(1)}, bf16[32,8,128]{2,1,0:T(8,128)(2,1)S(1)}, u32[]{:S(2)}, u32[]{:S(2)}) collective-permute-start(bf16[32,8,128]{2,1,0:T(8,128)(2,1)S(1)} %get-tuple-element.18), channel_id=1, source_target_pairs={{0,32},{32,0},{64,96},{96,64},{128,160},{160,128},{192,224},{224,1... | collective-permute-start | bytes 196616 | tf_op jit(solution)/shard_map/ppermute | solution.py:17
  149.3 8.6 %collective-permute-start.3 = (bf16[32,8,128]{2,1,0:T(8,128)(2,1)S(1)}, bf16[32,8,128]{2,1,0:T(8,128)(2,1)S(1)}, u32[]{:S(2)}, u32[]{:S(2)}) collective-permute-start(bf16[32,8,128]{2,1,0:T(8,128)(2,1)S(1)} %get-tuple-element.19), channel_id=1, source_target_pairs={{0,480},{32,64},{64,32},{96,128},{128,96},{160,192},{192,160},{224... | collective-permute-start | bytes 196616 | tf_op jit(solution)/shard_map/ppermute | solution.py:22

commit v6 on v5

--- a/solution.py
+++ b/solution.py
@@ -10,6 +10,7 @@
 
 SUB = 8
 LANE = 128
+SEGMENT = 8
 MIB = 1 << 20
 
 
@@ -28,6 +29,10 @@
 
 def smem():
     return pl.BlockSpec(memory_space=pltpu.SMEM)
+
+
+def hbm():
+    return pl.BlockSpec(memory_space=pltpu.HBM)
 
 
 def call(kernel, mib, out_shape, in_specs, out_specs, scratch=()):
@@ -53,12 +58,15 @@
     names_ref[:, pl.ds(0, cols_ref.shape[1])] = cols_ref[...].astype(jnp.float32)
     lane = lax.broadcasted_iota(jnp.int32, (rows, LANE), 1)
     note = jnp.where(lane < LANE // 2, names_ref[...], degree).reshape(groups, SUB, LANE).astype(jnp.bfloat16)
+    members = out_ref.shape[0]
     for half in range(2):
         scaled = x_ref[:, half * LANE : (half + 1) * LANE].astype(jnp.float32) * dinv
         scaled = scaled.reshape(groups, SUB, LANE).astype(jnp.bfloat16)
+        for q in range(members):
+            for sub in range(2):
+                out_ref[q, 2 * half + sub] = scaled[2 * (q % SEGMENT) + sub]
         for a in range(groups):
-            out_ref[half * groups + a, 0] = scaled[a]
-            out_ref[half * groups + a, 1] = note[a]
+            out_ref[half * groups + a, 4] = note[a]
 
 
 def cut(features, degree, cols):
@@ -67,7 +75,7 @@
         cut_kernel,
         60,
         (
-            jax.ShapeDtypeStruct((2 * rows // SUB, 2, SUB, LANE), jnp.bfloat16),
+            jax.ShapeDtypeStruct((2 * rows // SUB, 5, SUB, LANE), jnp.bfloat16),
             jax.ShapeDtypeStruct((rows, 1), jnp.float32),
         ),
         [vmem()] * 3,
@@ -113,40 +121,64 @@
     )(xk, yk)
 
 
-def select_kernel(members, per_part, idx_ref, first_ref, own_ref, second_ref, out_ref, near_ref):
-    listed = 3 * per_part
+def select_own_kernel(per_part, idx_ref, own_ref, out_ref, made_ref, sem):
+    members = own_ref.shape[0]
+    for d in range(SEGMENT):
+        for t in range(per_part):
+            at = jnp.bitwise_and(idx_ref[d * 3 * per_part + per_part + t], members - 1)
+            made_ref[d, t] = own_ref[at]
+    copy = pltpu.make_async_copy(made_ref, out_ref, sem)
+    copy.start()
+    copy.wait()
+
+
+def select_own(idx, own, per_part):
+    shape = (SEGMENT, per_part) + own.shape[1:]
+    return call(
+        functools.partial(select_own_kernel, per_part),
+        6,
+        jax.ShapeDtypeStruct(shape, own.dtype),
+        [smem(), vmem()],
+        hbm(),
+        [pltpu.VMEM(shape, own.dtype), pltpu.SemaphoreType.DMA],
+    )(idx, own)
+
+
+def select_far_kernel(per_part, idx_ref, first_ref, second_ref, out_ref, near_ref):
+    members = first_ref.shape[0]
     near_ref[pl.ds(0, members)] = first_ref[...]
     near_ref[pl.ds(members, members)] = second_ref[...]
-
-    def one(d, carry):
-        for t in range(listed):
-            at = idx_ref[d * listed + t]
-            if t // per_part == 1:
-                out_ref[d, t] = own_ref[jnp.bitwise_and(at, members - 1)]
-            else:
-                out_ref[d, t] = near_ref[jnp.bitwise_and(at, 2 * members - 1)]
-        return carry
-
-    lax.fori_loop(0, members, one, 0)
-
-
-def select(idx, first, own, second, per_part):
-    members = own.shape[0]
-    return call(
-        functools.partial(select_kernel, members, per_part),
+    for d in range(SEGMENT):
+        for t in range(2 * per_part):
+            place = t if t < per_part else t + per_part
+            at = jnp.bitwise_and(idx_ref[d * 3 * per_part + place], 2 * members - 1)
+            out_ref[d, t] = near_ref[at]
+
+
+def select_far(idx, first, second, per_part):
+    members = first.shape[0]
+    return call(
+        functools.partial(select_far_kernel, per_part),
         6,
-        jax.ShapeDtypeStruct((members, 3 * per_part, SUB, LANE), own.dtype),
-        [smem()] + [vmem()] * 3,
+        jax.ShapeDtypeStruct((SEGMENT, 2 * per_part) + first.shape[1:], first.dtype),
+        [smem(), vmem(), vmem()],
         vmem(),
-        [pltpu.VMEM((2 * members, SUB, LANE), own.dtype)],
-    )(idx, first, own, second)
-
-
-def layer_kernel(listed, slab_ref, x_ref, weight_ref, dinv_ref, bias_ref, cot_ref, hid_ref, part_ref):
+        [pltpu.VMEM((2 * members,) + first.shape[1:], first.dtype)],
+    )(idx, first, second)
+
+
+def layer_kernel(listed, slab_ref, xown_ref, xfar_ref, weight_ref, dinv_ref, bias_ref, cot_ref, hid_ref, part_ref):
     dinv = dinv_ref[...]
     groups = part_ref.shape[1]
-    span = listed * SUB
-    rows = [jnp.dot(slab_ref[...], x_ref[half], preferred_element_type=jnp.float32) for half in range(2)]
+    per_part = listed // 3
+    tall = 2 * SUB
+    edge = xown_ref.shape[0] * tall
+    rows = []
+    for half in range(2):
+        near = xown_ref[:, half].reshape(edge, LANE)
+        far = xfar_ref[:, half].reshape(2 * edge, LANE)
+        total = jnp.dot(slab_ref[:, :edge], near, preferred_element_type=jnp.float32)
+        rows.append(total + jnp.dot(slab_ref[:, edge:], far, preferred_element_type=jnp.float32))
     gathered = jnp.concatenate(rows, axis=1)
     high = gathered.astype(jnp.bfloat16)
     low = (gathered - high.astype(jnp.float32)).astype(jnp.bfloat16)
@@ -174,9 +206,17 @@
     for half in range(2):
         lanes = slice(half * LANE, (half + 1) * LANE)
         partial = lax.dot_general(slab_ref[...], back[:, lanes], contract, preferred_element_type=jnp.float32)
+        for holder in range(groups // 2):
+            at = holder * per_part * tall
+            near = partial[at : at + per_part * tall].reshape(per_part, 2, SUB, LANE)
+            at = edge + 2 * at
+            far = partial[at : at + 2 * per_part * tall].reshape(2 * per_part, 2, SUB, LANE)
+            for sub in range(2):
+                a = 2 * holder + sub
+                part_ref[half, a, pl.ds(0, per_part)] = far[:per_part, sub].astype(jnp.bfloat16)
+                part_ref[half, a, pl.ds(per_part, per_part)] = near[:, sub].astype(jnp.bfloat16)
+                part_ref[half, a, pl.ds(2 * per_part, per_part)] = far[per_part:, sub].astype(jnp.bfloat16)
         for a in range(groups):
-            piece = partial[a * span : (a + 1) * span, :].reshape(listed, SUB, LANE)
-            part_ref[half, a, pl.ds(0, listed)] = piece.astype(jnp.bfloat16)
             part_ref[half, a, listed] = extra
             top = (half * groups + a) * SUB
             for other in range(2):
@@ -184,16 +224,16 @@
                 part_ref[half, a, listed + 1 + other] = block.astype(jnp.bfloat16)
 
 
-def layer(slab, x, weight, dinv, bias, cotangent, listed):
+def layer(slab, xown, xfar, weight, dinv, bias, cotangent, listed):
     rows, width = cotangent.shape
     shape = (2, rows // SUB, listed + 3, SUB, LANE)
     return call(
         functools.partial(layer_kernel, listed),
         16,
         (jax.ShapeDtypeStruct((rows, width), jnp.bfloat16), jax.ShapeDtypeStruct(shape, jnp.bfloat16)),
-        [vmem()] * 6,
+        [vmem()] * 7,
         (vmem(), vmem()),
-    )(slab, x, weight, dinv, bias, cotangent)
+    )(slab, xown, xfar, weight, dinv, bias, cotangent)
 
 
 def collect_kernel(members, per_part, parts, chains, idx_ref, got_ref, *refs):
@@ -242,7 +282,7 @@
         bias_ref[:, half * LANE : (half + 1) * LANE] = total[0, half : half + 1] + total[0, half + 2 : half + 3]
     rows = [total[1].astype(jnp.bfloat16), total[2].astype(jnp.bfloat16)]
     for m in range(members):
-        dinv = lax.rsqrt(got_ref[m, 1].astype(jnp.float32)[:, LANE // 2 : LANE // 2 + 1])
+        dinv = lax.rsqrt(got_ref[m, 4].astype(jnp.float32)[:, LANE // 2 : LANE // 2 + 1])
         grad = own_ref[m] + first_ref[m].astype(jnp.float32) + second_ref[m].astype(jnp.float32)
         out_ref[m, 0] = (grad * dinv).astype(jnp.bfloat16)
         out_ref[m, 1] = rows[0]
@@ -295,6 +335,11 @@
     return lax.all_to_all(x, axis, 0, 0, tiled=True)
 
 
+def segment_swap(x, members):
+    groups = [list(range(first, first + SEGMENT)) for first in range(0, members, SEGMENT)]
+    return lax.all_to_all(x, "grp", 0, 0, axis_index_groups=groups, tiled=True)
+
+
 def per_device(features, weight, bias, cotangent, degree, tile_cols, edge_tile, edge_row, edge_col):
     rows, _ = features.shape
     members = lax.axis_size("grp")
@@ -304,24 +349,41 @@
 
     payload, dinv = cut(features, degree[None, :], tile_cols)
     got = swap(payload, "grp")
-    own = got[:, 0]
+    own = got[:, :4]
     first = with_partner(own, "rep")
     second = with_other(own, "rep")
 
-    names = got[:, 1, 0, :listed].astype(jnp.int32)
+    names = got[:, 4, 0, :listed].astype(jnp.int32)
     part = lax.broadcasted_iota(jnp.int32, names.shape, 1) // per_part
     even = lax.axis_index("rep") % 2 == 0
     late = jnp.where(even, part == 0, part == 2)
-    idx = (names % members + jnp.where(late, members, 0)).reshape(-1)
+    idx = names % members + jnp.where(late, members, 0)
+    segment = lax.axis_index("grp") // SEGMENT
+    idx = idx.reshape(-1)
+    near_idx = lax.dynamic_slice_in_dim(idx, segment * SEGMENT * listed, SEGMENT * listed, 0)
 
     tile = edge_tile[0]
     col = edge_col[0]
-    key = (col // SUB) * (listed * SUB) + tile * SUB + col % SUB
+    tall = 2 * SUB
+    far_tile = jnp.where(tile < per_part, tile, tile - per_part)
+    is_own = (tile >= per_part) & (tile < 2 * per_part)
+    own_key = (col // tall * per_part + tile - per_part) * tall
+    far_key = per_part * rows + (col // tall * 2 * per_part + far_tile) * tall
+    key = jnp.where(is_own, own_key, far_key) + col % tall
     slab = build_slab(edge_row[0], key, rows, listed * rows)
 
-    window = swap(select(idx, first, own, second, per_part), "grp")
+    chosen_own = select_own(near_idx, own, per_part)
+    window_own = segment_swap(chosen_own, members)
+    window_far = segment_swap(select_far(near_idx, first, second, per_part), members)
     hidden, partial = layer(
-        slab, window.reshape(2, listed * rows, LANE), weight, dinv, bias[None, :], cotangent, listed
+        slab,
+        window_own.reshape(rows // tall * per_part, 2, tall, LANE),
+        window_far.reshape(rows // tall * 2 * per_part, 2, tall, LANE),
+        weight,
+        dinv,
+        bias[None, :],
+        cotangent,
+        listed,
     )
     mine = swap(partial.reshape(members, listed + 3, SUB, LANE), "grp")
 

time: 176 us -> 167 us (0.949)
  waiting for transfers between devices: 51.7 us -> 35.3 us
  starting transfers between devices: 42.4 us -> 49.2 us
    all_to_all x3 -> x2, waiting for transfers between devices: 44.8 us -> 12.5 us  [swap(): return lax.all_to_all(x, axis, 0, 0, tiled=True)]
    all_to_all x0 -> x2, waiting for transfers between devices: none -> 9.91 us  [segment_swap(): return lax.all_to_all(x, 'grp', 0, 0, axis_index_groups=groups, tiled=True)]
    all_to_all x0 -> x2, starting transfers between devices: none -> 9.05 us  [segment_swap(): return lax.all_to_all(x, 'grp', 0, 0, axis_index_groups=groups, tiled=True)]
    ppermute x2, waiting for transfers between devices: 2.46 us -> 7.15 us  [with_other(): lax.ppermute(x, axis, [(i, (i + 1 if i % 2 else i - 1) % size) for i in r...]
    all_to_all x3 -> x2, starting transfers between devices: 19.5 us -> 17 us  [swap(): return lax.all_to_all(x, axis, 0, 0, tiled=True)]
    pallas_call x2 -> x3, Pallas kernels: 4.61 us -> 4.87 us  [the longest x1 1.73 us: cut(): call(cut_kernel, 60, (jax.ShapeDtypeStruct((2 * rows // SUB, 5, SUB, LANE...]
  transfers between devices with their start and end apart: 7 -> 8, of which waited for: 4 -> 5; matrix products, arithmetic and copies ran while one was open for 0% -> 0% of each run, Pallas kernels for 4% -> 5%
where the time goes in v6:
time: 167 us; the launch traced here: 166 us
  blocking collectives  63.9 us (38%)
  starting transfers between devices  49.2 us (29%)
  waiting for transfers between devices  35.3 us (21%)
  Pallas kernels  15.2 us (9%)
    all_to_all x2, blocking collectives, swap(): return lax.all_to_all(x, axis, 0, 0, tiled=True)  63.9 us
    all_to_all x2, starting transfers between devices, swap(): return lax.all_to_all(x, axis, 0, 0, tiled=True)  17 us
    ppermute x2, starting transfers between devices, with_other(): lax.ppermute(x, axis, [(i, (i + 1 if i % 2 else i - 1) % size) for i in r...  16.5 us
    all_to_all x2, waiting for transfers between devices, swap(): return lax.all_to_all(x, axis, 0, 0, tiled=True)  12.5 us
    all_to_all x2, waiting for transfers between devices, segment_swap(): return lax.all_to_all(x, 'grp', 0, 0, axis_index_groups=groups, tiled=True)  9.91 us
    all_to_all x2, starting transfers between devices, segment_swap(): return lax.all_to_all(x, 'grp', 0, 0, axis_index_groups=groups, tiled=True)  9.05 us
    ppermute x2, waiting for transfers between devices, with_other(): lax.ppermute(x, axis, [(i, (i + 1 if i % 2 else i - 1) % size) for i in r...  7.15 us
    ppermute x2, starting transfers between devices, with_partner(): lax.ppermute(x, axis, [(i, i ^ 1) for i in range(lax.axis_size(axis))])  6.7 us
  transfers between devices with their start and end apart: 8, of which 5 were waited for; matrix products, arithmetic and copies ran while one was open for 0% of the time, Pallas kernels for 5%

profile of v6, /device:TPU:1, one launch (start us, length us, event | category | flops | bytes accessed | tf_op | source)
XLA Modules:
  0.0 165.9 jit_solution(5423477136415405356)
XLA Ops:
  0.6 1.7 %shard_map.120 = (bf16[32,5,8,128]{3,2,1,0:T(8,128)(2,1)}, f32[128,1]{1,0:T(8,128)}) custom-call(bf16[128,256]{1,0:T(8,128)(2,1)} %x_ref.1, s32[1,128]{1,0:T(1,128)} %bitcast.10, s32[1,24]{1,0:T(1,128)} %cols_ref.1), custom_call_target="tpu_custom_call" | custom-call | tf_op jit(solution)/shard_map/pallas_call | solution.py:74
  2.4 10.4 %all-to-all-start = ((bf16[32,5,8,128]{3,2,1,0:T(8,128)(2,1)}), bf16[32,5,8,128]{3,2,1,0:T(8,128)(2,1)S(1)}, u32[]{:S(2)}, u32[]{:S(2)}) async-start(bf16[32,5,8,128]{3,2,1,0:T(8,128)(2,1)} %get-tuple-element.14), calls=%async_computation | async-start | bytes 655360 | tf_op jit(solution)/shard_map/all_to_all | solution.py:335
  12.9 12.5 %all-to-all-done.got_ref = bf16[32,5,8,128]{3,2,1,0:T(8,128)(2,1)S(1)} async-done(((bf16[32,5,8,128]{3,2,1,0:T(8,128)(2,1)}), bf16[32,5,8,128]{3,2,1,0:T(8,128)(2,1)S(1)}, u32[]{:S(2)}, u32[]{:S(2)}) %all-to-all-start) | async-done | bytes 327712 | tf_op jit(solution)/shard_map/all_to_all | solution.py:335
  25.6 1.4 shard_map.121
  27.1 4.9 %all-to-all-start.1 = ((bf16[8,8,4,8,128]{4,3,2,1,0:T(8,128)(2,1)}), bf16[8,8,4,8,128]{4,3,2,1,0:T(8,128)(2,1)S(1)}, u32[]{:S(2)}, u32[]{:S(2)}) async-start(bf16[8,8,4,8,128]{4,3,2,1,0:T(8,128)(2,1)} %shard_map.121), calls=%async_computation.1 | async-start | bytes 1048576 | tf_op jit(solution)/shard_map/all_to_all | solution.py:340
  32.0 12.2 %collective-permute-start.1 = (bf16[32,4,8,128]{3,2,1,0:T(8,128)(2,1)S(1)}, bf16[32,4,8,128]{3,2,1,0:T(8,128)(2,1)S(1)}, u32[]{:S(2)}, u32[]{:S(2)}) collective-permute-start(bf16[32,4,8,128]{3,2,1,0:T(8,128)(2,1)S(1)} %slice.13.own_ref), channel_id=1, source_target_pairs={{0,480},{32,64},{64,32},{96,128},{128,96},{160,192},{192,160},{224... | collective-permute-start | bytes 786440 | tf_op jit(solution)/shard_map/ppermute | solution.py:23
  44.2 1.9 %collective-permute-start = (bf16[32,4,8,128]{3,2,1,0:T(8,128)(2,1)S(1)}, bf16[32,4,8,128]{3,2,1,0:T(8,128)(2,1)S(1)}, u32[]{:S(2)}, u32[]{:S(2)}) collective-permute-start(bf16[32,4,8,128]{3,2,1,0:T(8,128)(2,1)S(1)} %slice.13.own_ref), channel_id=1, source_target_pairs={{0,32},{32,0},{64,96},{96,64},{128,160},{160,128},{192,224},{224,1... | collective-permute-start | bytes 786440 | tf_op jit(solution)/shard_map/ppermute | solution.py:18
  46.1 4.6 %collective-permute-done.1.second_ref = bf16[32,4,8,128]{3,2,1,0:T(8,128)(2,1)S(1)} collective-permute-done((bf16[32,4,8,128]{3,2,1,0:T(8,128)(2,1)S(1)}, bf16[32,4,8,128]{3,2,1,0:T(8,128)(2,1)S(1)}, u32[]{:S(2)}, u32[]{:S(2)}) %collective-permute-start.1) | collective-permute-done | bytes 262176 | tf_op jit(solution)/shard_map/ppermute | solution.py:23
  50.7 5.8 %collective-permute-done.first_ref = bf16[32,4,8,128]{3,2,1,0:T(8,128)(2,1)S(1)} collective-permute-done((bf16[32,4,8,128]{3,2,1,0:T(8,128)(2,1)S(1)}, bf16[32,4,8,128]{3,2,1,0:T(8,128)(2,1)S(1)}, u32[]{:S(2)}, u32[]{:S(2)}) %collective-permute-start) | collective-permute-done | bytes 262176 | tf_op jit(solution)/shard_map/ppermute | solution.py:18
  56.5 1.7 %shard_map.122 = bf16[8,16,4,8,128]{4,3,2,1,0:T(8,128)(2,1)} custom-call(s32[192]{0:T(256)S(1)} %dynamic_slice.3.idx_ref, bf16[32,4,8,128]{3,2,1,0:T(8,128)(2,1)S(1)} %collective-permute-done.first_ref, bf16[32,4,8,128]{3,2,1,0:T(8,128)(2,1)S(1)} %collective-permute-done.1.second_ref), custom_call_target="tpu_custom_call" | custom-call | tf_op jit(solution)/shard_map/pallas_call | solution.py:160
  58.2 4.1 %all-to-all-start.2 = ((bf16[8,16,4,8,128]{4,3,2,1,0:T(8,128)(2,1)}), bf16[8,16,4,8,128]{4,3,2,1,0:T(8,128)(2,1)S(1)}, u32[]{:S(2)}, u32[]{:S(2)}) async-start(bf16[8,16,4,8,128]{4,3,2,1,0:T(8,128)(2,1)} %shard_map.122), calls=%async_computation.2 | async-start | bytes 2097152 | tf_op jit(solution)/shard_map/all_to_all | solution.py:340
  62.7 3.3 %count.1.slab_ref = bf16[128,3072]{1,0:T(8,128)(2,1)S(1)} custom-call(s32[1,3840]{1,0:T(1,128)S(1)} %multiply_add_fusion.xk_ref, s32[1,3840]{1,0:T(1,128)S(1)} %get-tuple-element.24.yk_ref), custom_call_target="tpu_custom_call" | custom-call | tf_op jit(solution)/shard_map/count/pallas_call | solution.py:113
  66.0 9.9 %all-to-all-done.2 = bf16[8,16,4,8,128]{4,3,2,1,0:T(8,128)(2,1)S(1)} async-done(((bf16[8,16,4,8,128]{4,3,2,1,0:T(8,128)(2,1)}), bf16[8,16,4,8,128]{4,3,2,1,0:T(8,128)(2,1)S(1)}, u32[]{:S(2)}, u32[]{:S(2)}) %all-to-all-start.2) | async-done | bytes 1048608 | tf_op jit(solution)/shard_map/all_to_all | solution.py:340
  75.9 1.5 shard_map.123
  77.4 48.1 %all_to_all.30.got_ref = bf16[32,27,8,128]{3,2,1,0:T(8,128)(2,1)S(1)} all-to-all(bf16[32,27,8,128]{3,2,1,0:T(8,128)(2,1)S(1)} %bitcast.8), channel_id=1, replica_groups=mesh['rep'=16,'grp'=32] {'grp'}, dimensions={0} | all-to-all | bytes 3538944 | tf_op jit(solution)/shard_map/all_to_all | solution.py:335
  125.5 0.7 broadcast_in_dim.18
  126.2 6.6 %all-to-all-start.4 = ((f32[16,3,8,128]{3,2,1,0:T(8,128)}), f32[16,3,8,128]{3,2,1,0:T(8,128)S(1)}, u32[]{:S(2)}, u32[]{:S(2)}) async-start(f32[16,3,8,128]{3,2,1,0:T(8,128)} %broadcast_in_dim.18), calls=%async_computation.4 | async-start | bytes 393216 | tf_op jit(solution)/shard_map/all_to_all | solution.py:335
  132.8 2.4 %shard_map.125 = (bf16[32,8,128]{2,1,0:T(8,128)(2,1)S(1)}, bf16[32,8,128]{2,1,0:T(8,128)(2,1)S(1)}) custom-call(s32[768]{0:T(1024)S(1)} %fusion.6.idx_ref, bf16[32,27,8,128]{3,2,1,0:T(8,128)(2,1)S(1)} %all_to_all.30.got_ref), custom_call_target="tpu_custom_call" | custom-call | tf_op jit(solution)/shard_map/pallas_call | solution.py:266
  135.2 4.8 %collective-permute-start.2 = (bf16[32,8,128]{2,1,0:T(8,128)(2,1)S(1)}, bf16[32,8,128]{2,1,0:T(8,128)(2,1)S(1)}, u32[]{:S(2)}, u32[]{:S(2)}) collective-permute-start(bf16[32,8,128]{2,1,0:T(8,128)(2,1)S(1)} %get-tuple-element.18), channel_id=1, source_target_pairs={{0,32},{32,0},{64,96},{96,64},{128,160},{160,128},{192,224},{224,1... | collective-permute-start | bytes 196616 | tf_op jit(solution)/shard_map/ppermute | solution.py:18
  140.0 4.3 %collective-permute-start.3 = (bf16[32,8,128]{2,1,0:T(8,128)(2,1)S(1)}, bf16[32,8,128]{2,1,0:T(8,128)(2,1)S(1)}, u32[]{:S(2)}, u32[]{:S(2)}) collective-permute-start(bf16[32,8,128]{2,1,0:T(8,128)(2,1)S(1)} %get-tuple-element.19), channel_id=1, source_target_pairs={{0,480},{32,64},{64,32},{96,128},{128,96},{160,192},{192,160},{224... | collective-permute-start | bytes 196616 | tf_op jit(solution)/shard_map/ppermute | solution.py:23
  144.3 1.7 %shard_map.124.own_ref = f32[32,8,128]{2,1,0:T(8,128)S(1)} custom-call(s32[768]{0:T(1024)S(1)} %fusion.6.idx_ref, bf16[32,27,8,128]{3,2,1,0:T(8,128)(2,1)S(1)} %all_to_all.30.got_ref), custom_call_target="tpu_custom_call" | custom-call | tf_op jit(solution)/shard_map/pallas_call | solution.py:266
  146.1 2.5 %collective-permute-done.3.second_ref = bf16[32,8,128]{2,1,0:T(8,128)(2,1)S(1)} collective-permute-done((bf16[32,8,128]{2,1,0:T(8,128)(2,1)S(1)}, bf16[32,8,128]{2,1,0:T(8,128)(2,1)S(1)}, u32[]{:S(2)}, u32[]{:S(2)}) %collective-permute-start.3) | collective-permute-done | bytes 65568 | tf_op jit(solution)/shard_map/ppermute | solution.py:23
  149.2 15.8 %all_to_all.31.final_ref = bf16[32,3,8,128]{3,2,1,0:T(8,128)(2,1)S(1)} all-to-all(bf16[32,3,8,128]{3,2,1,0:T(8,128)(2,1)S(1)} %get-tuple-element.20), channel_id=1, replica_groups=mesh['rep'=16,'grp'=32] {'grp'}, dimensions={0} | all-to-all | bytes 393216 | tf_op jit(solution)/shard_map/all_to_all | solution.py:335
  165.0 0.8 shard_map.127
  (30 shorter events, 1.3 us)
Async XLA Ops:
  2.4 23.0 %all-to-all-start = ((bf16[32,5,8,128]{3,2,1,0:T(8,128)(2,1)}), bf16[32,5,8,128]{3,2,1,0:T(8,128)(2,1)S(1)}, u32[]{:S(2)}, u32[]{:S(2)}) async-start(bf16[32,5,8,128]{3,2,1,0:T(8,128)(2,1)} %get-tuple-element.14), calls=%async_computation | async-start | bytes 655360 | tf_op jit(solution)/shard_map/all_to_all | solution.py:335
  27.1 31.2 %all-to-all-start.1 = ((bf16[8,8,4,8,128]{4,3,2,1,0:T(8,128)(2,1)}), bf16[8,8,4,8,128]{4,3,2,1,0:T(8,128)(2,1)S(1)}, u32[]{:S(2)}, u32[]{:S(2)}) async-start(bf16[8,8,4,8,128]{4,3,2,1,0:T(8,128)(2,1)} %shard_map.121), calls=%async_computation.1 | async-start | bytes 1048576 | tf_op jit(solution)/shard_map/all_to_all | solution.py:340
  32.0 30.4 %copy-start.5 = (s32[1,3840]{1,0:T(1,128)S(1)}, s32[1,3840]{1,0:T(1,128)}, u32[]{:S(2)}) copy-start(s32[1,3840]{1,0:T(1,128)} %param.15) | copy-start | bytes 46084
  32.0 30.4 %copy-start.6 = (s32[1,3840]{1,0:T(1,128)S(1)}, s32[1,3840]{1,0:T(1,128)}, u32[]{:S(2)}) copy-start(s32[1,3840]{1,0:T(1,128)} %param.17) | copy-start | bytes 46084
  32.0 30.6 %copy-start.4 = (s32[1,3840]{1,0:T(1,128)S(1)}, s32[1,3840]{1,0:T(1,128)}, u32[]{:S(2)}) copy-start(s32[1,3840]{1,0:T(1,128)} %param.16) | copy-start | bytes 46084
  32.0 18.7 %collective-permute-start.1 = (bf16[32,4,8,128]{3,2,1,0:T(8,128)(2,1)S(1)}, bf16[32,4,8,128]{3,2,1,0:T(8,128)(2,1)S(1)}, u32[]{:S(2)}, u32[]{:S(2)}) collective-permute-start(bf16[32,4,8,128]{3,2,1,0:T(8,128)(2,1)S(1)} %slice.13.own_ref), channel_id=1, source_target_pairs={{0,480},{32,64},{64,32},{96,128},{128,96},{160,192},{192,160},{224... | collective-permute-start | bytes 786440 | tf_op jit(solution)/shard_map/ppermute | solution.py:23
  44.2 12.3 %collective-permute-start = (bf16[32,4,8,128]{3,2,1,0:T(8,128)(2,1)S(1)}, bf16[32,4,8,128]{3,2,1,0:T(8,128)(2,1)S(1)}, u32[]{:S(2)}, u32[]{:S(2)}) collective-permute-start(bf16[32,4,8,128]{3,2,1,0:T(8,128)(2,1)S(1)} %slice.13.own_ref), channel_id=1, source_target_pairs={{0,32},{32,0},{64,96},{96,64},{128,160},{160,128},{192,224},{224,1... | collective-permute-start | bytes 786440 | tf_op jit(solution)/shard_map/ppermute | solution.py:18
  58.2 17.7 %copy-start = (bf16[256,256]{1,0:T(8,128)(2,1)S(1)}, bf16[256,256]{1,0:T(8,128)(2,1)}, u32[]{:S(2)}) copy-start(bf16[256,256]{1,0:T(8,128)(2,1)} %weight_ref.3) | copy-start | bytes 393220
  58.2 17.7 %copy-start.1 = (bf16[128,256]{1,0:T(8,128)(2,1)S(1)}, bf16[128,256]{1,0:T(8,128)(2,1)}, u32[]{:S(2)}) copy-start(bf16[128,256]{1,0:T(8,128)(2,1)} %cot_ref.1) | copy-start | bytes 196612
  58.2 17.7 %copy-start.2 = (f32[128,1]{1,0:T(8,128)S(1)}, f32[128,1]{1,0:T(8,128)}, u32[]{:S(2)}) copy-start(f32[128,1]{1,0:T(8,128)} %get-tuple-element.15.dinv_ref) | copy-start | bytes 1540
  58.2 17.7 %copy-start.3 = (f32[256]{0:T(256)S(1)}, f32[256]{0:T(256)}, u32[]{:S(2)}) copy-start(f32[256]{0:T(256)} %param.11) | copy-start | bytes 3076
  58.2 17.7 %all-to-all-start.2 = ((bf16[8,16,4,8,128]{4,3,2,1,0:T(8,128)(2,1)}), bf16[8,16,4,8,128]{4,3,2,1,0:T(8,128)(2,1)S(1)}, u32[]{:S(2)}, u32[]{:S(2)}) async-start(bf16[8,16,4,8,128]{4,3,2,1,0:T(8,128)(2,1)} %shard_map.122), calls=%async_computation.2 | async-start | bytes 2097152 | tf_op jit(solution)/shard_map/all_to_all | solution.py:340
  126.2 22.4 %all-to-all-start.4 = ((f32[16,3,8,128]{3,2,1,0:T(8,128)}), f32[16,3,8,128]{3,2,1,0:T(8,128)S(1)}, u32[]{:S(2)}, u32[]{:S(2)}) async-start(f32[16,3,8,128]{3,2,1,0:T(8,128)} %broadcast_in_dim.18), calls=%async_computation.4 | async-start | bytes 393216 | tf_op jit(solution)/shard_map/all_to_all | solution.py:335
  135.2 10.9 %collective-permute-start.2 = (bf16[32,8,128]{2,1,0:T(8,128)(2,1)S(1)}, bf16[32,8,128]{2,1,0:T(8,128)(2,1)S(1)}, u32[]{:S(2)}, u32[]{:S(2)}) collective-permute-start(bf16[32,8,128]{2,1,0:T(8,128)(2,1)S(1)} %get-tuple-element.18), channel_id=1, source_target_pairs={{0,32},{32,0},{64,96},{96,64},{128,160},{160,128},{192,224},{224,1... | collective-permute-start | bytes 196616 | tf_op jit(solution)/shard_map/ppermute | solution.py:18
  140.0 8.6 %collective-permute-start.3 = (bf16[32,8,128]{2,1,0:T(8,128)(2,1)S(1)}, bf16[32,8,128]{2,1,0:T(8,128)(2,1)S(1)}, u32[]{:S(2)}, u32[]{:S(2)}) collective-permute-start(bf16[32,8,128]{2,1,0:T(8,128)(2,1)S(1)} %get-tuple-element.19), channel_id=1, source_target_pairs={{0,480},{32,64},{64,32},{96,128},{128,96},{160,192},{192,160},{224... | collective-permute-start | bytes 196616 | tf_op jit(solution)/shard_map/ppermute | solution.py:23

commit v7 on v6

--- a/solution.py
+++ b/solution.py
@@ -167,9 +167,9 @@
     )(idx, first, second)
 
 
-def layer_kernel(listed, slab_ref, xown_ref, xfar_ref, weight_ref, dinv_ref, bias_ref, cot_ref, hid_ref, part_ref):
+def layer_kernel(listed, slab_ref, xown_ref, xfar_ref, weight_ref, dinv_ref, bias_ref, cot_ref, hid_ref, part_ref, out_ref, grad_ref, sem):
     dinv = dinv_ref[...]
-    groups = part_ref.shape[1]
+    members = grad_ref.shape[0]
     per_part = listed // 3
     tall = 2 * SUB
     edge = xown_ref.shape[0] * tall
@@ -203,36 +203,42 @@
             lanes = slice(half * LANE, (half + 1) * LANE)
             extra = jnp.where(at == 2 * index + half, value[:, lanes], extra)
     extra = extra.astype(jnp.bfloat16)
+    for q in range(members):
+        grad_ref[q, 0] = extra
+        for half in range(2):
+            block = grad[q * SUB : (q + 1) * SUB, half * LANE : (half + 1) * LANE]
+            grad_ref[q, 1 + half] = block.astype(jnp.bfloat16)
+    copy = pltpu.make_async_copy(grad_ref, out_ref, sem)
+    copy.start()
     for half in range(2):
         lanes = slice(half * LANE, (half + 1) * LANE)
+        pair = pl.ds(2 * half, 2)
         partial = lax.dot_general(slab_ref[...], back[:, lanes], contract, preferred_element_type=jnp.float32)
-        for holder in range(groups // 2):
+        for holder in range(SEGMENT):
             at = holder * per_part * tall
-            near = partial[at : at + per_part * tall].reshape(per_part, 2, SUB, LANE)
+            near = partial[at : at + per_part * tall].reshape(per_part, 2, SUB, LANE).astype(jnp.bfloat16)
             at = edge + 2 * at
-            far = partial[at : at + 2 * per_part * tall].reshape(2 * per_part, 2, SUB, LANE)
-            for sub in range(2):
-                a = 2 * holder + sub
-                part_ref[half, a, pl.ds(0, per_part)] = far[:per_part, sub].astype(jnp.bfloat16)
-                part_ref[half, a, pl.ds(per_part, per_part)] = near[:, sub].astype(jnp.bfloat16)
-                part_ref[half, a, pl.ds(2 * per_part, per_part)] = far[per_part:, sub].astype(jnp.bfloat16)
-        for a in range(groups):
-            part_ref[half, a, listed] = extra
-            top = (half * groups + a) * SUB
-            for other in range(2):
-                block = grad[top : top + SUB, other * LANE : (other + 1) * LANE]
-                part_ref[half, a, listed + 1 + other] = block.astype(jnp.bfloat16)
-
-
-def layer(slab, xown, xfar, weight, dinv, bias, cotangent, listed):
+            far = partial[at : at + 2 * per_part * tall].reshape(2 * per_part, 2, SUB, LANE).astype(jnp.bfloat16)
+            part_ref[holder, pl.ds(0, per_part), pair] = far[:per_part]
+            part_ref[holder, pl.ds(per_part, per_part), pair] = near
+            part_ref[holder, pl.ds(2 * per_part, per_part), pair] = far[per_part:]
+    copy.wait()
+
+
+def layer(slab, xown, xfar, weight, dinv, bias, cotangent, members, listed):
     rows, width = cotangent.shape
-    shape = (2, rows // SUB, listed + 3, SUB, LANE)
+    grad = (members, 3, SUB, LANE)
     return call(
         functools.partial(layer_kernel, listed),
         16,
-        (jax.ShapeDtypeStruct((rows, width), jnp.bfloat16), jax.ShapeDtypeStruct(shape, jnp.bfloat16)),
+        (
+            jax.ShapeDtypeStruct((rows, width), jnp.bfloat16),
+            jax.ShapeDtypeStruct((SEGMENT, listed, 4, SUB, LANE), jnp.bfloat16),
+            jax.ShapeDtypeStruct(grad, jnp.bfloat16),
+        ),
         [vmem()] * 7,
-        (vmem(), vmem()),
+        (vmem(), vmem(), hbm()),
+        [pltpu.VMEM(grad, jnp.bfloat16), pltpu.SemaphoreType.DMA],
     )(slab, xown, xfar, weight, dinv, bias, cotangent)
 
 
@@ -240,17 +246,13 @@
     outs, acc_ref = refs[:-1], refs[-1]
     acc_ref[...] = jnp.zeros_like(acc_ref)
     tiles = acc_ref.shape[1]
-
-    def some(step, carry):
+    for step in range(SEGMENT // chains):
         for part in parts:
             for t in range(part * per_part, (part + 1) * per_part):
                 for j in range(chains):
                     d = step * chains + j
                     at = jnp.bitwise_and(idx_ref[d * 3 * per_part + t], tiles - 1)
                     acc_ref[j, at] += got_ref[d, t].astype(jnp.float32)
-        return carry
-
-    lax.fori_loop(0, members // chains, some, 0)
     for number, ref in enumerate(outs):
         part = pl.ds(number * members, members)
         value = acc_ref[0, part]
@@ -259,21 +261,20 @@
         ref[...] = value.astype(ref.dtype)
 
 
-def collect(idx, parts, got, per_part, dtype):
-    members = got.shape[0]
-    chains = 4
-    piece = (members, SUB, LANE)
+def collect(idx, parts, got, members, per_part, dtype):
+    chains = 2
+    piece = (members,) + got.shape[2:]
     return call(
         functools.partial(collect_kernel, members, per_part, parts, chains),
-        6,
+        8,
         tuple(jax.ShapeDtypeStruct(piece, dtype) for _ in parts),
         [smem(), vmem()],
         (vmem(),) * len(parts),
-        [pltpu.VMEM((chains, len(parts) * members, SUB, LANE), jnp.float32)],
+        [pltpu.VMEM((chains, len(parts) * members) + got.shape[2:], jnp.float32)],
     )(idx, got)
 
 
-def join_kernel(got_ref, own_ref, first_ref, second_ref, share_ref, out_ref, bias_ref):
+def join_kernel(own_ref, first_ref, second_ref, share_ref, out_ref, bias_ref):
     members = own_ref.shape[0]
     total = share_ref[0]
     for ring in range(1, share_ref.shape[0]):
@@ -282,43 +283,48 @@
         bias_ref[:, half * LANE : (half + 1) * LANE] = total[0, half : half + 1] + total[0, half + 2 : half + 3]
     rows = [total[1].astype(jnp.bfloat16), total[2].astype(jnp.bfloat16)]
     for m in range(members):
-        dinv = lax.rsqrt(got_ref[m, 4].astype(jnp.float32)[:, LANE // 2 : LANE // 2 + 1])
         grad = own_ref[m] + first_ref[m].astype(jnp.float32) + second_ref[m].astype(jnp.float32)
-        out_ref[m, 0] = (grad * dinv).astype(jnp.bfloat16)
-        out_ref[m, 1] = rows[0]
-        out_ref[m, 2] = rows[1]
-
-
-def join(got, own, first, second, share):
+        out_ref[m, pl.ds(0, 4)] = grad.astype(jnp.bfloat16)
+        out_ref[m, 4] = rows[0]
+        out_ref[m, 5] = rows[1]
+
+
+def join(own, first, second, share):
     members = own.shape[0]
     return call(
         join_kernel,
-        4,
+        6,
         (
-            jax.ShapeDtypeStruct((members, 3, SUB, LANE), jnp.bfloat16),
+            jax.ShapeDtypeStruct((members, 6, SUB, LANE), jnp.bfloat16),
             jax.ShapeDtypeStruct((1, 2 * LANE), jnp.float32),
         ),
-        [vmem()] * 5,
+        [vmem()] * 4,
         (vmem(), vmem()),
-    )(got, own, first, second, share)
-
-
-def finish_kernel(final_ref, weight_ref, features_ref, weight_grad_ref):
+    )(own, first, second, share)
+
+
+def finish_kernel(final_ref, dinv_ref, weight_ref, features_ref, weight_grad_ref):
     members = final_ref.shape[0]
-    groups = members // 2
-    sides = [final_ref[pl.ds(half * groups, groups), 0].astype(jnp.float32).reshape(-1, LANE) for half in range(2)]
+    dinv = dinv_ref[...]
+    sides = []
+    for half in range(2):
+        pair = pl.ds(2 * half, 2)
+        total = final_ref[pl.ds(0, SEGMENT), pair].astype(jnp.float32)
+        for first in range(SEGMENT, members, SEGMENT):
+            total = total + final_ref[pl.ds(first, SEGMENT), pair].astype(jnp.float32)
+        sides.append(total.reshape(-1, LANE) * dinv)
     grad = jnp.concatenate(sides, axis=1).astype(jnp.bfloat16)
     features_ref[...] = lax.dot_general(
         grad, weight_ref[...], (((1,), (1,)), ((), ())), preferred_element_type=jnp.float32
     ).astype(features_ref.dtype)
     for half in range(2):
-        rows = final_ref[:, 1 + half].astype(jnp.float32).reshape(-1, LANE)
+        rows = final_ref[:, 4 + half].astype(jnp.float32).reshape(-1, LANE)
         weight_grad_ref[:, half * LANE : (half + 1) * LANE] = rows
 
 
-def finish(final, weight):
+def finish(final, dinv, weight):
     width = weight.shape[0]
-    rows = final.shape[0] // 2 * SUB
+    rows = dinv.shape[0]
     return call(
         finish_kernel,
         6,
@@ -326,9 +332,9 @@
             jax.ShapeDtypeStruct((rows, width), jnp.bfloat16),
             jax.ShapeDtypeStruct((width, width), jnp.float32),
         ),
-        [vmem(), vmem()],
+        [vmem()] * 3,
         (vmem(), vmem()),
-    )(final, weight)
+    )(final, dinv, weight)
 
 
 def swap(x, axis):
@@ -375,7 +381,7 @@
     chosen_own = select_own(near_idx, own, per_part)
     window_own = segment_swap(chosen_own, members)
     window_far = segment_swap(select_far(near_idx, first, second, per_part), members)
-    hidden, partial = layer(
+    hidden, partial, grad = layer(
         slab,
         window_own.reshape(rows // tall * per_part, 2, tall, LANE),
         window_far.reshape(rows // tall * 2 * per_part, 2, tall, LANE),
@@ -383,20 +389,21 @@
         dinv,
         bias[None, :],
         cotangent,
+        members,
         listed,
     )
-    mine = swap(partial.reshape(members, listed + 3, SUB, LANE), "grp")
-
-    share = mine[:, listed:].astype(jnp.float32).sum(axis=0)
+    mine = segment_swap(partial, members)
+    grad = swap(grad, "grp")
+    share = grad.astype(jnp.float32).sum(axis=0)
     share = swap(jnp.broadcast_to(share[None], (rings, 3, SUB, LANE)), "rep")
-    to_first, to_second = collect(idx, (0, 2), mine, per_part, jnp.bfloat16)
+    to_first, to_second = collect(near_idx, (0, 2), mine, members, per_part, jnp.bfloat16)
     from_first = with_partner(to_first, "rep")
     from_second = with_other(to_second, "rep")
-    (own_sum,) = collect(idx, (1,), mine, per_part, jnp.float32)
-
-    final, grad_bias = join(got, own_sum, from_first, from_second, share)
+    (own_sum,) = collect(near_idx, (1,), mine, members, per_part, jnp.float32)
+
+    final, grad_bias = join(own_sum, from_first, from_second, share)
     final = swap(final, "grp")
-    grad_features, grad_weight = finish(final, weight)
+    grad_features, grad_weight = finish(final, dinv, weight)
     return (hidden, grad_features, grad_weight, grad_bias[0])
 
 

time: 167 us -> 165 us (0.988)
  blocking collectives: 63.9 us -> 34 us
  waiting for transfers between devices: 35.3 us -> 58.2 us
  starting transfers between devices: 49.2 us -> 53.4 us
    all_to_all x2, blocking collectives: 63.9 us -> 34 us  [swap(): return lax.all_to_all(x, axis, 0, 0, tiled=True)]
    all_to_all x2 -> x3, waiting for transfers between devices: 9.91 us -> 29 us  [segment_swap(): return lax.all_to_all(x, 'grp', 0, 0, axis_index_groups=groups, tiled=True)]
    ppermute x2, waiting for transfers between devices: 5.8 us -> 11 us  [with_partner(): lax.ppermute(x, axis, [(i, i ^ 1) for i in range(lax.axis_size(axis))])]
    all_to_all x2 -> x3, starting transfers between devices: 9.05 us -> 13.3 us  [segment_swap(): return lax.all_to_all(x, 'grp', 0, 0, axis_index_groups=groups, tiled=True)]
  transfers between devices with their start and end apart: 8 -> 9, of which waited for: 5 -> 7; matrix products, arithmetic and copies ran while one was open for 0% -> 0% of each run, Pallas kernels for 5% -> 5%
where the time goes in v7:
time: 165 us; the launch traced here: 164 us
  waiting for transfers between devices  58.2 us (35%)
  starting transfers between devices  53.4 us (32%)
  blocking collectives  34 us (21%)
  Pallas kernels  15 us (9%)
  local copies, waits for them, and re-layouts  2.12 us (1%)
    all_to_all x2, blocking collectives, swap(): return lax.all_to_all(x, axis, 0, 0, tiled=True)  34 us
    all_to_all x3, waiting for transfers between devices, segment_swap(): return lax.all_to_all(x, 'grp', 0, 0, axis_index_groups=groups, tiled=True)  29 us
    all_to_all x2, starting transfers between devices, swap(): return lax.all_to_all(x, axis, 0, 0, tiled=True)  17 us
    ppermute x2, starting transfers between devices, with_other(): lax.ppermute(x, axis, [(i, (i + 1 if i % 2 else i - 1) % size) for i in r...  16.5 us
    all_to_all x3, starting transfers between devices, segment_swap(): return lax.all_to_all(x, 'grp', 0, 0, axis_index_groups=groups, tiled=True)  13.3 us
    all_to_all x2, waiting for transfers between devices, swap(): return lax.all_to_all(x, axis, 0, 0, tiled=True)  12.5 us
    ppermute x2, waiting for transfers between devices, with_partner(): lax.ppermute(x, axis, [(i, i ^ 1) for i in range(lax.axis_size(axis))])  11 us
    ppermute x2, starting transfers between devices, with_partner(): lax.ppermute(x, axis, [(i, i ^ 1) for i in range(lax.axis_size(axis))])  6.68 us
  transfers between devices with their start and end apart: 9, of which 7 were waited for; matrix products, arithmetic and copies ran while one was open for 0% of the time, Pallas kernels for 5%

profile of v7, /device:TPU:1, one launch (start us, length us, event | category | flops | bytes accessed | tf_op | source)
XLA Modules:
  0.0 164.1 jit_solution(1202542894013947591)
XLA Ops:
  0.6 1.7 %shard_map.120 = (bf16[32,5,8,128]{3,2,1,0:T(8,128)(2,1)}, f32[128,1]{1,0:T(8,128)}) custom-call(bf16[128,256]{1,0:T(8,128)(2,1)} %x_ref.1, s32[1,128]{1,0:T(1,128)} %bitcast.8, s32[1,24]{1,0:T(1,128)} %cols_ref.1), custom_call_target="tpu_custom_call" | custom-call | tf_op jit(solution)/shard_map/pallas_call | solution.py:74
  2.3 10.4 %all-to-all-start = ((bf16[32,5,8,128]{3,2,1,0:T(8,128)(2,1)}), bf16[32,5,8,128]{3,2,1,0:T(8,128)(2,1)S(1)}, u32[]{:S(2)}, u32[]{:S(2)}) async-start(bf16[32,5,8,128]{3,2,1,0:T(8,128)(2,1)} %get-tuple-element.15), calls=%async_computation | async-start | bytes 655360 | tf_op jit(solution)/shard_map/all_to_all | solution.py:341
  12.9 12.5 %all-to-all-done = bf16[32,5,8,128]{3,2,1,0:T(8,128)(2,1)S(1)} async-done(((bf16[32,5,8,128]{3,2,1,0:T(8,128)(2,1)}), bf16[32,5,8,128]{3,2,1,0:T(8,128)(2,1)S(1)}, u32[]{:S(2)}, u32[]{:S(2)}) %all-to-all-start) | async-done | bytes 327712 | tf_op jit(solution)/shard_map/all_to_all | solution.py:341
  25.6 1.4 shard_map.121
  27.0 4.9 %all-to-all-start.1 = ((bf16[8,8,4,8,128]{4,3,2,1,0:T(8,128)(2,1)}), bf16[8,8,4,8,128]{4,3,2,1,0:T(8,128)(2,1)S(1)}, u32[]{:S(2)}, u32[]{:S(2)}) async-start(bf16[8,8,4,8,128]{4,3,2,1,0:T(8,128)(2,1)} %shard_map.121), calls=%async_computation.1 | async-start | bytes 1048576 | tf_op jit(solution)/shard_map/all_to_all | solution.py:346
  32.0 12.2 %collective-permute-start.1 = (bf16[32,4,8,128]{3,2,1,0:T(8,128)(2,1)S(1)}, bf16[32,4,8,128]{3,2,1,0:T(8,128)(2,1)S(1)}, u32[]{:S(2)}, u32[]{:S(2)}) collective-permute-start(bf16[32,4,8,128]{3,2,1,0:T(8,128)(2,1)S(1)} %slice.9.own_ref), channel_id=1, source_target_pairs={{0,480},{32,64},{64,32},{96,128},{128,96},{160,192},{192,160},{224... | collective-permute-start | bytes 786440 | tf_op jit(solution)/shard_map/ppermute | solution.py:23
  44.1 1.9 %collective-permute-start = (bf16[32,4,8,128]{3,2,1,0:T(8,128)(2,1)S(1)}, bf16[32,4,8,128]{3,2,1,0:T(8,128)(2,1)S(1)}, u32[]{:S(2)}, u32[]{:S(2)}) collective-permute-start(bf16[32,4,8,128]{3,2,1,0:T(8,128)(2,1)S(1)} %slice.9.own_ref), channel_id=1, source_target_pairs={{0,32},{32,0},{64,96},{96,64},{128,160},{160,128},{192,224},{224,1... | collective-permute-start | bytes 786440 | tf_op jit(solution)/shard_map/ppermute | solution.py:18
  46.1 4.6 %collective-permute-done.1.second_ref = bf16[32,4,8,128]{3,2,1,0:T(8,128)(2,1)S(1)} collective-permute-done((bf16[32,4,8,128]{3,2,1,0:T(8,128)(2,1)S(1)}, bf16[32,4,8,128]{3,2,1,0:T(8,128)(2,1)S(1)}, u32[]{:S(2)}, u32[]{:S(2)}) %collective-permute-start.1) | collective-permute-done | bytes 262176 | tf_op jit(solution)/shard_map/ppermute | solution.py:23
  50.7 5.8 %collective-permute-done.first_ref = bf16[32,4,8,128]{3,2,1,0:T(8,128)(2,1)S(1)} collective-permute-done((bf16[32,4,8,128]{3,2,1,0:T(8,128)(2,1)S(1)}, bf16[32,4,8,128]{3,2,1,0:T(8,128)(2,1)S(1)}, u32[]{:S(2)}, u32[]{:S(2)}) %collective-permute-start) | collective-permute-done | bytes 262176 | tf_op jit(solution)/shard_map/ppermute | solution.py:18
  56.5 1.7 %shard_map.122 = bf16[8,16,4,8,128]{4,3,2,1,0:T(8,128)(2,1)} custom-call(s32[192]{0:T(256)S(1)} %dynamic_slice.3.idx_ref, bf16[32,4,8,128]{3,2,1,0:T(8,128)(2,1)S(1)} %collective-permute-done.first_ref, bf16[32,4,8,128]{3,2,1,0:T(8,128)(2,1)S(1)} %collective-permute-done.1.second_ref), custom_call_target="tpu_custom_call" | custom-call | tf_op jit(solution)/shard_map/pallas_call | solution.py:160
  58.2 4.1 %all-to-all-start.2 = ((bf16[8,16,4,8,128]{4,3,2,1,0:T(8,128)(2,1)}), bf16[8,16,4,8,128]{4,3,2,1,0:T(8,128)(2,1)S(1)}, u32[]{:S(2)}, u32[]{:S(2)}) async-start(bf16[8,16,4,8,128]{4,3,2,1,0:T(8,128)(2,1)} %shard_map.122), calls=%async_computation.2 | async-start | bytes 2097152 | tf_op jit(solution)/shard_map/all_to_all | solution.py:346
  62.7 3.3 %count.1.slab_ref = bf16[128,3072]{1,0:T(8,128)(2,1)S(1)} custom-call(s32[1,3840]{1,0:T(1,128)S(1)} %multiply_add_fusion.xk_ref, s32[1,3840]{1,0:T(1,128)S(1)} %get-tuple-element.26.yk_ref), custom_call_target="tpu_custom_call" | custom-call | tf_op jit(solution)/shard_map/count/pallas_call | solution.py:113
  66.0 9.9 %all-to-all-done.2 = bf16[8,16,4,8,128]{4,3,2,1,0:T(8,128)(2,1)S(1)} async-done(((bf16[8,16,4,8,128]{4,3,2,1,0:T(8,128)(2,1)}), bf16[8,16,4,8,128]{4,3,2,1,0:T(8,128)(2,1)S(1)}, u32[]{:S(2)}, u32[]{:S(2)}) %all-to-all-start.2) | async-done | bytes 1048608 | tf_op jit(solution)/shard_map/all_to_all | solution.py:346
  75.9 2.5 %shard_map.123 = (bf16[128,256]{1,0:T(8,128)(2,1)}, bf16[8,24,4,8,128]{4,3,2,1,0:T(8,128)(2,1)S(1)}, bf16[32,3,8,128]{3,2,1,0:T(8,128)(2,1)S(1)}) custom-call(bf16[128,3072]{1,0:T(8,128)(2,1)S(1)} %count.1.slab_ref, bf16[64,2,16,128]{3,2,1,0:T(8,128)(2,1)S(1)} %bitcast.6, bf16[128,2,16,128]{3,2,1,0:T(8,128)(2,1)S(1)} %bitcast.5, ...), custom_call_target="tpu_custom_call" | custom-call | tf_op jit(solution)/shard_map/pallas_call | solution.py:231
  78.4 1.2 copy-done
  79.6 14.6 %all_to_all.35 = bf16[32,3,8,128]{3,2,1,0:T(8,128)(2,1)S(1)} all-to-all(bf16[32,3,8,128]{3,2,1,0:T(8,128)(2,1)S(1)} %get-tuple-element.21), channel_id=1, replica_groups=mesh['rep'=16,'grp'=32] {'grp'}, dimensions={0} | all-to-all | bytes 393216 | tf_op jit(solution)/shard_map/all_to_all | solution.py:341
  94.2 4.2 %all-to-all-start.3 = ((bf16[8,24,4,8,128]{4,3,2,1,0:T(8,128)(2,1)}), bf16[8,24,4,8,128]{4,3,2,1,0:T(8,128)(2,1)S(1)}, u32[]{:S(2)}, u32[]{:S(2)}) async-start(bf16[8,24,4,8,128]{4,3,2,1,0:T(8,128)(2,1)} %copy-done), calls=%async_computation.3 | async-start | bytes 3145728 | tf_op jit(solution)/shard_map/all_to_all | solution.py:346
  98.5 19.1 %all-to-all-done.3.got_ref = bf16[8,24,4,8,128]{4,3,2,1,0:T(8,128)(2,1)S(1)} async-done(((bf16[8,24,4,8,128]{4,3,2,1,0:T(8,128)(2,1)}), bf16[8,24,4,8,128]{4,3,2,1,0:T(8,128)(2,1)S(1)}, u32[]{:S(2)}, u32[]{:S(2)}) %all-to-all-start.3) | async-done | bytes 1572896 | tf_op jit(solution)/shard_map/all_to_all | solution.py:346
  118.3 6.6 %all-to-all-start.5 = ((f32[16,3,8,128]{3,2,1,0:T(8,128)}), f32[16,3,8,128]{3,2,1,0:T(8,128)S(1)}, u32[]{:S(2)}, u32[]{:S(2)}) async-start(f32[16,3,8,128]{3,2,1,0:T(8,128)} %broadcast_in_dim.18), calls=%async_computation.5 | async-start | bytes 393216 | tf_op jit(solution)/shard_map/all_to_all | solution.py:341
  124.9 1.8 %shard_map.125 = (bf16[32,4,8,128]{3,2,1,0:T(8,128)(2,1)}, bf16[32,4,8,128]{3,2,1,0:T(8,128)(2,1)S(1)}) custom-call(s32[192]{0:T(256)S(1)} %dynamic_slice.3.idx_ref, bf16[8,24,4,8,128]{4,3,2,1,0:T(8,128)(2,1)S(1)} %all-to-all-done.3.got_ref), custom_call_target="tpu_custom_call" | custom-call | tf_op jit(solution)/shard_map/pallas_call | solution.py:267
  126.8 4.8 %collective-permute-start.2 = (bf16[32,4,8,128]{3,2,1,0:T(8,128)(2,1)}, bf16[32,4,8,128]{3,2,1,0:T(8,128)(2,1)S(1)}, u32[]{:S(2)}, u32[]{:S(2)}) collective-permute-start(bf16[32,4,8,128]{3,2,1,0:T(8,128)(2,1)} %get-tuple-element.19), channel_id=1, source_target_pairs={{0,32},{32,0},{64,96},{96,64},{128,160},{160,128},{192,224},{224,1... | collective-permute-start | bytes 786440 | tf_op jit(solution)/shard_map/ppermute | solution.py:18
  131.5 4.3 %collective-permute-start.3 = (bf16[32,4,8,128]{3,2,1,0:T(8,128)(2,1)S(1)}, bf16[32,4,8,128]{3,2,1,0:T(8,128)(2,1)S(1)}, u32[]{:S(2)}, u32[]{:S(2)}) collective-permute-start(bf16[32,4,8,128]{3,2,1,0:T(8,128)(2,1)S(1)} %get-tuple-element.20), channel_id=1, source_target_pairs={{0,480},{32,64},{64,32},{96,128},{128,96},{160,192},{192,160},{224... | collective-permute-start | bytes 786440 | tf_op jit(solution)/shard_map/ppermute | solution.py:23
  136.9 5.2 %collective-permute-done.2.first_ref = bf16[32,4,8,128]{3,2,1,0:T(8,128)(2,1)S(1)} collective-permute-done((bf16[32,4,8,128]{3,2,1,0:T(8,128)(2,1)}, bf16[32,4,8,128]{3,2,1,0:T(8,128)(2,1)S(1)}, u32[]{:S(2)}, u32[]{:S(2)}) %collective-permute-start.2) | collective-permute-done | bytes 262176 | tf_op jit(solution)/shard_map/ppermute | solution.py:18
  143.8 19.4 %all_to_all.36.final_ref = bf16[32,6,8,128]{3,2,1,0:T(8,128)(2,1)S(1)} all-to-all(bf16[32,6,8,128]{3,2,1,0:T(8,128)(2,1)S(1)} %get-tuple-element.22), channel_id=1, replica_groups=mesh['rep'=16,'grp'=32] {'grp'}, dimensions={0} | all-to-all | bytes 786432 | tf_op jit(solution)/shard_map/all_to_all | solution.py:341
  (34 shorter events, 4.9 us)
Async XLA Ops:
  2.3 23.0 %all-to-all-start = ((bf16[32,5,8,128]{3,2,1,0:T(8,128)(2,1)}), bf16[32,5,8,128]{3,2,1,0:T(8,128)(2,1)S(1)}, u32[]{:S(2)}, u32[]{:S(2)}) async-start(bf16[32,5,8,128]{3,2,1,0:T(8,128)(2,1)} %get-tuple-element.15), calls=%async_computation | async-start | bytes 655360 | tf_op jit(solution)/shard_map/all_to_all | solution.py:341
  27.0 31.2 %all-to-all-start.1 = ((bf16[8,8,4,8,128]{4,3,2,1,0:T(8,128)(2,1)}), bf16[8,8,4,8,128]{4,3,2,1,0:T(8,128)(2,1)S(1)}, u32[]{:S(2)}, u32[]{:S(2)}) async-start(bf16[8,8,4,8,128]{4,3,2,1,0:T(8,128)(2,1)} %shard_map.121), calls=%async_computation.1 | async-start | bytes 1048576 | tf_op jit(solution)/shard_map/all_to_all | solution.py:346
  31.9 30.4 %copy-start.6 = (s32[1,3840]{1,0:T(1,128)S(1)}, s32[1,3840]{1,0:T(1,128)}, u32[]{:S(2)}) copy-start(s32[1,3840]{1,0:T(1,128)} %param.15) | copy-start | bytes 46084
  31.9 30.4 %copy-start.7 = (s32[1,3840]{1,0:T(1,128)S(1)}, s32[1,3840]{1,0:T(1,128)}, u32[]{:S(2)}) copy-start(s32[1,3840]{1,0:T(1,128)} %param.17) | copy-start | bytes 46084
  32.0 30.6 %copy-start.5 = (s32[1,3840]{1,0:T(1,128)S(1)}, s32[1,3840]{1,0:T(1,128)}, u32[]{:S(2)}) copy-start(s32[1,3840]{1,0:T(1,128)} %param.16) | copy-start | bytes 46084
  32.0 18.7 %collective-permute-start.1 = (bf16[32,4,8,128]{3,2,1,0:T(8,128)(2,1)S(1)}, bf16[32,4,8,128]{3,2,1,0:T(8,128)(2,1)S(1)}, u32[]{:S(2)}, u32[]{:S(2)}) collective-permute-start(bf16[32,4,8,128]{3,2,1,0:T(8,128)(2,1)S(1)} %slice.9.own_ref), channel_id=1, source_target_pairs={{0,480},{32,64},{64,32},{96,128},{128,96},{160,192},{192,160},{224... | collective-permute-start | bytes 786440 | tf_op jit(solution)/shard_map/ppermute | solution.py:23
  44.1 12.3 %collective-permute-start = (bf16[32,4,8,128]{3,2,1,0:T(8,128)(2,1)S(1)}, bf16[32,4,8,128]{3,2,1,0:T(8,128)(2,1)S(1)}, u32[]{:S(2)}, u32[]{:S(2)}) collective-permute-start(bf16[32,4,8,128]{3,2,1,0:T(8,128)(2,1)S(1)} %slice.9.own_ref), channel_id=1, source_target_pairs={{0,32},{32,0},{64,96},{96,64},{128,160},{160,128},{192,224},{224,1... | collective-permute-start | bytes 786440 | tf_op jit(solution)/shard_map/ppermute | solution.py:18
  58.2 17.7 %copy-start.1 = (bf16[256,256]{1,0:T(8,128)(2,1)S(1)}, bf16[256,256]{1,0:T(8,128)(2,1)}, u32[]{:S(2)}) copy-start(bf16[256,256]{1,0:T(8,128)(2,1)} %weight_ref.3) | copy-start | bytes 393220
  58.2 17.7 %copy-start.2 = (f32[128,1]{1,0:T(8,128)S(1)}, f32[128,1]{1,0:T(8,128)}, u32[]{:S(2)}) copy-start(f32[128,1]{1,0:T(8,128)} %get-tuple-element.16.dinv_ref) | copy-start | bytes 1540
  58.2 17.7 %copy-start.3 = (bf16[128,256]{1,0:T(8,128)(2,1)S(1)}, bf16[128,256]{1,0:T(8,128)(2,1)}, u32[]{:S(2)}) copy-start(bf16[128,256]{1,0:T(8,128)(2,1)} %cot_ref.1) | copy-start | bytes 196612
  58.2 17.7 %copy-start.4 = (f32[256]{0:T(256)S(1)}, f32[256]{0:T(256)}, u32[]{:S(2)}) copy-start(f32[256]{0:T(256)} %param.11) | copy-start | bytes 3076
  58.2 17.7 %all-to-all-start.2 = ((bf16[8,16,4,8,128]{4,3,2,1,0:T(8,128)(2,1)}), bf16[8,16,4,8,128]{4,3,2,1,0:T(8,128)(2,1)S(1)}, u32[]{:S(2)}, u32[]{:S(2)}) async-start(bf16[8,16,4,8,128]{4,3,2,1,0:T(8,128)(2,1)} %shard_map.122), calls=%async_computation.2 | async-start | bytes 2097152 | tf_op jit(solution)/shard_map/all_to_all | solution.py:346
  78.4 1.2 copy-start
  94.2 23.4 %all-to-all-start.3 = ((bf16[8,24,4,8,128]{4,3,2,1,0:T(8,128)(2,1)}), bf16[8,24,4,8,128]{4,3,2,1,0:T(8,128)(2,1)S(1)}, u32[]{:S(2)}, u32[]{:S(2)}) async-start(bf16[8,24,4,8,128]{4,3,2,1,0:T(8,128)(2,1)} %copy-done), calls=%async_computation.3 | async-start | bytes 3145728 | tf_op jit(solution)/shard_map/all_to_all | solution.py:346
  118.3 18.6 %all-to-all-start.5 = ((f32[16,3,8,128]{3,2,1,0:T(8,128)}), f32[16,3,8,128]{3,2,1,0:T(8,128)S(1)}, u32[]{:S(2)}, u32[]{:S(2)}) async-start(f32[16,3,8,128]{3,2,1,0:T(8,128)} %broadcast_in_dim.18), calls=%async_computation.5 | async-start | bytes 393216 | tf_op jit(solution)/shard_map/all_to_all | solution.py:341
  126.8 15.3 %collective-permute-start.2 = (bf16[32,4,8,128]{3,2,1,0:T(8,128)(2,1)}, bf16[32,4,8,128]{3,2,1,0:T(8,128)(2,1)S(1)}, u32[]{:S(2)}, u32[]{:S(2)}) collective-permute-start(bf16[32,4,8,128]{3,2,1,0:T(8,128)(2,1)} %get-tuple-element.19), channel_id=1, source_target_pairs={{0,32},{32,0},{64,96},{96,64},{128,160},{160,128},{192,224},{224,1... | collective-permute-start | bytes 786440 | tf_op jit(solution)/shard_map/ppermute | solution.py:18
  131.5 11.6 %collective-permute-start.3 = (bf16[32,4,8,128]{3,2,1,0:T(8,128)(2,1)S(1)}, bf16[32,4,8,128]{3,2,1,0:T(8,128)(2,1)S(1)}, u32[]{:S(2)}, u32[]{:S(2)}) collective-permute-start(bf16[32,4,8,128]{3,2,1,0:T(8,128)(2,1)S(1)} %get-tuple-element.20), channel_id=1, source_target_pairs={{0,480},{32,64},{64,32},{96,128},{128,96},{160,192},{192,160},{224... | collective-permute-start | bytes 786440 | tf_op jit(solution)/shard_map/ppermute | solution.py:23

commit v8 on v7

--- a/solution.py
+++ b/solution.py
@@ -167,9 +167,8 @@
     )(idx, first, second)
 
 
-def layer_kernel(listed, slab_ref, xown_ref, xfar_ref, weight_ref, dinv_ref, bias_ref, cot_ref, hid_ref, part_ref, out_ref, grad_ref, sem):
+def layer_kernel(listed, slab_ref, xown_ref, xfar_ref, weight_ref, dinv_ref, bias_ref, cot_ref, hid_ref, part_ref):
     dinv = dinv_ref[...]
-    members = grad_ref.shape[0]
     per_part = listed // 3
     tall = 2 * SUB
     edge = xown_ref.shape[0] * tall
@@ -203,43 +202,66 @@
             lanes = slice(half * LANE, (half + 1) * LANE)
             extra = jnp.where(at == 2 * index + half, value[:, lanes], extra)
     extra = extra.astype(jnp.bfloat16)
-    for q in range(members):
-        grad_ref[q, 0] = extra
-        for half in range(2):
-            block = grad[q * SUB : (q + 1) * SUB, half * LANE : (half + 1) * LANE]
-            grad_ref[q, 1 + half] = block.astype(jnp.bfloat16)
-    copy = pltpu.make_async_copy(grad_ref, out_ref, sem)
-    copy.start()
+    segments = grad.shape[0] // (SUB * SEGMENT)
     for half in range(2):
         lanes = slice(half * LANE, (half + 1) * LANE)
-        pair = pl.ds(2 * half, 2)
         partial = lax.dot_general(slab_ref[...], back[:, lanes], contract, preferred_element_type=jnp.float32)
         for holder in range(SEGMENT):
             at = holder * per_part * tall
             near = partial[at : at + per_part * tall].reshape(per_part, 2, SUB, LANE).astype(jnp.bfloat16)
             at = edge + 2 * at
             far = partial[at : at + 2 * per_part * tall].reshape(2 * per_part, 2, SUB, LANE).astype(jnp.bfloat16)
-            part_ref[holder, pl.ds(0, per_part), pair] = far[:per_part]
-            part_ref[holder, pl.ds(per_part, per_part), pair] = near
-            part_ref[holder, pl.ds(2 * per_part, per_part), pair] = far[per_part:]
-    copy.wait()
-
-
-def layer(slab, xown, xfar, weight, dinv, bias, cotangent, members, listed):
+            for t in range(per_part):
+                part_ref[holder, pl.ds(4 * t + 2 * half, 2)] = far[t]
+                part_ref[holder, pl.ds(4 * (per_part + t) + 2 * half, 2)] = near[t]
+                part_ref[holder, pl.ds(4 * (2 * per_part + t) + 2 * half, 2)] = far[per_part + t]
+            part_ref[holder, 4 * listed] = extra
+            for segment in range(segments):
+                top = (segment * SEGMENT + holder) * SUB
+                block = grad[top : top + SUB, lanes]
+                part_ref[holder, 4 * listed + 1 + 2 * segment + half] = block.astype(jnp.bfloat16)
+
+
+def layer(slab, xown, xfar, weight, dinv, bias, cotangent, listed):
     rows, width = cotangent.shape
-    grad = (members, 3, SUB, LANE)
+    pieces = 4 * listed + 1 + 2 * (width // (SUB * SEGMENT))
     return call(
         functools.partial(layer_kernel, listed),
         16,
         (
             jax.ShapeDtypeStruct((rows, width), jnp.bfloat16),
-            jax.ShapeDtypeStruct((SEGMENT, listed, 4, SUB, LANE), jnp.bfloat16),
-            jax.ShapeDtypeStruct(grad, jnp.bfloat16),
+            jax.ShapeDtypeStruct((SEGMENT, pieces, SUB, LANE), jnp.bfloat16),
         ),
         [vmem()] * 7,
-        (vmem(), vmem(), hbm()),
-        [pltpu.VMEM(grad, jnp.bfloat16), pltpu.SemaphoreType.DMA],
+        (vmem(), vmem()),
     )(slab, xown, xfar, weight, dinv, bias, cotangent)
+
+
+def fold_kernel(got_ref, out_ref, made_ref, sem):
+    segments = made_ref.shape[0]
+    first = got_ref.shape[1] - 1 - 2 * segments
+    total = got_ref[0, pl.ds(first, 1 + 2 * segments)].astype(jnp.float32)
+    for d in range(1, got_ref.shape[0]):
+        total = total + got_ref[d, pl.ds(first, 1 + 2 * segments)].astype(jnp.float32)
+    for segment in range(segments):
+        made_ref[segment, 0] = total[0]
+        made_ref[segment, 1] = total[1 + 2 * segment]
+        made_ref[segment, 2] = total[2 + 2 * segment]
+    copy = pltpu.make_async_copy(made_ref, out_ref, sem)
+    copy.start()
+    copy.wait()
+
+
+def fold(got, segments):
+    shape = (segments, 3, SUB, LANE)
+    return call(
+        fold_kernel,
+        4,
+        jax.ShapeDtypeStruct(shape, jnp.float32),
+        [vmem()],
+        hbm(),
+        [pltpu.VMEM(shape, jnp.float32), pltpu.SemaphoreType.DMA],
+    )(got)
 
 
 def collect_kernel(members, per_part, parts, chains, idx_ref, got_ref, *refs):
@@ -252,7 +274,7 @@
                 for j in range(chains):
                     d = step * chains + j
                     at = jnp.bitwise_and(idx_ref[d * 3 * per_part + t], tiles - 1)
-                    acc_ref[j, at] += got_ref[d, t].astype(jnp.float32)
+                    acc_ref[j, at] += got_ref[d, pl.ds(4 * t, 4)].astype(jnp.float32)
     for number, ref in enumerate(outs):
         part = pl.ds(number * members, members)
         value = acc_ref[0, part]
@@ -263,14 +285,14 @@
 
 def collect(idx, parts, got, members, per_part, dtype):
     chains = 2
-    piece = (members,) + got.shape[2:]
+    piece = (members, 4, SUB, LANE)
     return call(
         functools.partial(collect_kernel, members, per_part, parts, chains),
         8,
         tuple(jax.ShapeDtypeStruct(piece, dtype) for _ in parts),
         [smem(), vmem()],
         (vmem(),) * len(parts),
-        [pltpu.VMEM((chains, len(parts) * members) + got.shape[2:], jnp.float32)],
+        [pltpu.VMEM((chains, len(parts) * members, 4, SUB, LANE), jnp.float32)],
     )(idx, got)
 
 
@@ -346,6 +368,11 @@
     return lax.all_to_all(x, "grp", 0, 0, axis_index_groups=groups, tiled=True)
 
 
+def across_swap(x, members):
+    groups = [list(range(first, members, SEGMENT)) for first in range(SEGMENT)]
+    return lax.all_to_all(x, "grp", 0, 0, axis_index_groups=groups, tiled=True)
+
+
 def per_device(features, weight, bias, cotangent, degree, tile_cols, edge_tile, edge_row, edge_col):
     rows, _ = features.shape
     members = lax.axis_size("grp")
@@ -381,7 +408,7 @@
     chosen_own = select_own(near_idx, own, per_part)
     window_own = segment_swap(chosen_own, members)
     window_far = segment_swap(select_far(near_idx, first, second, per_part), members)
-    hidden, partial, grad = layer(
+    hidden, partial = layer(
         slab,
         window_own.reshape(rows // tall * per_part, 2, tall, LANE),
         window_far.reshape(rows // tall * 2 * per_part, 2, tall, LANE),
@@ -389,12 +416,11 @@
         dinv,
         bias[None, :],
         cotangent,
-        members,
         listed,
     )
     mine = segment_swap(partial, members)
-    grad = swap(grad, "grp")
-    share = grad.astype(jnp.float32).sum(axis=0)
+    grad = across_swap(fold(mine, members // SEGMENT), members)
+    share = grad.sum(axis=0)
     share = swap(jnp.broadcast_to(share[None], (rings, 3, SUB, LANE)), "rep")
     to_first, to_second = collect(near_idx, (0, 2), mine, members, per_part, jnp.bfloat16)
     from_first = with_partner(to_first, "rep")

time: 165 us -> 159 us (0.964)
  blocking collectives: 34 us -> 54.8 us
  waiting for transfers between devices: 58.2 us -> 38.3 us
  starting transfers between devices: 53.4 us -> 49.2 us
    all_to_all x0 -> x2, blocking collectives: none -> 34.2 us  [the longest x1 25 us: segment_swap(): return lax.all_to_all(x, 'grp', 0, 0, axis_index_groups=groups, tiled=True)]
    all_to_all x3 -> x2, waiting for transfers between devices: 29 us -> 9.9 us  [segment_swap(): return lax.all_to_all(x, 'grp', 0, 0, axis_index_groups=groups, tiled=True)]
    all_to_all x2 -> x1, blocking collectives: 34 us -> 20.6 us  [swap(): return lax.all_to_all(x, axis, 0, 0, tiled=True)]
    all_to_all x3 -> x2, starting transfers between devices: 13.3 us -> 9.05 us  [segment_swap(): return lax.all_to_all(x, 'grp', 0, 0, axis_index_groups=groups, tiled=True)]
  transfers between devices with their start and end apart: 9 -> 8, of which waited for: 7 -> 6; matrix products, arithmetic and copies ran while one was open for 0% -> 0% of each run, Pallas kernels for 5% -> 5%
where the time goes in v8:
time: 159 us; the launch traced here: 158 us
  blocking collectives  54.8 us (34%)
  starting transfers between devices  49.2 us (31%)
  waiting for transfers between devices  38.3 us (24%)
  Pallas kernels  13.5 us (8%)
    all_to_all x1, blocking collectives, segment_swap(): return lax.all_to_all(x, 'grp', 0, 0, axis_index_groups=groups, tiled=True)  25 us
    all_to_all x1, blocking collectives, swap(): return lax.all_to_all(x, axis, 0, 0, tiled=True)  20.6 us
    all_to_all x2, starting transfers between devices, swap(): return lax.all_to_all(x, axis, 0, 0, tiled=True)  17 us
    ppermute x2, starting transfers between devices, with_other(): lax.ppermute(x, axis, [(i, (i + 1 if i % 2 else i - 1) % size) for i in r...  16.5 us
    all_to_all x2, waiting for transfers between devices, swap(): return lax.all_to_all(x, axis, 0, 0, tiled=True)  12.5 us
    ppermute x2, waiting for transfers between devices, with_partner(): lax.ppermute(x, axis, [(i, i ^ 1) for i in range(lax.axis_size(axis))])  10.2 us
    all_to_all x2, waiting for transfers between devices, segment_swap(): return lax.all_to_all(x, 'grp', 0, 0, axis_index_groups=groups, tiled=True)  9.9 us
    all_to_all x1, blocking collectives, across_swap(): return lax.all_to_all(x, 'grp', 0, 0, axis_index_groups=groups, tiled=True)  9.2 us
  transfers between devices with their start and end apart: 8, of which 6 were waited for; matrix products, arithmetic and copies ran while one was open for 0% of the time, Pallas kernels for 5%

profile of v8, /device:TPU:1, one launch (start us, length us, event | category | flops | bytes accessed | tf_op | source)
XLA Modules:
  0.0 158.0 jit_solution(15028672547072465166)
XLA Ops:
  0.6 1.7 %shard_map.120 = (bf16[32,5,8,128]{3,2,1,0:T(8,128)(2,1)}, f32[128,1]{1,0:T(8,128)}) custom-call(bf16[128,256]{1,0:T(8,128)(2,1)} %x_ref.1, s32[1,128]{1,0:T(1,128)} %bitcast.8, s32[1,24]{1,0:T(1,128)} %cols_ref.1), custom_call_target="tpu_custom_call" | custom-call | tf_op jit(solution)/shard_map/pallas_call | solution.py:74
  2.4 10.4 %all-to-all-start = ((bf16[32,5,8,128]{3,2,1,0:T(8,128)(2,1)}), bf16[32,5,8,128]{3,2,1,0:T(8,128)(2,1)S(1)}, u32[]{:S(2)}, u32[]{:S(2)}) async-start(bf16[32,5,8,128]{3,2,1,0:T(8,128)(2,1)} %get-tuple-element.14), calls=%async_computation | async-start | bytes 655360 | tf_op jit(solution)/shard_map/all_to_all | solution.py:363
  12.9 12.5 %all-to-all-done = bf16[32,5,8,128]{3,2,1,0:T(8,128)(2,1)S(1)} async-done(((bf16[32,5,8,128]{3,2,1,0:T(8,128)(2,1)}), bf16[32,5,8,128]{3,2,1,0:T(8,128)(2,1)S(1)}, u32[]{:S(2)}, u32[]{:S(2)}) %all-to-all-start) | async-done | bytes 327712 | tf_op jit(solution)/shard_map/all_to_all | solution.py:363
  25.6 1.4 shard_map.121
  27.1 4.9 %all-to-all-start.1 = ((bf16[8,8,4,8,128]{4,3,2,1,0:T(8,128)(2,1)}), bf16[8,8,4,8,128]{4,3,2,1,0:T(8,128)(2,1)S(1)}, u32[]{:S(2)}, u32[]{:S(2)}) async-start(bf16[8,8,4,8,128]{4,3,2,1,0:T(8,128)(2,1)} %shard_map.121), calls=%async_computation.1 | async-start | bytes 1048576 | tf_op jit(solution)/shard_map/all_to_all | solution.py:368
  32.0 12.2 %collective-permute-start.1 = (bf16[32,4,8,128]{3,2,1,0:T(8,128)(2,1)S(1)}, bf16[32,4,8,128]{3,2,1,0:T(8,128)(2,1)S(1)}, u32[]{:S(2)}, u32[]{:S(2)}) collective-permute-start(bf16[32,4,8,128]{3,2,1,0:T(8,128)(2,1)S(1)} %slice.9.own_ref), channel_id=1, source_target_pairs={{0,480},{32,64},{64,32},{96,128},{128,96},{160,192},{192,160},{224... | collective-permute-start | bytes 786440 | tf_op jit(solution)/shard_map/ppermute | solution.py:23
  44.2 1.9 %collective-permute-start = (bf16[32,4,8,128]{3,2,1,0:T(8,128)(2,1)S(1)}, bf16[32,4,8,128]{3,2,1,0:T(8,128)(2,1)S(1)}, u32[]{:S(2)}, u32[]{:S(2)}) collective-permute-start(bf16[32,4,8,128]{3,2,1,0:T(8,128)(2,1)S(1)} %slice.9.own_ref), channel_id=1, source_target_pairs={{0,32},{32,0},{64,96},{96,64},{128,160},{160,128},{192,224},{224,1... | collective-permute-start | bytes 786440 | tf_op jit(solution)/shard_map/ppermute | solution.py:18
  46.1 4.6 %collective-permute-done.1.second_ref = bf16[32,4,8,128]{3,2,1,0:T(8,128)(2,1)S(1)} collective-permute-done((bf16[32,4,8,128]{3,2,1,0:T(8,128)(2,1)S(1)}, bf16[32,4,8,128]{3,2,1,0:T(8,128)(2,1)S(1)}, u32[]{:S(2)}, u32[]{:S(2)}) %collective-permute-start.1) | collective-permute-done | bytes 262176 | tf_op jit(solution)/shard_map/ppermute | solution.py:23
  50.7 5.8 %collective-permute-done.first_ref = bf16[32,4,8,128]{3,2,1,0:T(8,128)(2,1)S(1)} collective-permute-done((bf16[32,4,8,128]{3,2,1,0:T(8,128)(2,1)S(1)}, bf16[32,4,8,128]{3,2,1,0:T(8,128)(2,1)S(1)}, u32[]{:S(2)}, u32[]{:S(2)}) %collective-permute-start) | collective-permute-done | bytes 262176 | tf_op jit(solution)/shard_map/ppermute | solution.py:18
  56.5 1.7 %shard_map.122 = bf16[8,16,4,8,128]{4,3,2,1,0:T(8,128)(2,1)} custom-call(s32[192]{0:T(256)S(1)} %dynamic_slice.3.idx_ref, bf16[32,4,8,128]{3,2,1,0:T(8,128)(2,1)S(1)} %collective-permute-done.first_ref, bf16[32,4,8,128]{3,2,1,0:T(8,128)(2,1)S(1)} %collective-permute-done.1.second_ref), custom_call_target="tpu_custom_call" | custom-call | tf_op jit(solution)/shard_map/pallas_call | solution.py:160
  58.2 4.1 %all-to-all-start.2 = ((bf16[8,16,4,8,128]{4,3,2,1,0:T(8,128)(2,1)}), bf16[8,16,4,8,128]{4,3,2,1,0:T(8,128)(2,1)S(1)}, u32[]{:S(2)}, u32[]{:S(2)}) async-start(bf16[8,16,4,8,128]{4,3,2,1,0:T(8,128)(2,1)} %shard_map.122), calls=%async_computation.2 | async-start | bytes 2097152 | tf_op jit(solution)/shard_map/all_to_all | solution.py:368
  62.7 3.3 %count.1.slab_ref = bf16[128,3072]{1,0:T(8,128)(2,1)S(1)} custom-call(s32[1,3840]{1,0:T(1,128)S(1)} %multiply_add_fusion.xk_ref, s32[1,3840]{1,0:T(1,128)S(1)} %get-tuple-element.24.yk_ref), custom_call_target="tpu_custom_call" | custom-call | tf_op jit(solution)/shard_map/count/pallas_call | solution.py:113
  66.0 9.9 %all-to-all-done.2 = bf16[8,16,4,8,128]{4,3,2,1,0:T(8,128)(2,1)S(1)} async-done(((bf16[8,16,4,8,128]{4,3,2,1,0:T(8,128)(2,1)}), bf16[8,16,4,8,128]{4,3,2,1,0:T(8,128)(2,1)S(1)}, u32[]{:S(2)}, u32[]{:S(2)}) %all-to-all-start.2) | async-done | bytes 1048608 | tf_op jit(solution)/shard_map/all_to_all | solution.py:368
  75.9 1.5 shard_map.123
  77.4 25.0 %all_to_all.35.got_ref = bf16[8,105,8,128]{3,2,1,0:T(8,128)(2,1)S(1)} all-to-all(bf16[8,105,8,128]{3,2,1,0:T(8,128)(2,1)S(1)} %get-tuple-element.17), channel_id=1, replica_groups={{0,1,2,3,4,5,6,7},{8,9,10,11,12,13,14,15},{16,17,18,19,20,21,22,23},{24..., dimensions={0} | all-to-all | bytes 3440640 | tf_op jit(solution)/shard_map/all_to_all | solution.py:368
  102.5 9.2 %all_to_all.36 = f32[4,3,8,128]{3,2,1,0:T(8,128)S(1)} all-to-all(f32[4,3,8,128]{3,2,1,0:T(8,128)S(1)} %shard_map.126), channel_id=1, replica_groups={{0,8,16,24},{1,9,17,25},{2,10,18,26},{3,11,19,27},{4,12,20,28},{5,13,21..., dimensions={0} | all-to-all | bytes 98304 | tf_op jit(solution)/shard_map/all_to_all | solution.py:373
  112.4 6.6 %all-to-all-start.5 = ((f32[16,3,8,128]{3,2,1,0:T(8,128)}), f32[16,3,8,128]{3,2,1,0:T(8,128)S(1)}, u32[]{:S(2)}, u32[]{:S(2)}) async-start(f32[16,3,8,128]{3,2,1,0:T(8,128)} %broadcast_in_dim.18), calls=%async_computation.5 | async-start | bytes 393216 | tf_op jit(solution)/shard_map/all_to_all | solution.py:363
  119.0 1.3 shard_map.125
  120.3 4.8 %collective-permute-start.2 = (bf16[32,4,8,128]{3,2,1,0:T(8,128)(2,1)S(1)}, bf16[32,4,8,128]{3,2,1,0:T(8,128)(2,1)S(1)}, u32[]{:S(2)}, u32[]{:S(2)}) collective-permute-start(bf16[32,4,8,128]{3,2,1,0:T(8,128)(2,1)S(1)} %get-tuple-element.18), channel_id=1, source_target_pairs={{0,32},{32,0},{64,96},{96,64},{128,160},{160,128},{192,224},{224,1... | collective-permute-start | bytes 786440 | tf_op jit(solution)/shard_map/ppermute | solution.py:18
  125.1 4.3 %collective-permute-start.3 = (bf16[32,4,8,128]{3,2,1,0:T(8,128)(2,1)S(1)}, bf16[32,4,8,128]{3,2,1,0:T(8,128)(2,1)S(1)}, u32[]{:S(2)}, u32[]{:S(2)}) collective-permute-start(bf16[32,4,8,128]{3,2,1,0:T(8,128)(2,1)S(1)} %get-tuple-element.19), channel_id=1, source_target_pairs={{0,480},{32,64},{64,32},{96,128},{128,96},{160,192},{192,160},{224... | collective-permute-start | bytes 786440 | tf_op jit(solution)/shard_map/ppermute | solution.py:23
  129.4 1.0 shard_map.124.own_ref
  130.4 4.4 %collective-permute-done.2.first_ref = bf16[32,4,8,128]{3,2,1,0:T(8,128)(2,1)S(1)} collective-permute-done((bf16[32,4,8,128]{3,2,1,0:T(8,128)(2,1)S(1)}, bf16[32,4,8,128]{3,2,1,0:T(8,128)(2,1)S(1)}, u32[]{:S(2)}, u32[]{:S(2)}) %collective-permute-start.2) | collective-permute-done | bytes 262176 | tf_op jit(solution)/shard_map/ppermute | solution.py:18
  134.8 1.1 collective-permute-done.3.second_ref
  136.5 20.6 %all_to_all.37.final_ref = bf16[32,6,8,128]{3,2,1,0:T(8,128)(2,1)S(1)} all-to-all(bf16[32,6,8,128]{3,2,1,0:T(8,128)(2,1)S(1)} %get-tuple-element.20), channel_id=1, replica_groups=mesh['rep'=16,'grp'=32] {'grp'}, dimensions={0} | all-to-all | bytes 786432 | tf_op jit(solution)/shard_map/all_to_all | solution.py:363
  (32 shorter events, 2.9 us)
Async XLA Ops:
  2.4 23.0 %all-to-all-start = ((bf16[32,5,8,128]{3,2,1,0:T(8,128)(2,1)}), bf16[32,5,8,128]{3,2,1,0:T(8,128)(2,1)S(1)}, u32[]{:S(2)}, u32[]{:S(2)}) async-start(bf16[32,5,8,128]{3,2,1,0:T(8,128)(2,1)} %get-tuple-element.14), calls=%async_computation | async-start | bytes 655360 | tf_op jit(solution)/shard_map/all_to_all | solution.py:363
  27.1 31.2 %all-to-all-start.1 = ((bf16[8,8,4,8,128]{4,3,2,1,0:T(8,128)(2,1)}), bf16[8,8,4,8,128]{4,3,2,1,0:T(8,128)(2,1)S(1)}, u32[]{:S(2)}, u32[]{:S(2)}) async-start(bf16[8,8,4,8,128]{4,3,2,1,0:T(8,128)(2,1)} %shard_map.121), calls=%async_computation.1 | async-start | bytes 1048576 | tf_op jit(solution)/shard_map/all_to_all | solution.py:368
  32.0 30.4 %copy-start.5 = (s32[1,3840]{1,0:T(1,128)S(1)}, s32[1,3840]{1,0:T(1,128)}, u32[]{:S(2)}) copy-start(s32[1,3840]{1,0:T(1,128)} %param.15) | copy-start | bytes 46084
  32.0 30.4 %copy-start.6 = (s32[1,3840]{1,0:T(1,128)S(1)}, s32[1,3840]{1,0:T(1,128)}, u32[]{:S(2)}) copy-start(s32[1,3840]{1,0:T(1,128)} %param.17) | copy-start | bytes 46084
  32.0 30.6 %copy-start.4 = (s32[1,3840]{1,0:T(1,128)S(1)}, s32[1,3840]{1,0:T(1,128)}, u32[]{:S(2)}) copy-start(s32[1,3840]{1,0:T(1,128)} %param.16) | copy-start | bytes 46084
  32.0 18.7 %collective-permute-start.1 = (bf16[32,4,8,128]{3,2,1,0:T(8,128)(2,1)S(1)}, bf16[32,4,8,128]{3,2,1,0:T(8,128)(2,1)S(1)}, u32[]{:S(2)}, u32[]{:S(2)}) collective-permute-start(bf16[32,4,8,128]{3,2,1,0:T(8,128)(2,1)S(1)} %slice.9.own_ref), channel_id=1, source_target_pairs={{0,480},{32,64},{64,32},{96,128},{128,96},{160,192},{192,160},{224... | collective-permute-start | bytes 786440 | tf_op jit(solution)/shard_map/ppermute | solution.py:23
  44.2 12.3 %collective-permute-start = (bf16[32,4,8,128]{3,2,1,0:T(8,128)(2,1)S(1)}, bf16[32,4,8,128]{3,2,1,0:T(8,128)(2,1)S(1)}, u32[]{:S(2)}, u32[]{:S(2)}) collective-permute-start(bf16[32,4,8,128]{3,2,1,0:T(8,128)(2,1)S(1)} %slice.9.own_ref), channel_id=1, source_target_pairs={{0,32},{32,0},{64,96},{96,64},{128,160},{160,128},{192,224},{224,1... | collective-permute-start | bytes 786440 | tf_op jit(solution)/shard_map/ppermute | solution.py:18
  58.2 17.7 %copy-start = (bf16[256,256]{1,0:T(8,128)(2,1)S(1)}, bf16[256,256]{1,0:T(8,128)(2,1)}, u32[]{:S(2)}) copy-start(bf16[256,256]{1,0:T(8,128)(2,1)} %weight_ref.3) | copy-start | bytes 393220
  58.2 17.7 %copy-start.1 = (f32[128,1]{1,0:T(8,128)S(1)}, f32[128,1]{1,0:T(8,128)}, u32[]{:S(2)}) copy-start(f32[128,1]{1,0:T(8,128)} %get-tuple-element.15.dinv_ref) | copy-start | bytes 1540
  58.2 17.7 %copy-start.2 = (bf16[128,256]{1,0:T(8,128)(2,1)S(1)}, bf16[128,256]{1,0:T(8,128)(2,1)}, u32[]{:S(2)}) copy-start(bf16[128,256]{1,0:T(8,128)(2,1)} %cot_ref.1) | copy-start | bytes 196612
  58.2 17.7 %copy-start.3 = (f32[256]{0:T(256)S(1)}, f32[256]{0:T(256)}, u32[]{:S(2)}) copy-start(f32[256]{0:T(256)} %param.11) | copy-start | bytes 3076
  58.2 17.7 %all-to-all-start.2 = ((bf16[8,16,4,8,128]{4,3,2,1,0:T(8,128)(2,1)}), bf16[8,16,4,8,128]{4,3,2,1,0:T(8,128)(2,1)S(1)}, u32[]{:S(2)}, u32[]{:S(2)}) async-start(bf16[8,16,4,8,128]{4,3,2,1,0:T(8,128)(2,1)} %shard_map.122), calls=%async_computation.2 | async-start | bytes 2097152 | tf_op jit(solution)/shard_map/all_to_all | solution.py:368
  112.4 23.6 %all-to-all-start.5 = ((f32[16,3,8,128]{3,2,1,0:T(8,128)}), f32[16,3,8,128]{3,2,1,0:T(8,128)S(1)}, u32[]{:S(2)}, u32[]{:S(2)}) async-start(f32[16,3,8,128]{3,2,1,0:T(8,128)} %broadcast_in_dim.18), calls=%async_computation.5 | async-start | bytes 393216 | tf_op jit(solution)/shard_map/all_to_all | solution.py:363
  120.3 14.5 %collective-permute-start.2 = (bf16[32,4,8,128]{3,2,1,0:T(8,128)(2,1)S(1)}, bf16[32,4,8,128]{3,2,1,0:T(8,128)(2,1)S(1)}, u32[]{:S(2)}, u32[]{:S(2)}) collective-permute-start(bf16[32,4,8,128]{3,2,1,0:T(8,128)(2,1)S(1)} %get-tuple-element.18), channel_id=1, source_target_pairs={{0,32},{32,0},{64,96},{96,64},{128,160},{160,128},{192,224},{224,1... | collective-permute-start | bytes 786440 | tf_op jit(solution)/shard_map/ppermute | solution.py:18
  125.1 10.8 %collective-permute-start.3 = (bf16[32,4,8,128]{3,2,1,0:T(8,128)(2,1)S(1)}, bf16[32,4,8,128]{3,2,1,0:T(8,128)(2,1)S(1)}, u32[]{:S(2)}, u32[]{:S(2)}) collective-permute-start(bf16[32,4,8,128]{3,2,1,0:T(8,128)(2,1)S(1)} %get-tuple-element.19), channel_id=1, source_target_pairs={{0,480},{32,64},{64,32},{96,128},{128,96},{160,192},{192,160},{224... | collective-permute-start | bytes 786440 | tf_op jit(solution)/shard_map/ppermute | solution.py:23

commit v9 on v8

--- a/solution.py
+++ b/solution.py
@@ -264,6 +264,39 @@
     )(got)
 
 
+def spread_kernel(got_ref, out_ref, made_ref, sem):
+    total = got_ref[0]
+    for segment in range(1, got_ref.shape[0]):
+        total = total + got_ref[segment]
+    top = total[0, 0:2] + total[0, 2:4]
+    high = top.astype(jnp.bfloat16).astype(jnp.float32)
+    low = top - high
+    at = lax.broadcasted_iota(jnp.int32, (SUB, LANE), 0)
+    piece = jnp.zeros((SUB, LANE), jnp.float32)
+    for index in range(2):
+        piece = jnp.where(at == index, high[index : index + 1], piece)
+        piece = jnp.where(at == 2 + index, low[index : index + 1], piece)
+    pieces = [piece.astype(jnp.bfloat16), total[1].astype(jnp.bfloat16), total[2].astype(jnp.bfloat16)]
+    for ring in range(made_ref.shape[0]):
+        for number, value in enumerate(pieces):
+            made_ref[ring, number] = value
+    copy = pltpu.make_async_copy(made_ref, out_ref, sem)
+    copy.start()
+    copy.wait()
+
+
+def spread(got, rings):
+    shape = (rings, 3, SUB, LANE)
+    return call(
+        spread_kernel,
+        4,
+        jax.ShapeDtypeStruct(shape, jnp.bfloat16),
+        [vmem()],
+        hbm(),
+        [pltpu.VMEM(shape, jnp.bfloat16), pltpu.SemaphoreType.DMA],
+    )(got)
+
+
 def collect_kernel(members, per_part, parts, chains, idx_ref, got_ref, *refs):
     outs, acc_ref = refs[:-1], refs[-1]
     acc_ref[...] = jnp.zeros_like(acc_ref)
@@ -298,9 +331,9 @@
 
 def join_kernel(own_ref, first_ref, second_ref, share_ref, out_ref, bias_ref):
     members = own_ref.shape[0]
-    total = share_ref[0]
+    total = share_ref[0].astype(jnp.float32)
     for ring in range(1, share_ref.shape[0]):
-        total = total + share_ref[ring]
+        total = total + share_ref[ring].astype(jnp.float32)
     for half in range(2):
         bias_ref[:, half * LANE : (half + 1) * LANE] = total[0, half : half + 1] + total[0, half + 2 : half + 3]
     rows = [total[1].astype(jnp.bfloat16), total[2].astype(jnp.bfloat16)]
@@ -420,8 +453,8 @@
     )
     mine = segment_swap(partial, members)
     grad = across_swap(fold(mine, members // SEGMENT), members)
-    share = grad.sum(axis=0)
-    share = swap(jnp.broadcast_to(share[None], (rings, 3, SUB, LANE)), "rep")
+    share = spread(grad, rings)
+    share = swap(share, "rep")
     to_first, to_second = collect(near_idx, (0, 2), mine, members, per_part, jnp.bfloat16)
     from_first = with_partner(to_first, "rep")
     from_second = with_other(to_second, "rep")

time: 159 us -> 161 us (1.013)
  waiting for transfers between devices: 38.3 us -> 41.6 us
    all_to_all x2, waiting for transfers between devices: 12.5 us -> 21.3 us  [swap(): return lax.all_to_all(x, axis, 0, 0, tiled=True)]
    ppermute x2, waiting for transfers between devices: 10.2 us -> 5.8 us  [with_partner(): lax.ppermute(x, axis, [(i, i ^ 1) for i in range(lax.axis_size(axis))])]
    ppermute x2, starting transfers between devices: 16.5 us -> 20.8 us  [with_other(): lax.ppermute(x, axis, [(i, (i + 1 if i % 2 else i - 1) % size) for i in r...]
    ppermute x2, starting transfers between devices: 6.7 us -> 3.83 us  [with_partner(): lax.ppermute(x, axis, [(i, i ^ 1) for i in range(lax.axis_size(axis))])]
    all_to_all x2, starting transfers between devices: 17 us -> 14.1 us  [swap(): return lax.all_to_all(x, axis, 0, 0, tiled=True)]
  transfers between devices with their start and end apart: 8 -> 8, of which waited for: 6 -> 5; matrix products, arithmetic and copies ran while one was open for 0% -> 0% of each run, Pallas kernels for 5% -> 4%
where the time goes in v9:
time: 161 us; the launch traced here: 160 us
  blocking collectives  54.8 us (34%)
  starting transfers between devices  47.8 us (30%)
  waiting for transfers between devices  41.6 us (26%)
  Pallas kernels  14.8 us (9%)
    all_to_all x1, blocking collectives, segment_swap(): return lax.all_to_all(x, 'grp', 0, 0, axis_index_groups=groups, tiled=True)  25 us
    all_to_all x2, waiting for transfers between devices, swap(): return lax.all_to_all(x, axis, 0, 0, tiled=True)  21.3 us
    ppermute x2, starting transfers between devices, with_other(): lax.ppermute(x, axis, [(i, (i + 1 if i % 2 else i - 1) % size) for i in r...  20.8 us
    all_to_all x1, blocking collectives, swap(): return lax.all_to_all(x, axis, 0, 0, tiled=True)  20.5 us
    all_to_all x2, starting transfers between devices, swap(): return lax.all_to_all(x, axis, 0, 0, tiled=True)  14.1 us
    all_to_all x2, waiting for transfers between devices, segment_swap(): return lax.all_to_all(x, 'grp', 0, 0, axis_index_groups=groups, tiled=True)  9.9 us
    all_to_all x1, blocking collectives, across_swap(): return lax.all_to_all(x, 'grp', 0, 0, axis_index_groups=groups, tiled=True)  9.28 us
    all_to_all x2, starting transfers between devices, segment_swap(): return lax.all_to_all(x, 'grp', 0, 0, axis_index_groups=groups, tiled=True)  9.05 us
  transfers between devices with their start and end apart: 8, of which 5 were waited for; matrix products, arithmetic and copies ran while one was open for 0% of the time, Pallas kernels for 4%

profile of v9, /device:TPU:1, one launch (start us, length us, event | category | flops | bytes accessed | tf_op | source)
XLA Modules:
  0.0 160.4 jit_solution(2149516651087237896)
XLA Ops:
  0.6 1.7 %shard_map.120 = (bf16[32,5,8,128]{3,2,1,0:T(8,128)(2,1)}, f32[128,1]{1,0:T(8,128)}) custom-call(bf16[128,256]{1,0:T(8,128)(2,1)} %x_ref.1, s32[1,128]{1,0:T(1,128)} %bitcast.8, s32[1,24]{1,0:T(1,128)} %cols_ref.1), custom_call_target="tpu_custom_call" | custom-call | tf_op jit(solution)/shard_map/pallas_call | solution.py:74
  2.3 10.4 %all-to-all-start = ((bf16[32,5,8,128]{3,2,1,0:T(8,128)(2,1)}), bf16[32,5,8,128]{3,2,1,0:T(8,128)(2,1)S(1)}, u32[]{:S(2)}, u32[]{:S(2)}) async-start(bf16[32,5,8,128]{3,2,1,0:T(8,128)(2,1)} %get-tuple-element.14), calls=%async_computation | async-start | bytes 655360 | tf_op jit(solution)/shard_map/all_to_all | solution.py:396
  12.9 12.5 %all-to-all-done = bf16[32,5,8,128]{3,2,1,0:T(8,128)(2,1)S(1)} async-done(((bf16[32,5,8,128]{3,2,1,0:T(8,128)(2,1)}), bf16[32,5,8,128]{3,2,1,0:T(8,128)(2,1)S(1)}, u32[]{:S(2)}, u32[]{:S(2)}) %all-to-all-start) | async-done | bytes 327712 | tf_op jit(solution)/shard_map/all_to_all | solution.py:396
  25.6 1.4 shard_map.121
  27.0 4.9 %all-to-all-start.1 = ((bf16[8,8,4,8,128]{4,3,2,1,0:T(8,128)(2,1)}), bf16[8,8,4,8,128]{4,3,2,1,0:T(8,128)(2,1)S(1)}, u32[]{:S(2)}, u32[]{:S(2)}) async-start(bf16[8,8,4,8,128]{4,3,2,1,0:T(8,128)(2,1)} %shard_map.121), calls=%async_computation.1 | async-start | bytes 1048576 | tf_op jit(solution)/shard_map/all_to_all | solution.py:401
  32.0 12.2 %collective-permute-start.1 = (bf16[32,4,8,128]{3,2,1,0:T(8,128)(2,1)S(1)}, bf16[32,4,8,128]{3,2,1,0:T(8,128)(2,1)S(1)}, u32[]{:S(2)}, u32[]{:S(2)}) collective-permute-start(bf16[32,4,8,128]{3,2,1,0:T(8,128)(2,1)S(1)} %slice.9.own_ref), channel_id=1, source_target_pairs={{0,480},{32,64},{64,32},{96,128},{128,96},{160,192},{192,160},{224... | collective-permute-start | bytes 786440 | tf_op jit(solution)/shard_map/ppermute | solution.py:23
  44.1 1.9 %collective-permute-start = (bf16[32,4,8,128]{3,2,1,0:T(8,128)(2,1)S(1)}, bf16[32,4,8,128]{3,2,1,0:T(8,128)(2,1)S(1)}, u32[]{:S(2)}, u32[]{:S(2)}) collective-permute-start(bf16[32,4,8,128]{3,2,1,0:T(8,128)(2,1)S(1)} %slice.9.own_ref), channel_id=1, source_target_pairs={{0,32},{32,0},{64,96},{96,64},{128,160},{160,128},{192,224},{224,1... | collective-permute-start | bytes 786440 | tf_op jit(solution)/shard_map/ppermute | solution.py:18
  46.1 4.6 %collective-permute-done.1.second_ref = bf16[32,4,8,128]{3,2,1,0:T(8,128)(2,1)S(1)} collective-permute-done((bf16[32,4,8,128]{3,2,1,0:T(8,128)(2,1)S(1)}, bf16[32,4,8,128]{3,2,1,0:T(8,128)(2,1)S(1)}, u32[]{:S(2)}, u32[]{:S(2)}) %collective-permute-start.1) | collective-permute-done | bytes 262176 | tf_op jit(solution)/shard_map/ppermute | solution.py:23
  50.7 5.8 %collective-permute-done.first_ref = bf16[32,4,8,128]{3,2,1,0:T(8,128)(2,1)S(1)} collective-permute-done((bf16[32,4,8,128]{3,2,1,0:T(8,128)(2,1)S(1)}, bf16[32,4,8,128]{3,2,1,0:T(8,128)(2,1)S(1)}, u32[]{:S(2)}, u32[]{:S(2)}) %collective-permute-start) | collective-permute-done | bytes 262176 | tf_op jit(solution)/shard_map/ppermute | solution.py:18
  56.5 1.7 %shard_map.122 = bf16[8,16,4,8,128]{4,3,2,1,0:T(8,128)(2,1)} custom-call(s32[192]{0:T(256)S(1)} %dynamic_slice.3.idx_ref, bf16[32,4,8,128]{3,2,1,0:T(8,128)(2,1)S(1)} %collective-permute-done.first_ref, bf16[32,4,8,128]{3,2,1,0:T(8,128)(2,1)S(1)} %collective-permute-done.1.second_ref), custom_call_target="tpu_custom_call" | custom-call | tf_op jit(solution)/shard_map/pallas_call | solution.py:160
  58.2 4.1 %all-to-all-start.2 = ((bf16[8,16,4,8,128]{4,3,2,1,0:T(8,128)(2,1)}), bf16[8,16,4,8,128]{4,3,2,1,0:T(8,128)(2,1)S(1)}, u32[]{:S(2)}, u32[]{:S(2)}) async-start(bf16[8,16,4,8,128]{4,3,2,1,0:T(8,128)(2,1)} %shard_map.122), calls=%async_computation.2 | async-start | bytes 2097152 | tf_op jit(solution)/shard_map/all_to_all | solution.py:401
  62.7 3.3 %count.1.slab_ref = bf16[128,3072]{1,0:T(8,128)(2,1)S(1)} custom-call(s32[1,3840]{1,0:T(1,128)S(1)} %multiply_add_fusion.xk_ref, s32[1,3840]{1,0:T(1,128)S(1)} %get-tuple-element.24.yk_ref), custom_call_target="tpu_custom_call" | custom-call | tf_op jit(solution)/shard_map/count/pallas_call | solution.py:113
  66.0 9.9 %all-to-all-done.2 = bf16[8,16,4,8,128]{4,3,2,1,0:T(8,128)(2,1)S(1)} async-done(((bf16[8,16,4,8,128]{4,3,2,1,0:T(8,128)(2,1)}), bf16[8,16,4,8,128]{4,3,2,1,0:T(8,128)(2,1)S(1)}, u32[]{:S(2)}, u32[]{:S(2)}) %all-to-all-start.2) | async-done | bytes 1048608 | tf_op jit(solution)/shard_map/all_to_all | solution.py:401
  75.9 1.5 shard_map.123
  77.3 25.0 %all_to_all.35.got_ref = bf16[8,105,8,128]{3,2,1,0:T(8,128)(2,1)S(1)} all-to-all(bf16[8,105,8,128]{3,2,1,0:T(8,128)(2,1)S(1)} %get-tuple-element.17), channel_id=1, replica_groups={{0,1,2,3,4,5,6,7},{8,9,10,11,12,13,14,15},{16,17,18,19,20,21,22,23},{24..., dimensions={0} | all-to-all | bytes 3440640 | tf_op jit(solution)/shard_map/all_to_all | solution.py:401
  102.3 2.0 %shard_map.125 = (bf16[32,4,8,128]{3,2,1,0:T(8,128)(2,1)}, bf16[32,4,8,128]{3,2,1,0:T(8,128)(2,1)S(1)}) custom-call(s32[192]{0:T(256)S(1)} %dynamic_slice.3.idx_ref, bf16[8,105,8,128]{3,2,1,0:T(8,128)(2,1)S(1)} %all_to_all.35.got_ref), custom_call_target="tpu_custom_call" | custom-call | tf_op jit(solution)/shard_map/pallas_call | solution.py:322
  104.3 1.9 %collective-permute-start.2 = (bf16[32,4,8,128]{3,2,1,0:T(8,128)(2,1)}, bf16[32,4,8,128]{3,2,1,0:T(8,128)(2,1)S(1)}, u32[]{:S(2)}, u32[]{:S(2)}) collective-permute-start(bf16[32,4,8,128]{3,2,1,0:T(8,128)(2,1)} %get-tuple-element.18), channel_id=1, source_target_pairs={{0,32},{32,0},{64,96},{96,64},{128,160},{160,128},{192,224},{224,1... | collective-permute-start | bytes 786440 | tf_op jit(solution)/shard_map/ppermute | solution.py:18
  106.2 8.6 %collective-permute-start.3 = (bf16[32,4,8,128]{3,2,1,0:T(8,128)(2,1)S(1)}, bf16[32,4,8,128]{3,2,1,0:T(8,128)(2,1)S(1)}, u32[]{:S(2)}, u32[]{:S(2)}) collective-permute-start(bf16[32,4,8,128]{3,2,1,0:T(8,128)(2,1)S(1)} %get-tuple-element.19), channel_id=1, source_target_pairs={{0,480},{32,64},{64,32},{96,128},{128,96},{160,192},{192,160},{224... | collective-permute-start | bytes 786440 | tf_op jit(solution)/shard_map/ppermute | solution.py:23
  115.0 9.3 %all_to_all.36.got_ref = f32[4,3,8,128]{3,2,1,0:T(8,128)S(1)} all-to-all(f32[4,3,8,128]{3,2,1,0:T(8,128)S(1)} %shard_map.126), channel_id=1, replica_groups={{0,8,16,24},{1,9,17,25},{2,10,18,26},{3,11,19,27},{4,12,20,28},{5,13,21..., dimensions={0} | all-to-all | bytes 98304 | tf_op jit(solution)/shard_map/all_to_all | solution.py:406
  124.9 3.8 %all-to-all-start.5 = ((bf16[16,3,8,128]{3,2,1,0:T(8,128)(2,1)}), bf16[16,3,8,128]{3,2,1,0:T(8,128)(2,1)S(1)}, u32[]{:S(2)}, u32[]{:S(2)}) async-start(bf16[16,3,8,128]{3,2,1,0:T(8,128)(2,1)} %shard_map.127), calls=%async_computation.5 | async-start | bytes 196608 | tf_op jit(solution)/shard_map/all_to_all | solution.py:396
  128.7 1.0 shard_map.124.own_ref
  129.7 8.8 %all-to-all-done.5.share_ref = bf16[16,3,8,128]{3,2,1,0:T(8,128)(2,1)S(1)} async-done(((bf16[16,3,8,128]{3,2,1,0:T(8,128)(2,1)}), bf16[16,3,8,128]{3,2,1,0:T(8,128)(2,1)S(1)}, u32[]{:S(2)}, u32[]{:S(2)}) %all-to-all-start.5) | async-done | bytes 98336 | tf_op jit(solution)/shard_map/all_to_all | solution.py:396
  139.1 20.5 %all_to_all.37.final_ref = bf16[32,6,8,128]{3,2,1,0:T(8,128)(2,1)S(1)} all-to-all(bf16[32,6,8,128]{3,2,1,0:T(8,128)(2,1)S(1)} %get-tuple-element.20), channel_id=1, replica_groups=mesh['rep'=16,'grp'=32] {'grp'}, dimensions={0} | all-to-all | bytes 786432 | tf_op jit(solution)/shard_map/all_to_all | solution.py:396
  159.6 0.8 shard_map.129
  (31 shorter events, 2.1 us)
Async XLA Ops:
  2.3 23.0 %all-to-all-start = ((bf16[32,5,8,128]{3,2,1,0:T(8,128)(2,1)}), bf16[32,5,8,128]{3,2,1,0:T(8,128)(2,1)S(1)}, u32[]{:S(2)}, u32[]{:S(2)}) async-start(bf16[32,5,8,128]{3,2,1,0:T(8,128)(2,1)} %get-tuple-element.14), calls=%async_computation | async-start | bytes 655360 | tf_op jit(solution)/shard_map/all_to_all | solution.py:396
  27.0 31.2 %all-to-all-start.1 = ((bf16[8,8,4,8,128]{4,3,2,1,0:T(8,128)(2,1)}), bf16[8,8,4,8,128]{4,3,2,1,0:T(8,128)(2,1)S(1)}, u32[]{:S(2)}, u32[]{:S(2)}) async-start(bf16[8,8,4,8,128]{4,3,2,1,0:T(8,128)(2,1)} %shard_map.121), calls=%async_computation.1 | async-start | bytes 1048576 | tf_op jit(solution)/shard_map/all_to_all | solution.py:401
  31.9 30.4 %copy-start.5 = (s32[1,3840]{1,0:T(1,128)S(1)}, s32[1,3840]{1,0:T(1,128)}, u32[]{:S(2)}) copy-start(s32[1,3840]{1,0:T(1,128)} %param.15) | copy-start | bytes 46084
  31.9 30.4 %copy-start.6 = (s32[1,3840]{1,0:T(1,128)S(1)}, s32[1,3840]{1,0:T(1,128)}, u32[]{:S(2)}) copy-start(s32[1,3840]{1,0:T(1,128)} %param.17) | copy-start | bytes 46084
  32.0 30.6 %copy-start.4 = (s32[1,3840]{1,0:T(1,128)S(1)}, s32[1,3840]{1,0:T(1,128)}, u32[]{:S(2)}) copy-start(s32[1,3840]{1,0:T(1,128)} %param.16) | copy-start | bytes 46084
  32.0 18.7 %collective-permute-start.1 = (bf16[32,4,8,128]{3,2,1,0:T(8,128)(2,1)S(1)}, bf16[32,4,8,128]{3,2,1,0:T(8,128)(2,1)S(1)}, u32[]{:S(2)}, u32[]{:S(2)}) collective-permute-start(bf16[32,4,8,128]{3,2,1,0:T(8,128)(2,1)S(1)} %slice.9.own_ref), channel_id=1, source_target_pairs={{0,480},{32,64},{64,32},{96,128},{128,96},{160,192},{192,160},{224... | collective-permute-start | bytes 786440 | tf_op jit(solution)/shard_map/ppermute | solution.py:23
  44.1 12.3 %collective-permute-start = (bf16[32,4,8,128]{3,2,1,0:T(8,128)(2,1)S(1)}, bf16[32,4,8,128]{3,2,1,0:T(8,128)(2,1)S(1)}, u32[]{:S(2)}, u32[]{:S(2)}) collective-permute-start(bf16[32,4,8,128]{3,2,1,0:T(8,128)(2,1)S(1)} %slice.9.own_ref), channel_id=1, source_target_pairs={{0,32},{32,0},{64,96},{96,64},{128,160},{160,128},{192,224},{224,1... | collective-permute-start | bytes 786440 | tf_op jit(solution)/shard_map/ppermute | solution.py:18
  58.2 17.7 %copy-start = (bf16[256,256]{1,0:T(8,128)(2,1)S(1)}, bf16[256,256]{1,0:T(8,128)(2,1)}, u32[]{:S(2)}) copy-start(bf16[256,256]{1,0:T(8,128)(2,1)} %weight_ref.3) | copy-start | bytes 393220
  58.2 17.7 %copy-start.1 = (f32[128,1]{1,0:T(8,128)S(1)}, f32[128,1]{1,0:T(8,128)}, u32[]{:S(2)}) copy-start(f32[128,1]{1,0:T(8,128)} %get-tuple-element.15.dinv_ref) | copy-start | bytes 1540
  58.2 17.7 %copy-start.2 = (bf16[128,256]{1,0:T(8,128)(2,1)S(1)}, bf16[128,256]{1,0:T(8,128)(2,1)}, u32[]{:S(2)}) copy-start(bf16[128,256]{1,0:T(8,128)(2,1)} %cot_ref.1) | copy-start | bytes 196612
  58.2 17.7 %copy-start.3 = (f32[256]{0:T(256)S(1)}, f32[256]{0:T(256)}, u32[]{:S(2)}) copy-start(f32[256]{0:T(256)} %param.11) | copy-start | bytes 3076
  58.2 17.7 %all-to-all-start.2 = ((bf16[8,16,4,8,128]{4,3,2,1,0:T(8,128)(2,1)}), bf16[8,16,4,8,128]{4,3,2,1,0:T(8,128)(2,1)S(1)}, u32[]{:S(2)}, u32[]{:S(2)}) async-start(bf16[8,16,4,8,128]{4,3,2,1,0:T(8,128)(2,1)} %shard_map.122), calls=%async_computation.2 | async-start | bytes 2097152 | tf_op jit(solution)/shard_map/all_to_all | solution.py:401
  104.3 34.2 %collective-permute-start.2 = (bf16[32,4,8,128]{3,2,1,0:T(8,128)(2,1)}, bf16[32,4,8,128]{3,2,1,0:T(8,128)(2,1)S(1)}, u32[]{:S(2)}, u32[]{:S(2)}) collective-permute-start(bf16[32,4,8,128]{3,2,1,0:T(8,128)(2,1)} %get-tuple-element.18), channel_id=1, source_target_pairs={{0,32},{32,0},{64,96},{96,64},{128,160},{160,128},{192,224},{224,1... | collective-permute-start | bytes 786440 | tf_op jit(solution)/shard_map/ppermute | solution.py:18
  106.2 32.3 %collective-permute-start.3 = (bf16[32,4,8,128]{3,2,1,0:T(8,128)(2,1)S(1)}, bf16[32,4,8,128]{3,2,1,0:T(8,128)(2,1)S(1)}, u32[]{:S(2)}, u32[]{:S(2)}) collective-permute-start(bf16[32,4,8,128]{3,2,1,0:T(8,128)(2,1)S(1)} %get-tuple-element.19), channel_id=1, source_target_pairs={{0,480},{32,64},{64,32},{96,128},{128,96},{160,192},{192,160},{224... | collective-permute-start | bytes 786440 | tf_op jit(solution)/shard_map/ppermute | solution.py:23
  124.9 13.6 %all-to-all-start.5 = ((bf16[16,3,8,128]{3,2,1,0:T(8,128)(2,1)}), bf16[16,3,8,128]{3,2,1,0:T(8,128)(2,1)S(1)}, u32[]{:S(2)}, u32[]{:S(2)}) async-start(bf16[16,3,8,128]{3,2,1,0:T(8,128)(2,1)} %shard_map.127), calls=%async_computation.5 | async-start | bytes 196608 | tf_op jit(solution)/shard_map/all_to_all | solution.py:396

commit v10 on v9

--- a/solution.py
+++ b/solution.py
@@ -237,33 +237,6 @@
     )(slab, xown, xfar, weight, dinv, bias, cotangent)
 
 
-def fold_kernel(got_ref, out_ref, made_ref, sem):
-    segments = made_ref.shape[0]
-    first = got_ref.shape[1] - 1 - 2 * segments
-    total = got_ref[0, pl.ds(first, 1 + 2 * segments)].astype(jnp.float32)
-    for d in range(1, got_ref.shape[0]):
-        total = total + got_ref[d, pl.ds(first, 1 + 2 * segments)].astype(jnp.float32)
-    for segment in range(segments):
-        made_ref[segment, 0] = total[0]
-        made_ref[segment, 1] = total[1 + 2 * segment]
-        made_ref[segment, 2] = total[2 + 2 * segment]
-    copy = pltpu.make_async_copy(made_ref, out_ref, sem)
-    copy.start()
-    copy.wait()
-
-
-def fold(got, segments):
-    shape = (segments, 3, SUB, LANE)
-    return call(
-        fold_kernel,
-        4,
-        jax.ShapeDtypeStruct(shape, jnp.float32),
-        [vmem()],
-        hbm(),
-        [pltpu.VMEM(shape, jnp.float32), pltpu.SemaphoreType.DMA],
-    )(got)
-
-
 def spread_kernel(got_ref, out_ref, made_ref, sem):
     total = got_ref[0]
     for segment in range(1, got_ref.shape[0]):
@@ -297,10 +270,9 @@
     )(got)
 
 
-def collect_kernel(members, per_part, parts, chains, idx_ref, got_ref, *refs):
-    outs, acc_ref = refs[:-1], refs[-1]
+def add_parts(per_part, parts, idx_ref, got_ref, acc_ref):
     acc_ref[...] = jnp.zeros_like(acc_ref)
-    tiles = acc_ref.shape[1]
+    chains, tiles = acc_ref.shape[:2]
     for step in range(SEGMENT // chains):
         for part in parts:
             for t in range(part * per_part, (part + 1) * per_part):
@@ -308,24 +280,64 @@
                     d = step * chains + j
                     at = jnp.bitwise_and(idx_ref[d * 3 * per_part + t], tiles - 1)
                     acc_ref[j, at] += got_ref[d, pl.ds(4 * t, 4)].astype(jnp.float32)
-    for number, ref in enumerate(outs):
-        part = pl.ds(number * members, members)
-        value = acc_ref[0, part]
-        for j in range(1, chains):
-            value = value + acc_ref[j, part]
-        ref[...] = value.astype(ref.dtype)
-
-
-def collect(idx, parts, got, members, per_part, dtype):
-    chains = 2
-    piece = (members, 4, SUB, LANE)
-    return call(
-        functools.partial(collect_kernel, members, per_part, parts, chains),
+
+
+def added(acc_ref, ref, number):
+    part = pl.ds(number * ref.shape[0], ref.shape[0])
+    value = acc_ref[0, part]
+    for j in range(1, acc_ref.shape[0]):
+        value = value + acc_ref[j, part]
+    ref[...] = value.astype(ref.dtype)
+
+
+def near_kernel(per_part, idx_ref, got_ref, first_ref, second_ref, out_ref, acc_ref, made_ref, sem):
+    segments = made_ref.shape[0]
+    extra = pl.ds(got_ref.shape[1] - 1 - 2 * segments, 1 + 2 * segments)
+    total = got_ref[0, extra].astype(jnp.float32)
+    for d in range(1, got_ref.shape[0]):
+        total = total + got_ref[d, extra].astype(jnp.float32)
+    for segment in range(segments):
+        made_ref[segment, 0] = total[0]
+        made_ref[segment, 1] = total[1 + 2 * segment]
+        made_ref[segment, 2] = total[2 + 2 * segment]
+    copy = pltpu.make_async_copy(made_ref, out_ref, sem)
+    copy.start()
+    add_parts(per_part, (0, 2), idx_ref, got_ref, acc_ref)
+    added(acc_ref, first_ref, 0)
+    added(acc_ref, second_ref, 1)
+    copy.wait()
+
+
+def collect_near(idx, got, members, per_part):
+    piece = jax.ShapeDtypeStruct((members, 4, SUB, LANE), jnp.bfloat16)
+    shape = (members // SEGMENT, 3, SUB, LANE)
+    return call(
+        functools.partial(near_kernel, per_part),
         8,
-        tuple(jax.ShapeDtypeStruct(piece, dtype) for _ in parts),
+        (piece, piece, jax.ShapeDtypeStruct(shape, jnp.float32)),
         [smem(), vmem()],
-        (vmem(),) * len(parts),
-        [pltpu.VMEM((chains, len(parts) * members, 4, SUB, LANE), jnp.float32)],
+        (vmem(), vmem(), hbm()),
+        [
+            pltpu.VMEM((2, 2 * members, 4, SUB, LANE), jnp.float32),
+            pltpu.VMEM(shape, jnp.float32),
+            pltpu.SemaphoreType.DMA,
+        ],
+    )(idx, got)
+
+
+def own_kernel(per_part, idx_ref, got_ref, own_ref, acc_ref):
+    add_parts(per_part, (1,), idx_ref, got_ref, acc_ref)
+    added(acc_ref, own_ref, 0)
+
+
+def collect_own(idx, got, members, per_part):
+    return call(
+        functools.partial(own_kernel, per_part),
+        8,
+        jax.ShapeDtypeStruct((members, 4, SUB, LANE), jnp.float32),
+        [smem(), vmem()],
+        vmem(),
+        [pltpu.VMEM((2, members, 4, SUB, LANE), jnp.float32)],
     )(idx, got)
 
 
@@ -452,13 +464,13 @@
         listed,
     )
     mine = segment_swap(partial, members)
-    grad = across_swap(fold(mine, members // SEGMENT), members)
+    to_first, to_second, grad = collect_near(near_idx, mine, members, per_part)
+    grad = across_swap(grad, members)
     share = spread(grad, rings)
     share = swap(share, "rep")
-    to_first, to_second = collect(near_idx, (0, 2), mine, members, per_part, jnp.bfloat16)
     from_first = with_partner(to_first, "rep")
     from_second = with_other(to_second, "rep")
-    (own_sum,) = collect(near_idx, (1,), mine, members, per_part, jnp.float32)
+    own_sum = collect_own(near_idx, mine, members, per_part)
 
     final, grad_bias = join(own_sum, from_first, from_second, share)
     final = swap(final, "grp")

time: 161 us -> 161 us (level)
  no operation moved by 1% of the time
where the time goes in v10:
time: 161 us; the launch traced here: 160 us
  blocking collectives  54.8 us (34%)
  starting transfers between devices  47.8 us (30%)
  waiting for transfers between devices  41.6 us (26%)
  Pallas kernels  14.8 us (9%)
    all_to_all x1, blocking collectives, segment_swap(): return lax.all_to_all(x, 'grp', 0, 0, axis_index_groups=groups, tiled=True)  25 us
    all_to_all x2, waiting for transfers between devices, swap(): return lax.all_to_all(x, axis, 0, 0, tiled=True)  21.3 us
    ppermute x2, starting transfers between devices, with_other(): lax.ppermute(x, axis, [(i, (i + 1 if i % 2 else i - 1) % size) for i in r...  20.8 us
    all_to_all x1, blocking collectives, swap(): return lax.all_to_all(x, axis, 0, 0, tiled=True)  20.5 us
    all_to_all x2, starting transfers between devices, swap(): return lax.all_to_all(x, axis, 0, 0, tiled=True)  14.1 us
    all_to_all x2, waiting for transfers between devices, segment_swap(): return lax.all_to_all(x, 'grp', 0, 0, axis_index_groups=groups, tiled=True)  9.9 us
    all_to_all x1, blocking collectives, across_swap(): return lax.all_to_all(x, 'grp', 0, 0, axis_index_groups=groups, tiled=True)  9.28 us
    all_to_all x2, starting transfers between devices, segment_swap(): return lax.all_to_all(x, 'grp', 0, 0, axis_index_groups=groups, tiled=True)  9.05 us
  transfers between devices with their start and end apart: 8, of which 5 were waited for; matrix products, arithmetic and copies ran while one was open for 0% of the time, Pallas kernels for 4%

profile of v10, /device:TPU:1, one launch (start us, length us, event | category | flops | bytes accessed | tf_op | source)
XLA Modules:
  0.0 160.5 jit_solution(15144868359543704461)
XLA Ops:
  0.6 1.7 %shard_map.120 = (bf16[32,5,8,128]{3,2,1,0:T(8,128)(2,1)}, f32[128,1]{1,0:T(8,128)}) custom-call(bf16[128,256]{1,0:T(8,128)(2,1)} %x_ref.1, s32[1,128]{1,0:T(1,128)} %bitcast.8, s32[1,24]{1,0:T(1,128)} %cols_ref.1), custom_call_target="tpu_custom_call" | custom-call | tf_op jit(solution)/shard_map/pallas_call | solution.py:74
  2.3 10.4 %all-to-all-start = ((bf16[32,5,8,128]{3,2,1,0:T(8,128)(2,1)}), bf16[32,5,8,128]{3,2,1,0:T(8,128)(2,1)S(1)}, u32[]{:S(2)}, u32[]{:S(2)}) async-start(bf16[32,5,8,128]{3,2,1,0:T(8,128)(2,1)} %get-tuple-element.15), calls=%async_computation | async-start | bytes 655360 | tf_op jit(solution)/shard_map/all_to_all | solution.py:408
  12.9 12.5 %all-to-all-done = bf16[32,5,8,128]{3,2,1,0:T(8,128)(2,1)S(1)} async-done(((bf16[32,5,8,128]{3,2,1,0:T(8,128)(2,1)}), bf16[32,5,8,128]{3,2,1,0:T(8,128)(2,1)S(1)}, u32[]{:S(2)}, u32[]{:S(2)}) %all-to-all-start) | async-done | bytes 327712 | tf_op jit(solution)/shard_map/all_to_all | solution.py:408
  25.6 1.4 shard_map.121
  27.0 4.9 %all-to-all-start.1 = ((bf16[8,8,4,8,128]{4,3,2,1,0:T(8,128)(2,1)}), bf16[8,8,4,8,128]{4,3,2,1,0:T(8,128)(2,1)S(1)}, u32[]{:S(2)}, u32[]{:S(2)}) async-start(bf16[8,8,4,8,128]{4,3,2,1,0:T(8,128)(2,1)} %shard_map.121), calls=%async_computation.1 | async-start | bytes 1048576 | tf_op jit(solution)/shard_map/all_to_all | solution.py:413
  32.0 12.2 %collective-permute-start.1 = (bf16[32,4,8,128]{3,2,1,0:T(8,128)(2,1)S(1)}, bf16[32,4,8,128]{3,2,1,0:T(8,128)(2,1)S(1)}, u32[]{:S(2)}, u32[]{:S(2)}) collective-permute-start(bf16[32,4,8,128]{3,2,1,0:T(8,128)(2,1)S(1)} %slice.9.own_ref), channel_id=1, source_target_pairs={{0,480},{32,64},{64,32},{96,128},{128,96},{160,192},{192,160},{224... | collective-permute-start | bytes 786440 | tf_op jit(solution)/shard_map/ppermute | solution.py:23
  44.1 1.9 %collective-permute-start = (bf16[32,4,8,128]{3,2,1,0:T(8,128)(2,1)S(1)}, bf16[32,4,8,128]{3,2,1,0:T(8,128)(2,1)S(1)}, u32[]{:S(2)}, u32[]{:S(2)}) collective-permute-start(bf16[32,4,8,128]{3,2,1,0:T(8,128)(2,1)S(1)} %slice.9.own_ref), channel_id=1, source_target_pairs={{0,32},{32,0},{64,96},{96,64},{128,160},{160,128},{192,224},{224,1... | collective-permute-start | bytes 786440 | tf_op jit(solution)/shard_map/ppermute | solution.py:18
  46.1 4.6 %collective-permute-done.1.second_ref = bf16[32,4,8,128]{3,2,1,0:T(8,128)(2,1)S(1)} collective-permute-done((bf16[32,4,8,128]{3,2,1,0:T(8,128)(2,1)S(1)}, bf16[32,4,8,128]{3,2,1,0:T(8,128)(2,1)S(1)}, u32[]{:S(2)}, u32[]{:S(2)}) %collective-permute-start.1) | collective-permute-done | bytes 262176 | tf_op jit(solution)/shard_map/ppermute | solution.py:23
  50.7 5.8 %collective-permute-done.first_ref = bf16[32,4,8,128]{3,2,1,0:T(8,128)(2,1)S(1)} collective-permute-done((bf16[32,4,8,128]{3,2,1,0:T(8,128)(2,1)S(1)}, bf16[32,4,8,128]{3,2,1,0:T(8,128)(2,1)S(1)}, u32[]{:S(2)}, u32[]{:S(2)}) %collective-permute-start) | collective-permute-done | bytes 262176 | tf_op jit(solution)/shard_map/ppermute | solution.py:18
  56.5 1.7 %shard_map.122 = bf16[8,16,4,8,128]{4,3,2,1,0:T(8,128)(2,1)} custom-call(s32[192]{0:T(256)S(1)} %dynamic_slice.3.idx_ref, bf16[32,4,8,128]{3,2,1,0:T(8,128)(2,1)S(1)} %collective-permute-done.first_ref, bf16[32,4,8,128]{3,2,1,0:T(8,128)(2,1)S(1)} %collective-permute-done.1.second_ref), custom_call_target="tpu_custom_call" | custom-call | tf_op jit(solution)/shard_map/pallas_call | solution.py:160
  58.2 4.1 %all-to-all-start.2 = ((bf16[8,16,4,8,128]{4,3,2,1,0:T(8,128)(2,1)}), bf16[8,16,4,8,128]{4,3,2,1,0:T(8,128)(2,1)S(1)}, u32[]{:S(2)}, u32[]{:S(2)}) async-start(bf16[8,16,4,8,128]{4,3,2,1,0:T(8,128)(2,1)} %shard_map.122), calls=%async_computation.2 | async-start | bytes 2097152 | tf_op jit(solution)/shard_map/all_to_all | solution.py:413
  62.7 3.3 %count.1.slab_ref = bf16[128,3072]{1,0:T(8,128)(2,1)S(1)} custom-call(s32[1,3840]{1,0:T(1,128)S(1)} %multiply_add_fusion.xk_ref, s32[1,3840]{1,0:T(1,128)S(1)} %get-tuple-element.26.yk_ref), custom_call_target="tpu_custom_call" | custom-call | tf_op jit(solution)/shard_map/count/pallas_call | solution.py:113
  66.0 9.9 %all-to-all-done.2 = bf16[8,16,4,8,128]{4,3,2,1,0:T(8,128)(2,1)S(1)} async-done(((bf16[8,16,4,8,128]{4,3,2,1,0:T(8,128)(2,1)}), bf16[8,16,4,8,128]{4,3,2,1,0:T(8,128)(2,1)S(1)}, u32[]{:S(2)}, u32[]{:S(2)}) %all-to-all-start.2) | async-done | bytes 1048608 | tf_op jit(solution)/shard_map/all_to_all | solution.py:413
  75.9 1.5 shard_map.123
  77.3 25.0 %all_to_all.35.got_ref = bf16[8,105,8,128]{3,2,1,0:T(8,128)(2,1)S(1)} all-to-all(bf16[8,105,8,128]{3,2,1,0:T(8,128)(2,1)S(1)} %get-tuple-element.18), channel_id=1, replica_groups={{0,1,2,3,4,5,6,7},{8,9,10,11,12,13,14,15},{16,17,18,19,20,21,22,23},{24..., dimensions={0} | all-to-all | bytes 3440640 | tf_op jit(solution)/shard_map/all_to_all | solution.py:413
  102.3 2.1 %shard_map.125 = (bf16[32,4,8,128]{3,2,1,0:T(8,128)(2,1)}, bf16[32,4,8,128]{3,2,1,0:T(8,128)(2,1)S(1)}, f32[4,3,8,128]{3,2,1,0:T(8,128)S(1)}) custom-call(s32[192]{0:T(256)S(1)} %dynamic_slice.3.idx_ref, bf16[8,105,8,128]{3,2,1,0:T(8,128)(2,1)S(1)} %all_to_all.35.got_ref), custom_call_target="tpu_custom_call" | custom-call | tf_op jit(solution)/shard_map/pallas_call | solution.py:314
  104.4 1.9 %collective-permute-start.2 = (bf16[32,4,8,128]{3,2,1,0:T(8,128)(2,1)}, bf16[32,4,8,128]{3,2,1,0:T(8,128)(2,1)S(1)}, u32[]{:S(2)}, u32[]{:S(2)}) collective-permute-start(bf16[32,4,8,128]{3,2,1,0:T(8,128)(2,1)} %get-tuple-element.19), channel_id=1, source_target_pairs={{0,32},{32,0},{64,96},{96,64},{128,160},{160,128},{192,224},{224,1... | collective-permute-start | bytes 786440 | tf_op jit(solution)/shard_map/ppermute | solution.py:18
  106.4 8.6 %collective-permute-start.3 = (bf16[32,4,8,128]{3,2,1,0:T(8,128)(2,1)S(1)}, bf16[32,4,8,128]{3,2,1,0:T(8,128)(2,1)S(1)}, u32[]{:S(2)}, u32[]{:S(2)}) collective-permute-start(bf16[32,4,8,128]{3,2,1,0:T(8,128)(2,1)S(1)} %get-tuple-element.20), channel_id=1, source_target_pairs={{0,480},{32,64},{64,32},{96,128},{128,96},{160,192},{192,160},{224... | collective-permute-start | bytes 786440 | tf_op jit(solution)/shard_map/ppermute | solution.py:23
  115.0 9.3 %all_to_all.36.got_ref = f32[4,3,8,128]{3,2,1,0:T(8,128)S(1)} all-to-all(f32[4,3,8,128]{3,2,1,0:T(8,128)S(1)} %get-tuple-element.21), channel_id=1, replica_groups={{0,8,16,24},{1,9,17,25},{2,10,18,26},{3,11,19,27},{4,12,20,28},{5,13,21..., dimensions={0} | all-to-all | bytes 98304 | tf_op jit(solution)/shard_map/all_to_all | solution.py:418
  125.0 3.8 %all-to-all-start.5 = ((bf16[16,3,8,128]{3,2,1,0:T(8,128)(2,1)}), bf16[16,3,8,128]{3,2,1,0:T(8,128)(2,1)S(1)}, u32[]{:S(2)}, u32[]{:S(2)}) async-start(bf16[16,3,8,128]{3,2,1,0:T(8,128)(2,1)} %shard_map.126), calls=%async_computation.5 | async-start | bytes 196608 | tf_op jit(solution)/shard_map/all_to_all | solution.py:408
  128.7 1.0 shard_map.124.own_ref
  129.7 8.8 %all-to-all-done.5.share_ref = bf16[16,3,8,128]{3,2,1,0:T(8,128)(2,1)S(1)} async-done(((bf16[16,3,8,128]{3,2,1,0:T(8,128)(2,1)}), bf16[16,3,8,128]{3,2,1,0:T(8,128)(2,1)S(1)}, u32[]{:S(2)}, u32[]{:S(2)}) %all-to-all-start.5) | async-done | bytes 98336 | tf_op jit(solution)/shard_map/all_to_all | solution.py:408
  139.2 20.5 %all_to_all.37.final_ref = bf16[32,6,8,128]{3,2,1,0:T(8,128)(2,1)S(1)} all-to-all(bf16[32,6,8,128]{3,2,1,0:T(8,128)(2,1)S(1)} %get-tuple-element.22), channel_id=1, replica_groups=mesh['rep'=16,'grp'=32] {'grp'}, dimensions={0} | all-to-all | bytes 786432 | tf_op jit(solution)/shard_map/all_to_all | solution.py:408
  159.6 0.8 shard_map.128
  (30 shorter events, 2.0 us)
Async XLA Ops:
  2.3 23.0 %all-to-all-start = ((bf16[32,5,8,128]{3,2,1,0:T(8,128)(2,1)}), bf16[32,5,8,128]{3,2,1,0:T(8,128)(2,1)S(1)}, u32[]{:S(2)}, u32[]{:S(2)}) async-start(bf16[32,5,8,128]{3,2,1,0:T(8,128)(2,1)} %get-tuple-element.15), calls=%async_computation | async-start | bytes 655360 | tf_op jit(solution)/shard_map/all_to_all | solution.py:408
  27.0 31.2 %all-to-all-start.1 = ((bf16[8,8,4,8,128]{4,3,2,1,0:T(8,128)(2,1)}), bf16[8,8,4,8,128]{4,3,2,1,0:T(8,128)(2,1)S(1)}, u32[]{:S(2)}, u32[]{:S(2)}) async-start(bf16[8,8,4,8,128]{4,3,2,1,0:T(8,128)(2,1)} %shard_map.121), calls=%async_computation.1 | async-start | bytes 1048576 | tf_op jit(solution)/shard_map/all_to_all | solution.py:413
  31.9 30.4 %copy-start.5 = (s32[1,3840]{1,0:T(1,128)S(1)}, s32[1,3840]{1,0:T(1,128)}, u32[]{:S(2)}) copy-start(s32[1,3840]{1,0:T(1,128)} %param.15) | copy-start | bytes 46084
  31.9 30.4 %copy-start.6 = (s32[1,3840]{1,0:T(1,128)S(1)}, s32[1,3840]{1,0:T(1,128)}, u32[]{:S(2)}) copy-start(s32[1,3840]{1,0:T(1,128)} %param.17) | copy-start | bytes 46084
  32.0 30.6 %copy-start.4 = (s32[1,3840]{1,0:T(1,128)S(1)}, s32[1,3840]{1,0:T(1,128)}, u32[]{:S(2)}) copy-start(s32[1,3840]{1,0:T(1,128)} %param.16) | copy-start | bytes 46084
  32.0 18.7 %collective-permute-start.1 = (bf16[32,4,8,128]{3,2,1,0:T(8,128)(2,1)S(1)}, bf16[32,4,8,128]{3,2,1,0:T(8,128)(2,1)S(1)}, u32[]{:S(2)}, u32[]{:S(2)}) collective-permute-start(bf16[32,4,8,128]{3,2,1,0:T(8,128)(2,1)S(1)} %slice.9.own_ref), channel_id=1, source_target_pairs={{0,480},{32,64},{64,32},{96,128},{128,96},{160,192},{192,160},{224... | collective-permute-start | bytes 786440 | tf_op jit(solution)/shard_map/ppermute | solution.py:23
  44.1 12.3 %collective-permute-start = (bf16[32,4,8,128]{3,2,1,0:T(8,128)(2,1)S(1)}, bf16[32,4,8,128]{3,2,1,0:T(8,128)(2,1)S(1)}, u32[]{:S(2)}, u32[]{:S(2)}) collective-permute-start(bf16[32,4,8,128]{3,2,1,0:T(8,128)(2,1)S(1)} %slice.9.own_ref), channel_id=1, source_target_pairs={{0,32},{32,0},{64,96},{96,64},{128,160},{160,128},{192,224},{224,1... | collective-permute-start | bytes 786440 | tf_op jit(solution)/shard_map/ppermute | solution.py:18
  58.2 17.7 %copy-start = (bf16[256,256]{1,0:T(8,128)(2,1)S(1)}, bf16[256,256]{1,0:T(8,128)(2,1)}, u32[]{:S(2)}) copy-start(bf16[256,256]{1,0:T(8,128)(2,1)} %weight_ref.3) | copy-start | bytes 393220
  58.2 17.7 %copy-start.1 = (f32[128,1]{1,0:T(8,128)S(1)}, f32[128,1]{1,0:T(8,128)}, u32[]{:S(2)}) copy-start(f32[128,1]{1,0:T(8,128)} %get-tuple-element.16.dinv_ref) | copy-start | bytes 1540
  58.2 17.7 %copy-start.2 = (bf16[128,256]{1,0:T(8,128)(2,1)S(1)}, bf16[128,256]{1,0:T(8,128)(2,1)}, u32[]{:S(2)}) copy-start(bf16[128,256]{1,0:T(8,128)(2,1)} %cot_ref.1) | copy-start | bytes 196612
  58.2 17.7 %copy-start.3 = (f32[256]{0:T(256)S(1)}, f32[256]{0:T(256)}, u32[]{:S(2)}) copy-start(f32[256]{0:T(256)} %param.11) | copy-start | bytes 3076
  58.2 17.7 %all-to-all-start.2 = ((bf16[8,16,4,8,128]{4,3,2,1,0:T(8,128)(2,1)}), bf16[8,16,4,8,128]{4,3,2,1,0:T(8,128)(2,1)S(1)}, u32[]{:S(2)}, u32[]{:S(2)}) async-start(bf16[8,16,4,8,128]{4,3,2,1,0:T(8,128)(2,1)} %shard_map.122), calls=%async_computation.2 | async-start | bytes 2097152 | tf_op jit(solution)/shard_map/all_to_all | solution.py:413
  104.4 34.1 %collective-permute-start.2 = (bf16[32,4,8,128]{3,2,1,0:T(8,128)(2,1)}, bf16[32,4,8,128]{3,2,1,0:T(8,128)(2,1)S(1)}, u32[]{:S(2)}, u32[]{:S(2)}) collective-permute-start(bf16[32,4,8,128]{3,2,1,0:T(8,128)(2,1)} %get-tuple-element.19), channel_id=1, source_target_pairs={{0,32},{32,0},{64,96},{96,64},{128,160},{160,128},{192,224},{224,1... | collective-permute-start | bytes 786440 | tf_op jit(solution)/shard_map/ppermute | solution.py:18
  106.4 32.2 %collective-permute-start.3 = (bf16[32,4,8,128]{3,2,1,0:T(8,128)(2,1)S(1)}, bf16[32,4,8,128]{3,2,1,0:T(8,128)(2,1)S(1)}, u32[]{:S(2)}, u32[]{:S(2)}) collective-permute-start(bf16[32,4,8,128]{3,2,1,0:T(8,128)(2,1)S(1)} %get-tuple-element.20), channel_id=1, source_target_pairs={{0,480},{32,64},{64,32},{96,128},{128,96},{160,192},{192,160},{224... | collective-permute-start | bytes 786440 | tf_op jit(solution)/shard_map/ppermute | solution.py:23
  125.0 13.6 %all-to-all-start.5 = ((bf16[16,3,8,128]{3,2,1,0:T(8,128)(2,1)}), bf16[16,3,8,128]{3,2,1,0:T(8,128)(2,1)S(1)}, u32[]{:S(2)}, u32[]{:S(2)}) async-start(bf16[16,3,8,128]{3,2,1,0:T(8,128)(2,1)} %shard_map.126), calls=%async_computation.5 | async-start | bytes 196608 | tf_op jit(solution)/shard_map/all_to_all | solution.py:408
